TPU v7x, 32 devices: a whole 2x2x4 slice. The times are simulated.
32 devices in a mesh: row: 16 (over z, y, core), col: 2 (over x).
Axes of the slice: x: 2, y: 2, z: 4, core: 2. Of those that a mesh axis runs over, the one named last changes fastest.
Arguments:
- anchor: bfloat16 [4096, 128], P(('row', 'col')), may hold values from -3 to 3
- injection: bfloat16 [4096, 128], P(('row', 'col')), may hold values from -6 to 6
- weight: bfloat16 [128, 128], replicated, may hold values from -0.25 to 0.25
- cotangent: bfloat16 [4096, 128], P(('row', 'col')), may hold values from -6 to 6
- node_mask: int32 [4096], P(('row', 'col')), may hold values 0 or 1
- tile_values: bfloat16 [16, 2, 64, 128, 128], P('row', 'col'), may hold values from -0.09375 to 0.09375
- tile_rows: int32 [16, 2, 64], P('row', 'col'), may hold values from 0 to 1
- tile_cols: int32 [16, 2, 64], P('row', 'col'), may hold values from 0 to 15
- tile_counts: int32 [16, 2], P('row', 'col'), may hold values from 1 to 64, as said below
Outputs:
- state: bfloat16 [4096, 128], P(('row', 'col'))
- adjoint: float32 [4096, 128], P(('row', 'col'))
- weight_grad: float32 [128, 128], replicated
Inputs may be any that keep to these rules, and one draw needn't show every extreme that they name: Slot k of device (r, c) is live exactly when k < tile_counts[r, c]; some device has all 64 slots live in every draw.
All inputs are finite; a program needn't handle non-finite values. No bound on the sum of `node_mask` on one device may be relied on, other than what follows from the above.
Results may differ from a plain program's by a relative error of at most 0.006.
Values may be sent and summed in bfloat16 or wider, within the bound.
No kernel may reach another device: no remote copies, remote signals or barrier semaphores. Data moves between devices by JAX's collectives and lax.ppermute only.
A program may use at most 64 MiB of HBM per device.

v0:
```python
import jax
import jax.numpy as jnp
from jax import lax
from jax.sharding import PartitionSpec as P

TILE = 128
ITERS = 3
ADJOINT = 3


def per_device(
    anchor, injection, weight, cotangent, node_mask, tile_values, tile_rows, tile_cols, tile_counts
):
    own = anchor.shape[0]
    hidden = anchor.shape[1]
    tiles = tile_values.reshape(-1, TILE, TILE)
    slots = tiles.shape[0]
    row_slot = tile_rows.reshape(-1)
    col_slot = tile_cols.reshape(-1)
    live_count = tile_counts.reshape(())
    span_rows = own * lax.axis_size("col")
    span_cols = own * lax.axis_size("row")
    row_tiles = span_rows // TILE
    col_tiles = span_cols // TILE
    alive = (jnp.arange(slots) < live_count).astype(jnp.float32)

    def apply_tiles(source, source_tiles, index, out_index, out_tiles, pattern, out_rows):
        shaped = source.reshape(source_tiles, TILE, hidden)
        empty = jnp.zeros((out_tiles, TILE * hidden), jnp.float32)
        block = min(16, slots)
        rounds = (live_count + block - 1) // block

        def one_block(turn, total):
            start = turn * block
            some_tiles = lax.dynamic_slice_in_dim(tiles, start, block, 0)
            some_index = lax.dynamic_slice_in_dim(index, start, block, 0)
            some_out = lax.dynamic_slice_in_dim(out_index, start, block, 0)
            some_alive = lax.dynamic_slice_in_dim(alive, start, block, 0)
            product = jnp.einsum(
                pattern, some_tiles, shaped[some_index], preferred_element_type=jnp.float32
            )
            return total.at[some_out].add(product.reshape(block, -1) * some_alive[:, None])

        total = lax.fori_loop(0, rounds, one_block, empty)
        return total.reshape(out_rows, hidden)

    anchor_f = anchor.astype(jnp.float32)
    inject_f = injection.astype(jnp.float32)
    state = anchor
    last_pre = inject_f
    last_state = anchor
    for step in range(ITERS):
        projected = jnp.dot(state, weight, preferred_element_type=jnp.float32).astype(jnp.bfloat16)
        column_states = lax.all_gather(projected, "row", axis=0, tiled=True)
        partial_value = apply_tiles(
            column_states, col_tiles, col_slot, row_slot, row_tiles, "kij,kjh->kih", span_rows
        )
        pre = lax.psum_scatter(partial_value, "col", scatter_dimension=0, tiled=True) + inject_f
        beta = 1.0 / (step + 2.0)
        last_pre = pre
        last_state = state
        state = (beta * anchor_f + (1.0 - beta) * jnp.tanh(pre)).astype(jnp.bfloat16)
    slope = 1.0 - jnp.tanh(last_pre) ** 2
    masked_grad = cotangent.astype(jnp.float32) * node_mask.astype(jnp.float32)[:, None]
    adjoint = masked_grad
    pulled = masked_grad
    weight_f = weight.astype(jnp.float32)
    for step in range(ADJOINT):
        scaled = (adjoint * slope).astype(jnp.bfloat16)
        block_states = lax.all_gather(scaled, "col", axis=0, tiled=True)
        partial_value = apply_tiles(
            block_states, row_tiles, row_slot, col_slot, col_tiles, "kij,kih->kjh", span_cols
        )
        pulled = lax.psum_scatter(partial_value, "row", scatter_dimension=0, tiled=True)
        adjoint = masked_grad + jnp.dot(pulled, weight_f.T, precision=lax.Precision.HIGHEST)
    local_grad = jnp.dot(
        last_state.astype(jnp.float32).T, pulled, precision=lax.Precision.HIGHEST
    ) / (own * lax.axis_size("col"))
    weight_grad = lax.psum(local_grad, ("row", "col"))
    return (state, adjoint, weight_grad)


def solution(mesh):
    in_specs = (
        P(("row", "col"), None),
        P(("row", "col"), None),
        P(),
        P(("row", "col"), None),
        P(("row", "col")),
        P("row", "col", None, None, None),
        P("row", "col", None),
        P("row", "col", None),
        P("row", "col"),
    )
    out_specs = (P(("row", "col"), None), P(("row", "col"), None), P())
    return jax.shard_map(
        per_device, mesh=mesh, in_specs=in_specs, out_specs=out_specs, check_vma=False
    )
```

profile of v0, /device:TPU:0, one launch (start us, length us, event | category | flops | bytes accessed | tf_op | source)
XLA Modules:
  0.0 580.6 jit_solution(11523583762760149427)
XLA Ops:
  8.8 24.6 %all_gather.18 = bf16[2048,128]{1,0:T(8,128)(2,1)S(1)} all-gather(bf16[128,128]{1,0:T(8,128)(2,1)S(1)} %convolution_convert_fusion.2), channel_id=1, replica_groups=mesh['row'=16,'col'=2] {'row'}, dimensions={0}, use_global_device_ids=true | all-gather | bytes 557056 | tf_op jit(solution)/shard_map/all_gather | solution.py:54
  33.5 16.9 %while.60 = (s32[]{:T(128)}, f32[2,16384]{1,0:T(2,128)S(1)}, s32[]{:T(128)}, s32[64]{0:T(128)}, bf16[64,128,128]{2,1,0:T(8,128)(2,1)}, /*index=5*/s32[64]{0:T(12...) while((s32[]{:T(128)}, f32[2,16384]{1,0:T(2,128)S(1)}, ...), condition=%wide.region_2.3_spmd, body=%wide.region_0.2_spmd.sunk | while | flops 67634280 | bytes 4330671 | solution.py:44
  36.3 5.6 scatter_custom_fusion.25
  44.8 5.6 scatter_custom_fusion.25
  51.2 22.7 %reduce-scatter.7.cloned.1.call-done = f32[128,128]{1,0:T(8,128)} async-done(((f32[256,128]{1,0:T(8,128)}), f32[128,128]{1,0:T(8,128)}) %reduce-scatter.7.cloned.1.call-update) | async-done | bytes 65552 | tf_op jit(solution)/shard_map/reduce_scatter | solution.py:58
  74.9 22.8 %all_gather.19 = bf16[2048,128]{1,0:T(8,128)(2,1)S(1)} all-gather(bf16[128,128]{1,0:T(8,128)(2,1)S(1)} %convolution_convert_fusion.1), channel_id=1, replica_groups=mesh['row'=16,'col'=2] {'row'}, dimensions={0}, use_global_device_ids=true | all-gather | bytes 557056 | tf_op jit(solution)/shard_map/all_gather | solution.py:54
  97.8 16.9 %while.61 = (s32[]{:T(128)}, f32[2,16384]{1,0:T(2,128)S(1)}, s32[]{:T(128)}, s32[64]{0:T(128)}, bf16[64,128,128]{2,1,0:T(8,128)(2,1)}, /*index=5*/s32[64]{0:T(12...) while((s32[]{:T(128)}, f32[2,16384]{1,0:T(2,128)S(1)}, ...), condition=%wide.region_6.7_spmd, body=%wide.region_4.6_spmd.sunk | while | flops 67634280 | bytes 4330671 | solution.py:44
  100.6 5.6 scatter_custom_fusion.27
  109.1 5.6 scatter_custom_fusion.27
  115.5 21.8 %reduce-scatter.9.cloned.1.call-done = f32[128,128]{1,0:T(8,128)} async-done(((f32[256,128]{1,0:T(8,128)}), f32[128,128]{1,0:T(8,128)}) %reduce-scatter.9.cloned.1.call-update) | async-done | bytes 65552 | tf_op jit(solution)/shard_map/reduce_scatter | solution.py:58
  138.4 22.8 %all_gather.20 = bf16[2048,128]{1,0:T(8,128)(2,1)S(1)} all-gather(bf16[128,128]{1,0:T(8,128)(2,1)S(1)} %convolution_convert_fusion), channel_id=1, replica_groups=mesh['row'=16,'col'=2] {'row'}, dimensions={0}, use_global_device_ids=true | all-gather | bytes 557056 | tf_op jit(solution)/shard_map/all_gather | solution.py:54
  161.2 17.1 %while.62 = (s32[]{:T(128)}, f32[2,16384]{1,0:T(2,128)S(1)}, s32[]{:T(128)}, s32[64]{0:T(128)}, bf16[64,128,128]{2,1,0:T(8,128)(2,1)}, /*index=5*/s32[64]{0:T(12...) while((s32[]{:T(128)}, f32[2,16384]{1,0:T(2,128)S(1)}, ...), condition=%wide.region_10.11_spmd, body=%wide.region_8.10_spmd.sunk | while | flops 67634280 | bytes 4330671 | solution.py:44
  164.3 5.6 scatter_custom_fusion.29
  172.8 5.6 scatter_custom_fusion.29
  179.3 4.1 copy.12
  183.3 17.7 %reduce-scatter.11.cloned.1.call-done = f32[128,128]{1,0:T(8,128)} async-done(((f32[256,128]{1,0:T(8,128)}), f32[128,128]{1,0:T(8,128)}) %reduce-scatter.11.cloned.1.call-update) | async-done | bytes 65552 | tf_op jit(solution)/shard_map/reduce_scatter | solution.py:58
  202.5 4.6 all_gather.21
  207.2 9.9 %while.63 = (s32[]{:T(128)}, f32[16,16384]{1,0:T(8,128)S(1)}, s32[]{:T(128)}, s32[64]{0:T(128)S(1)}, bf16[64,128,128]{1,2,0:T(8,128)(2,1)}, /*index=5*/s32[64]{0...) while((s32[]{:T(128)}, f32[16,16384]{1,0:T(8,128)S(1)}, ...), condition=%wide.region_14.15_spmd, body=%wide.region_12.14_spmd.sunk | while | flops 67634280 | bytes 5248175 | solution.py:44
  209.4 2.7 scatter_custom_fusion.31
  214.3 2.7 scatter_custom_fusion.31
  218.3 65.5 %reduce-scatter.13.cloned.1.call-done = f32[128,128]{1,0:T(8,128)} async-done(((f32[2048,128]{1,0:T(8,128)}), f32[128,128]{1,0:T(8,128)}) %reduce-scatter.13.cloned.1.call-update) | async-done | bytes 65552 | tf_op jit(solution)/shard_map/reduce_scatter | solution.py:74
  284.9 4.6 all_gather.22
  289.6 9.9 %while.64 = (s32[]{:T(128)}, f32[16,16384]{1,0:T(8,128)S(1)}, s32[]{:T(128)}, s32[64]{0:T(128)S(1)}, bf16[64,128,128]{1,2,0:T(8,128)(2,1)}, /*index=5*/s32[64]{0...) while((s32[]{:T(128)}, f32[16,16384]{1,0:T(8,128)S(1)}, ...), condition=%wide.region_18.19_spmd, body=%wide.region_16.18_spmd.sunk | while | flops 67634280 | bytes 5248175 | solution.py:44
  291.8 2.7 scatter_custom_fusion.33
  296.7 2.7 scatter_custom_fusion.33
  300.7 65.4 %reduce-scatter.15.cloned.1.call-done = f32[128,128]{1,0:T(8,128)} async-done(((f32[2048,128]{1,0:T(8,128)}), f32[128,128]{1,0:T(8,128)}) %reduce-scatter.15.cloned.1.call-update) | async-done | bytes 65552 | tf_op jit(solution)/shard_map/reduce_scatter | solution.py:74
  367.2 4.6 all_gather.23
  371.8 10.1 %while.65 = (s32[]{:T(128)}, f32[16,16384]{1,0:T(8,128)S(1)}, s32[]{:T(128)}, s32[64]{0:T(128)S(1)}, bf16[64,128,128]{1,2,0:T(8,128)(2,1)}, /*index=5*/s32[64]{0...) while((s32[]{:T(128)}, f32[16,16384]{1,0:T(8,128)S(1)}, ...), condition=%wide.region_22.23_spmd, body=%wide.region_20.22_spmd.sunk | while | flops 67634280 | bytes 5248175 | solution.py:44
  374.2 2.7 scatter_custom_fusion.35
  379.2 2.7 scatter_custom_fusion.35
  383.1 65.5 %reduce-scatter.17.cloned.1.call-done = f32[128,128]{1,0:T(8,128)} async-done(((f32[2048,128]{1,0:T(8,128)}), f32[128,128]{1,0:T(8,128)}) %reduce-scatter.17.cloned.1.call-update) | async-done | bytes 65552 | tf_op jit(solution)/shard_map/reduce_scatter | solution.py:74
  452.0 120.2 %all-reduce.2.cloned.1.call-done = f32[128,128]{1,0:T(8,128)} async-done(((f32[128,128]{1,0:T(8,128)}), f32[128,128]{1,0:T(8,128)}) %all-reduce.2.cloned.1.call-update) | async-done | bytes 65552 | tf_op jit(solution)/shard_map/psum | solution.py:79
  (114 shorter events, 47.7 us)
Async XLA Ops:
  7.2 0.8 copy-start
  7.2 66.7 %reduce-scatter.7.cloned.1.call-start = ((), (), s32[]{:S(2)}) async-start(), calls=%async_computation.6 | async-start | bytes 196608 | tf_op jit(solution)/shard_map/reduce_scatter | solution.py:58
  33.4 40.5 %copy-start.1 = (bf16[128,128]{1,0:T(8,128)(2,1)S(1)}, bf16[128,128]{1,0:T(8,128)(2,1)}, u32[]{:S(2)}) copy-start(bf16[128,128]{1,0:T(8,128)(2,1)} %param.22) | copy-start | bytes 98308
  33.4 40.5 %copy-start.3 = (bf16[128,128]{1,0:T(8,128)(2,1)S(1)}, bf16[128,128]{1,0:T(8,128)(2,1)}, u32[]{:S(2)}) copy-start(bf16[128,128]{1,0:T(8,128)(2,1)} %param.21) | copy-start | bytes 98308
  51.2 86.2 %reduce-scatter.9.cloned.1.call-start = ((), (), s32[]{:S(2)}) async-start(), calls=%async_computation.7 | async-start | bytes 196608 | tf_op jit(solution)/shard_map/reduce_scatter | solution.py:58
  115.5 85.5 %reduce-scatter.11.cloned.1.call-start = ((), (), s32[]{:S(2)}) async-start(), calls=%async_computation.8 | async-start | bytes 196608 | tf_op jit(solution)/shard_map/reduce_scatter | solution.py:58
  179.2 4.2 copy-start.7
  179.2 21.9 %copy-start.4 = (bf16[128,128]{1,0:T(8,128)(2,1)S(1)}, bf16[128,128]{1,0:T(8,128)(2,1)}, u32[]{:S(2)}) copy-start(bf16[128,128]{1,0:T(8,128)(2,1)} %param.24) | copy-start | bytes 98308
  179.2 28.0 %copy-start.5 = (s32[64]{0:T(128)S(1)}, s32[64]{0:T(128)}, u32[]{:S(2)}) copy-start(s32[64]{0:T(128)} %get-tuple-element.971) | copy-start | bytes 772
  179.2 28.0 %copy-start.6 = (s32[64]{0:T(128)S(1)}, s32[64]{0:T(128)}, u32[]{:S(2)}) copy-start(s32[64]{0:T(128)} %get-tuple-element.976) | copy-start | bytes 772
  179.2 104.7 %reduce-scatter.13.cloned.1.call-start = ((), (), s32[]{:S(2)}) async-start(), calls=%async_computation.9 | async-start | bytes 1114112 | tf_op jit(solution)/shard_map/reduce_scatter | solution.py:74
  217.1 66.8 %copy-start.2 = (f32[128,128]{1,0:T(8,128)S(1)}, f32[128,128]{1,0:T(8,128)}, u32[]{:S(2)}) copy-start(f32[128,128]{1,0:T(8,128)} %reduce-scatter.11.cloned.1.call-done) | copy-start | bytes 196612
  218.3 147.8 %reduce-scatter.15.cloned.1.call-start = ((), (), s32[]{:S(2)}) async-start(), calls=%async_computation.10 | async-start | bytes 1114112 | tf_op jit(solution)/shard_map/reduce_scatter | solution.py:74
  300.7 148.0 %reduce-scatter.17.cloned.1.call-start = ((), (), s32[]{:S(2)}) async-start(), calls=%async_computation.11 | async-start | bytes 1114112 | tf_op jit(solution)/shard_map/reduce_scatter | solution.py:74
  383.1 189.2 %all-reduce.2.cloned.1.call-start = ((), (), s32[]{:S(2)}) async-start(), calls=%async_computation.12 | async-start | bytes 131072 | tf_op jit(solution)/shard_map/psum | solution.py:79
Sparse Core Ops, SparseCore 0:
  51.3 22.5 reduce-scatter.6
  115.6 21.7 reduce-scatter.8
  179.3 21.7 reduce-scatter.10
  218.4 65.4 reduce-scatter.12
  300.8 65.2 reduce-scatter.14
  383.2 65.3 reduce-scatter.16
  455.7 116.4 all-reduce.1
where the time goes:
time: 585 us; the launch traced here: 581 us
  waiting for transfers between devices  379 us (65%)
  blocking collectives  84 us (14%)
  other arithmetic  57.4 us (10%)
  matrix products  23.6 us (4%)
  local copies, waits for them, and re-layouts  20.4 us (3%)
  between operations  15 us (3%)
    reduce_scatter x3, waiting for transfers between devices, per_device(): lax.psum_scatter(partial_value, 'row', scatter_dimension=0, tiled=True)  196 us
    psum x1, waiting for transfers between devices, per_device(): weight_grad = lax.psum(local_grad, ('row', 'col'))  120 us
    all_gather x3, blocking collectives, per_device(): column_states = lax.all_gather(projected, 'row', axis=0, tiled=True)  70.3 us
    reduce_scatter x3, waiting for transfers between devices, per_device(): lax.psum_scatter(partial_value, 'col', scatter_dimension=0, tiled=True)  62.2 us
    scatter-add x12, other arithmetic, one_block(): total.at[some_out].add(product.reshape(block, -1) * some_alive[:, None])  50 us
    dot_general x12, matrix products, one_block(): jnp.einsum(pattern, some_tiles, shaped[some_index], preferred_element_typ...  16.1 us
    all_gather x3, blocking collectives, per_device(): block_states = lax.all_gather(scaled, 'col', axis=0, tiled=True)  13.8 us
  transfers between devices with their start and end apart: 7, of which 7 were waited for; matrix products, arithmetic and copies ran while one was open for 1% of the time, Pallas kernels for 0%

commit v1 on v0

v1 whole, which is shorter than its diff:
```python
import jax
import jax.numpy as jnp
from jax import lax
from jax.experimental import pallas as pl
from jax.experimental.pallas import tpu as pltpu
from jax.sharding import PartitionSpec as P

TILE = 128
ITERS = 3
ADJOINT = 3
BF16 = jnp.bfloat16
F32 = jnp.float32
VMEM_LIMIT = 48 * 2**20


def vmem_call(body, outs, *args, smem=0, scratch=()):
    specs = [
        pl.BlockSpec(memory_space=pltpu.SMEM if i < smem else pltpu.VMEM) for i in range(len(args))
    ]
    out_specs = [pl.BlockSpec(memory_space=pltpu.VMEM) for _ in outs]
    return pl.pallas_call(
        body,
        out_shape=[jax.ShapeDtypeStruct(shape, dtype) for shape, dtype in outs],
        in_specs=specs,
        out_specs=out_specs,
        scratch_shapes=list(scratch),
        compiler_params=pltpu.CompilerParams(vmem_limit_bytes=VMEM_LIMIT),
    )(*args)


def split_dot(value, factor, dims):
    high = value.astype(BF16)
    low = (value - high.astype(F32)).astype(BF16)
    return lax.dot_general(high, factor, (dims, ((), ())), preferred_element_type=F32) + lax.dot_general(
        low, factor, (dims, ((), ())), preferred_element_type=F32
    )


def per_device(n_row, n_col, *args):
    anchor, injection, weight, cotangent, node_mask, tile_values, tile_rows, tile_cols, tile_counts = args
    own, hidden = anchor.shape
    assert own == TILE
    slots = tile_values.shape[2]
    me_row = lax.axis_index("row")
    me_col = lax.axis_index("col")
    z_step = n_row // 4
    y_steps = [1 << b for b in range(1, z_step.bit_length() - 1)]
    half = n_row // 2

    def exchange(value, axis, distance):
        size = n_row if axis == "row" else n_col
        return lax.ppermute(value, axis, [(i, i ^ distance) for i in range(size)])

    order = [z * z_step for z in range(4)]
    for step in y_steps + [1]:
        order = order + [s ^ step for s in order]

    def position(s):
        place = s // z_step
        weight_of = 4
        for step in y_steps + [1]:
            place = place + ((s // step) % 2) * weight_of
            weight_of *= 2
        return place

    def build(where, rows, cols, count, tiles, a_out, at_out, acc):
        acc[...] = jnp.zeros_like(acc)

        def add(k, carry):
            place = position(cols[k] ^ where[0])
            row = rows[k] ^ where[1]
            acc[row * n_row + place] += tiles[k].astype(F32)
            return carry

        lax.fori_loop(0, count[0], add, 0)

        def finish(p, carry):
            for row in range(n_col):
                tile = acc[row * n_row + p]
                lanes = pl.ds(pl.multiple_of(p * TILE, TILE), TILE)
                a_out[row * TILE : (row + 1) * TILE, lanes] = tile.astype(BF16)
                at_out[lanes, row * TILE : (row + 1) * TILE] = tile.T.astype(BF16)
            return carry

        lax.fori_loop(0, n_row, finish, 0)

    where = jnp.stack([me_row, me_col]).astype(jnp.int32)
    adjacency, adjacency_t = vmem_call(
        build,
        [((n_col * TILE, n_row * TILE), BF16), ((n_row * TILE, n_col * TILE), BF16)],
        where,
        tile_rows.reshape(-1),
        tile_cols.reshape(-1),
        tile_counts.reshape(-1),
        tile_values.reshape(slots, TILE, TILE),
        smem=4,
        scratch=[pltpu.VMEM((n_col * n_row, TILE, TILE), F32)],
    )
    masked_grad = cotangent.astype(F32) * node_mask.astype(F32)[:, None]

    def gather_rows(block):
        line = jnp.concatenate(
            [block] + [exchange(block, "row", z * z_step) for z in (1, 2, 3)], axis=0
        )
        for step in y_steps:
            line = jnp.concatenate([line, exchange(line, "row", step)], axis=0)
        return line, exchange(line, "row", 1)

    def forward_partial(near, far, a, *outs):
        cut = half * TILE
        total = jnp.dot(a[:, :cut], near[...], preferred_element_type=F32)
        total += jnp.dot(a[:, cut:], far[...], preferred_element_type=F32)
        outs[0][...] = total[:TILE]
        if n_col > 1:
            outs[1][...] = total[TILE:].astype(BF16)

    def reduce_cols(mine, rest):
        parts = [mine] + [rest[i * TILE : (i + 1) * TILE] for i in range(n_col - 1)]
        step = n_col // 2
        while step > 1:
            send = jnp.concatenate([p.astype(BF16) for p in parts[step : 2 * step]], axis=0)
            got = exchange(send, "col", step)
            parts = [
                parts[i].astype(F32) + got[i * TILE : (i + 1) * TILE].astype(F32) for i in range(step)
            ]
            step //= 2
        return parts[0], exchange(parts[1].astype(BF16), "col", 1)

    def advance(beta, last):
        def body(mine, got, w, anchor_ref, inject, *rest):
            u = mine[...] + got[...].astype(F32)
            pre = split_dot(u, w[...], ((1,), (0,))) + inject[...].astype(F32)
            bent = jnp.tanh(pre)
            outs = rest[1:] if last else rest
            outs[0][...] = (beta * anchor_ref[...].astype(F32) + (1.0 - beta) * bent).astype(BF16)
            if last:
                slope = 1.0 - bent * bent
                outs[1][...] = slope
                outs[2][...] = u
                outs[3][...] = (rest[0][...] * slope).astype(BF16)

        return body

    block = (TILE, hidden)
    state = anchor
    for step in range(ITERS):
        near, far = gather_rows(state)
        outs = [(block, F32), (((n_col - 1) * TILE, hidden), BF16)]
        mine, rest = vmem_call(forward_partial, outs, near, far, adjacency)
        mine, got = reduce_cols(mine, rest)
        beta = 1.0 / (step + 2.0)
        inputs = (mine, got, weight, anchor, injection)
        if step < ITERS - 1:
            (state,) = vmem_call(advance(beta, False), [(block, BF16)], *inputs)
        else:
            state, slope, mixed, scaled = vmem_call(
                advance(beta, True),
                [(block, BF16), (block, F32), (block, F32), (block, BF16)],
                *inputs,
                masked_grad,
            )

    def outer(u, h, out):
        out[...] = split_dot(u[...], h[...], ((0,), (0,)))

    def backward_partial(h, a_t, near, far):
        cut = half * TILE
        near[...] = jnp.dot(a_t[:cut], h[...], preferred_element_type=F32)
        far[...] = jnp.dot(a_t[cut:], h[...], preferred_element_type=F32).astype(BF16)

    def fold(kept, blocks):
        def body(held, got, keep, send):
            cut = blocks * TILE
            keep[...] = held[:cut] + got[:cut].astype(F32)
            send[...] = (held[cut : 2 * cut] + got[cut : 2 * cut].astype(F32)).astype(BF16)

        return body

    def pull(last):
        def body(held, got, r1, r2, r3, base, w, slope_ref, *outs):
            v = (held[...] + r1[...].astype(F32)) + (r2[...].astype(F32) + r3[...].astype(F32))
            g = base[...] + split_dot(v, w[...], ((1,), (1,)))
            outs[0][...] = g if last else (g * slope_ref[...]).astype(BF16)

        return body

    def gather_cols(value):
        step = 1
        while step < n_col:
            value = jnp.concatenate([value, exchange(value, "col", step)], axis=0)
            step *= 2
        return value

    for step in range(ADJOINT):
        last = step == ADJOINT - 1
        if last:
            (term,) = vmem_call(outer, [((hidden, hidden), F32)], mixed, scaled)
        block_states = gather_cols(scaled)
        near, far = vmem_call(
            backward_partial,
            [((half * TILE, hidden), F32), ((half * TILE, hidden), BF16)],
            block_states,
            adjacency_t,
        )
        held = near
        got = exchange(far, "row", 1)
        blocks = half
        for y_step in reversed(y_steps):
            blocks //= 2
            held, send = vmem_call(
                fold(held, blocks),
                [((blocks * TILE, hidden), F32), ((blocks * TILE, hidden), BF16)],
                held,
                got,
            )
            got = exchange(send, "row", y_step)
        total = held + got.astype(F32)
        parts = [total[i * TILE : (i + 1) * TILE] for i in range(4)]
        came = [exchange(parts[z].astype(BF16), "row", z * z_step) for z in (1, 2, 3)]
        (result,) = vmem_call(
            pull(last),
            [(block, F32 if last else BF16)],
            parts[0],
            parts[0],
            *came,
            masked_grad,
            weight,
            slope,
        )
        scaled = result
    adjoint = result

    col_steps = [1 << b for b in range(n_col.bit_length() - 1)]
    for axis, distance in [("col", s) for s in col_steps] + [("row", s) for s in [1] + y_steps]:
        term = term + exchange(term, axis, distance)
    others = [exchange(term, "row", z * z_step) for z in (1, 2, 3)]
    weight_grad = ((term + others[0]) + (others[1] + others[2])) / (own * n_col)
    return state, adjoint, weight_grad


def solution(mesh):
    in_specs = (
        P(("row", "col"), None),
        P(("row", "col"), None),
        P(),
        P(("row", "col"), None),
        P(("row", "col")),
        P("row", "col", None, None, None),
        P("row", "col", None),
        P("row", "col", None),
        P("row", "col"),
    )
    out_specs = (P(("row", "col"), None), P(("row", "col"), None), P())

    def whole(*args):
        return per_device(mesh.shape["row"], mesh.shape["col"], *args)

    return jax.shard_map(whole, mesh=mesh, in_specs=in_specs, out_specs=out_specs, check_vma=False)
```

time: 585 us -> 141 us (0.24)
  waiting for transfers between devices: 379 us -> 67.5 us
  blocking collectives: 84 us -> 0 us
  starting transfers between devices: 0.29 us -> 57 us
  other arithmetic: 57.4 us -> 1.74 us
  matrix products: 23.6 us -> 0 us
  local copies, waits for them, and re-layouts: 20.4 us -> 3.94 us
  between operations: 15 us -> 1.67 us
  Pallas kernels: 0 us -> 8.17 us
    reduce_scatter x6 -> x0, waiting for transfers between devices: 259 us -> none  [the longest x3 196 us: per_device(): lax.psum_scatter(partial_value, 'row', scatter_dimension=0, tiled=True)]
    psum x1 -> x0, waiting for transfers between devices: 120 us -> none  [per_device(): weight_grad = lax.psum(local_grad, ('row', 'col'))]
    all_gather x6 -> x0, blocking collectives: 84 us -> none  [the longest x3 70.3 us: per_device(): column_states = lax.all_gather(projected, 'row', axis=0, tiled=True)]
    ppermute x0 -> x42, waiting for transfers between devices: none -> 67.5 us  [exchange(): return lax.ppermute(value, axis, [(i, i ^ distance) for i in range(size)])]
    ppermute x0 -> x42, starting transfers between devices: none -> 57 us  [exchange(): return lax.ppermute(value, axis, [(i, i ^ distance) for i in range(size)])]
    scatter-add x12 -> x0, other arithmetic: 50 us -> none  [one_block(): total.at[some_out].add(product.reshape(block, -1) * some_alive[:, None])]
    dot_general x19 -> x0, matrix products: 23.6 us -> none  [the longest x12 16.1 us: one_block(): jnp.einsum(pattern, some_tiles, shaped[some_index], preferred_element_typ...]
    pallas_call x0 -> x17, Pallas kernels: none -> 8.17 us  [vmem_call(): pl.pallas_call(body, out_shape=[jax.ShapeDtypeStruct(shape, dtype) for sh...]
  transfers between devices with their start and end apart: 7 -> 42, of which waited for: 7 -> 29; matrix products, arithmetic and copies ran while one was open for 1% -> 1% of each run, Pallas kernels for 0% -> 2%
where the time goes in v1:
time: 141 us; the launch traced here: 140 us
  waiting for transfers between devices  67.5 us (48%)
  starting transfers between devices  57 us (40%)
  Pallas kernels  8.17 us (6%)
  local copies, waits for them, and re-layouts  3.94 us (3%)
  other arithmetic  1.74 us (1%)
  between operations  1.67 us (1%)
    ppermute x42, waiting for transfers between devices, exchange(): return lax.ppermute(value, axis, [(i, i ^ distance) for i in range(size)])  67.5 us
    ppermute x42, starting transfers between devices, exchange(): return lax.ppermute(value, axis, [(i, i ^ distance) for i in range(size)])  57 us
    pallas_call x17, Pallas kernels, vmem_call(): pl.pallas_call(body, out_shape=[jax.ShapeDtypeStruct(shape, dtype) for sh...  8.17 us
    unnamed x28, local copies, waits for them, and re-layouts  3.84 us
  transfers between devices with their start and end apart: 42, of which 29 were waited for; matrix products, arithmetic and copies ran while one was open for 1% of the time, Pallas kernels for 2%

profile of v1, /device:TPU:0, one launch (start us, length us, event | category | flops | bytes accessed | tf_op | source)
XLA Modules:
  0.0 140.1 jit_solution(15702832150735854650)
XLA Ops:
  0.6 3.1 %collective-permute-start = (bf16[128,128]{1,0:T(8,128)(2,1)}, bf16[128,128]{1,0:T(8,128)(2,1)S(1)}, u32[]{:S(2)}, u32[]{:S(2)}) collective-permute-start(bf16[128,128]{1,0:T(8,128)(2,1)} %anchor_ref.5), channel_id=1, source_target_pairs={{0,8},{2,10},{4,12},{6,14},{8,0},{10,2},{12,4},{14,6},{16,24},{18,... | collective-permute-start | bytes 98312 | tf_op jit(solution)/shard_map/ppermute | solution.py:52
  3.7 2.6 %collective-permute-start.1 = (bf16[128,128]{1,0:T(8,128)(2,1)}, bf16[128,128]{1,0:T(8,128)(2,1)S(1)}, u32[]{:S(2)}, u32[]{:S(2)}) collective-permute-start(bf16[128,128]{1,0:T(8,128)(2,1)} %anchor_ref.5), channel_id=1, source_target_pairs={{0,16},{2,18},{4,20},{6,22},{8,24},{10,26},{12,28},{14,30},{16,0},... | collective-permute-start | bytes 98312 | tf_op jit(solution)/shard_map/ppermute | solution.py:52
  7.1 2.2 %collective-permute-done.1 = bf16[128,128]{1,0:T(8,128)(2,1)S(1)} collective-permute-done((bf16[128,128]{1,0:T(8,128)(2,1)}, bf16[128,128]{1,0:T(8,128)(2,1)S(1)}, u32[]{:S(2)}, u32[]{:S(2)}) %collective-permute-start.1) | collective-permute-done | bytes 32800 | tf_op jit(solution)/shard_map/ppermute | solution.py:52
  9.3 2.9 %collective-permute-done.2 = bf16[128,128]{1,0:T(8,128)(2,1)S(1)} collective-permute-done((bf16[128,128]{1,0:T(8,128)(2,1)}, bf16[128,128]{1,0:T(8,128)(2,1)S(1)}, u32[]{:S(2)}, u32[]{:S(2)}) %collective-permute-start.2) | collective-permute-done | bytes 32800 | tf_op jit(solution)/shard_map/ppermute | solution.py:52
  14.7 3.4 %collective-permute-done.3 = bf16[512,128]{1,0:T(8,128)(2,1)S(1)} collective-permute-done((bf16[512,128]{1,0:T(8,128)(2,1)S(1)}, bf16[512,128]{1,0:T(8,128)(2,1)S(1)}, u32[]{:S(2)}, u32[]{:S(2)}) %collective-permute-start.3) | collective-permute-done | bytes 131104 | tf_op jit(solution)/shard_map/ppermute | solution.py:52
  21.8 3.0 %shard_map.112 = (bf16[256,2048]{1,0:T(8,128)(2,1)S(1)}, bf16[2048,256]{1,0:T(8,128)(2,1)S(1)}) custom-call(s32[2]{0:T(128)S(1)} %pad_add_fusion.where, s32[64]{0:T(128)S(1)} %bitcast.8, s32[64]{0:T(128)S(1)} %bitcast.9, s32[1]{0:T(128)} %bitcast.6.count, bf16[64,128,128]{2,1,0:T(8,128)(2,1)S(1)} %bitcast.7), custom_call_target="tpu_custom_call" | custom-call | tf_op jit(solution)/shard_map/pallas_call | solution.py:21
  25.3 2.2 %collective-permute-start.5 = (bf16[128,128]{1,0:T(8,128)(2,1)S(1)}, bf16[128,128]{1,0:T(8,128)(2,1)S(1)}, u32[]{:S(2)}, u32[]{:S(2)}) collective-permute-start(bf16[128,128]{1,0:T(8,128)(2,1)S(1)} %get-tuple-element.29), channel_id=1, source_target_pairs={{0,1},{1,0},{2,3},{3,2},{4,5},{5,4},{6,7},{7,6},{8,9},{9,8},{10,11... | collective-permute-start | bytes 98312 | tf_op jit(solution)/shard_map/ppermute | solution.py:52
  30.2 3.7 %collective-permute-start.8 = (bf16[128,128]{1,0:T(8,128)(2,1)S(1)}, bf16[128,128]{1,0:T(8,128)(2,1)S(1)}, u32[]{:S(2)}, u32[]{:S(2)}) collective-permute-start(bf16[128,128]{1,0:T(8,128)(2,1)S(1)} %shard_map.114), channel_id=1, source_target_pairs={{0,24},{2,26},{4,28},{6,30},{8,16},{10,18},{12,20},{14,22},{16,8},... | collective-permute-start | bytes 98312 | tf_op jit(solution)/shard_map/ppermute | solution.py:52
  36.2 1.9 %collective-permute-start.9 = (bf16[512,128]{1,0:T(8,128)(2,1)S(1)}, bf16[512,128]{1,0:T(8,128)(2,1)S(1)}, u32[]{:S(2)}, u32[]{:S(2)}) collective-permute-start(bf16[512,128]{1,0:T(8,128)(2,1)S(1)} %pad_maximum_fusion.1), channel_id=1, source_target_pairs={{0,4},{2,6},{4,0},{6,2},{8,12},{10,14},{12,8},{14,10},{16,20},{18,... | collective-permute-start | bytes 393224 | tf_op jit(solution)/shard_map/ppermute | solution.py:52
  38.2 3.1 %collective-permute-done.9 = bf16[512,128]{1,0:T(8,128)(2,1)S(1)} collective-permute-done((bf16[512,128]{1,0:T(8,128)(2,1)S(1)}, bf16[512,128]{1,0:T(8,128)(2,1)S(1)}, u32[]{:S(2)}, u32[]{:S(2)}) %collective-permute-start.9) | collective-permute-done | bytes 131104 | tf_op jit(solution)/shard_map/ppermute | solution.py:52
  43.3 2.1 %collective-permute-start.11 = (bf16[128,128]{1,0:T(8,128)(2,1)S(1)}, bf16[128,128]{1,0:T(8,128)(2,1)S(1)}, u32[]{:S(2)}, u32[]{:S(2)}) collective-permute-start(bf16[128,128]{1,0:T(8,128)(2,1)S(1)} %get-tuple-element.31), channel_id=1, source_target_pairs={{0,1},{1,0},{2,3},{3,2},{4,5},{5,4},{6,7},{7,6},{8,9},{9,8},{10,11... | collective-permute-start | bytes 98312 | tf_op jit(solution)/shard_map/ppermute | solution.py:52
  47.8 3.8 %collective-permute-start.13 = (bf16[128,128]{1,0:T(8,128)(2,1)S(1)}, bf16[128,128]{1,0:T(8,128)(2,1)S(1)}, u32[]{:S(2)}, u32[]{:S(2)}) collective-permute-start(bf16[128,128]{1,0:T(8,128)(2,1)S(1)} %shard_map.116), channel_id=1, source_target_pairs={{0,16},{2,18},{4,20},{6,22},{8,24},{10,26},{12,28},{14,30},{16,0},... | collective-permute-start | bytes 98312 | tf_op jit(solution)/shard_map/ppermute | solution.py:52
  53.5 3.8 %collective-permute-done.14 = bf16[128,128]{1,0:T(8,128)(2,1)S(1)} collective-permute-done((bf16[128,128]{1,0:T(8,128)(2,1)S(1)}, bf16[128,128]{1,0:T(8,128)(2,1)S(1)}, u32[]{:S(2)}, u32[]{:S(2)}) %collective-permute-start.14) | collective-permute-done | bytes 32800 | tf_op jit(solution)/shard_map/ppermute | solution.py:52
  57.3 1.9 %collective-permute-start.15 = (bf16[512,128]{1,0:T(8,128)(2,1)S(1)}, bf16[512,128]{1,0:T(8,128)(2,1)S(1)}, u32[]{:S(2)}, u32[]{:S(2)}) collective-permute-start(bf16[512,128]{1,0:T(8,128)(2,1)S(1)} %pad_maximum_fusion.2), channel_id=1, source_target_pairs={{0,4},{2,6},{4,0},{6,2},{8,12},{10,14},{12,8},{14,10},{16,20},{18,... | collective-permute-start | bytes 393224 | tf_op jit(solution)/shard_map/ppermute | solution.py:52
  59.2 3.1 %collective-permute-done.15 = bf16[512,128]{1,0:T(8,128)(2,1)S(1)} collective-permute-done((bf16[512,128]{1,0:T(8,128)(2,1)S(1)}, bf16[512,128]{1,0:T(8,128)(2,1)S(1)}, u32[]{:S(2)}, u32[]{:S(2)}) %collective-permute-start.15) | collective-permute-done | bytes 131104 | tf_op jit(solution)/shard_map/ppermute | solution.py:52
  64.4 2.1 %collective-permute-start.17 = (bf16[128,128]{1,0:T(8,128)(2,1)S(1)}, bf16[128,128]{1,0:T(8,128)(2,1)S(1)}, u32[]{:S(2)}, u32[]{:S(2)}) collective-permute-start(bf16[128,128]{1,0:T(8,128)(2,1)S(1)} %get-tuple-element.33), channel_id=1, source_target_pairs={{0,1},{1,0},{2,3},{3,2},{4,5},{5,4},{6,7},{7,6},{8,9},{9,8},{10,11... | collective-permute-start | bytes 98312 | tf_op jit(solution)/shard_map/ppermute | solution.py:52
  69.2 2.0 %collective-permute-start.18 = (bf16[128,128]{1,0:T(8,128)(2,1)S(1)}, bf16[128,128]{1,0:T(8,128)(2,1)S(1)}, u32[]{:S(2)}, u32[]{:S(2)}) collective-permute-start(bf16[128,128]{1,0:T(8,128)(2,1)S(1)} %get-tuple-element.35), channel_id=1, source_target_pairs={{0,1},{1,0},{2,3},{3,2},{4,5},{5,4},{6,7},{7,6},{8,9},{9,8},{10,11... | collective-permute-start | bytes 98312 | tf_op jit(solution)/shard_map/ppermute | solution.py:52
  77.1 3.8 %collective-permute-done.20 = bf16[512,128]{1,0:T(8,128)(2,1)S(1)} collective-permute-done((bf16[512,128]{1,0:T(8,128)(2,1)S(1)}, bf16[512,128]{1,0:T(8,128)(2,1)S(1)}, u32[]{:S(2)}, u32[]{:S(2)}) %collective-permute-start.20) | collective-permute-done | bytes 131104 | tf_op jit(solution)/shard_map/ppermute | solution.py:52
  81.9 3.5 %collective-permute-start.23 = (bf16[128,128]{1,0:T(8,128)(2,1)S(1)}, bf16[128,128]{1,0:T(8,128)(2,1)S(1)}, u32[]{:S(2)}, u32[]{:S(2)}) collective-permute-start(bf16[128,128]{1,0:T(8,128)(2,1)S(1)} %get-tuple-element.63), channel_id=1, source_target_pairs={{0,24},{2,26},{4,28},{6,30},{8,16},{10,18},{12,20},{14,22},{16,8},... | collective-permute-start | bytes 98312 | tf_op jit(solution)/shard_map/ppermute | solution.py:52
  87.8 2.0 %collective-permute-start.24 = (bf16[128,128]{1,0:T(8,128)(2,1)S(1)}, bf16[128,128]{1,0:T(8,128)(2,1)S(1)}, u32[]{:S(2)}, u32[]{:S(2)}) collective-permute-start(bf16[128,128]{1,0:T(8,128)(2,1)S(1)} %shard_map.121), channel_id=1, source_target_pairs={{0,1},{1,0},{2,3},{3,2},{4,5},{5,4},{6,7},{7,6},{8,9},{9,8},{10,11... | collective-permute-start | bytes 98312 | tf_op jit(solution)/shard_map/ppermute | solution.py:52
  89.8 2.0 %collective-permute-done.24 = bf16[128,128]{1,0:T(8,128)(2,1)S(1)} collective-permute-done((bf16[128,128]{1,0:T(8,128)(2,1)S(1)}, bf16[128,128]{1,0:T(8,128)(2,1)S(1)}, u32[]{:S(2)}, u32[]{:S(2)}) %collective-permute-start.24) | collective-permute-done | bytes 32800 | tf_op jit(solution)/shard_map/ppermute | solution.py:52
  95.7 3.8 %collective-permute-done.26 = bf16[512,128]{1,0:T(8,128)(2,1)S(1)} collective-permute-done((bf16[512,128]{1,0:T(8,128)(2,1)S(1)}, bf16[512,128]{1,0:T(8,128)(2,1)S(1)}, u32[]{:S(2)}, u32[]{:S(2)}) %collective-permute-start.26) | collective-permute-done | bytes 131104 | tf_op jit(solution)/shard_map/ppermute | solution.py:52
  99.8 3.8 %collective-permute-start.28 = (bf16[128,128]{1,0:T(8,128)(2,1)S(1)}, bf16[128,128]{1,0:T(8,128)(2,1)S(1)}, u32[]{:S(2)}, u32[]{:S(2)}) collective-permute-start(bf16[128,128]{1,0:T(8,128)(2,1)S(1)} %get-tuple-element.61), channel_id=1, source_target_pairs={{0,16},{2,18},{4,20},{6,22},{8,24},{10,26},{12,28},{14,30},{16,0},... | collective-permute-start | bytes 98312 | tf_op jit(solution)/shard_map/ppermute | solution.py:52
  105.5 3.8 %collective-permute-done.29.r3 = bf16[128,128]{1,0:T(8,128)(2,1)S(1)} collective-permute-done((bf16[128,128]{1,0:T(8,128)(2,1)S(1)}, bf16[128,128]{1,0:T(8,128)(2,1)S(1)}, u32[]{:S(2)}, u32[]{:S(2)}) %collective-permute-start.29) | collective-permute-done | bytes 32800 | tf_op jit(solution)/shard_map/ppermute | solution.py:52
  109.5 2.0 %collective-permute-start.30 = (bf16[128,128]{1,0:T(8,128)(2,1)S(1)}, bf16[128,128]{1,0:T(8,128)(2,1)S(1)}, u32[]{:S(2)}, u32[]{:S(2)}) collective-permute-start(bf16[128,128]{1,0:T(8,128)(2,1)S(1)} %shard_map.124.h), channel_id=1, source_target_pairs={{0,1},{1,0},{2,3},{3,2},{4,5},{5,4},{6,7},{7,6},{8,9},{9,8},{10,11... | collective-permute-start | bytes 98312 | tf_op jit(solution)/shard_map/ppermute | solution.py:52
  111.5 2.0 %collective-permute-done.30 = bf16[128,128]{1,0:T(8,128)(2,1)S(1)} collective-permute-done((bf16[128,128]{1,0:T(8,128)(2,1)S(1)}, bf16[128,128]{1,0:T(8,128)(2,1)S(1)}, u32[]{:S(2)}, u32[]{:S(2)}) %collective-permute-start.30) | collective-permute-done | bytes 32800 | tf_op jit(solution)/shard_map/ppermute | solution.py:52
  114.2 2.0 %collective-permute-start.36 = (f32[128,128]{1,0:T(8,128)S(1)}, f32[128,128]{1,0:T(8,128)S(1)}, u32[]{:S(2)}, u32[]{:S(2)}) collective-permute-start(f32[128,128]{1,0:T(8,128)S(1)} %shard_map.128), channel_id=1, source_target_pairs={{0,1},{1,0},{2,3},{3,2},{4,5},{5,4},{6,7},{7,6},{8,9},{9,8},{10,11... | collective-permute-start | bytes 196616 | tf_op jit(solution)/shard_map/ppermute | solution.py:52
  116.2 2.8 %collective-permute-done.36 = f32[128,128]{1,0:T(8,128)S(1)} collective-permute-done((f32[128,128]{1,0:T(8,128)S(1)}, f32[128,128]{1,0:T(8,128)S(1)}, u32[]{:S(2)}, u32[]{:S(2)}) %collective-permute-start.36) | collective-permute-done | bytes 65568 | tf_op jit(solution)/shard_map/ppermute | solution.py:52
  121.9 4.5 %collective-permute-done.38 = f32[128,128]{1,0:T(8,128)S(1)} collective-permute-done((f32[128,128]{1,0:T(8,128)S(1)}, f32[128,128]{1,0:T(8,128)S(1)}, u32[]{:S(2)}, u32[]{:S(2)}) %collective-permute-start.38) | collective-permute-done | bytes 65568 | tf_op jit(solution)/shard_map/ppermute | solution.py:52
  127.5 2.5 %collective-permute-start.39 = (f32[128,128]{1,0:T(8,128)S(1)}, f32[128,128]{1,0:T(8,128)S(1)}, u32[]{:S(2)}, u32[]{:S(2)}) collective-permute-start(f32[128,128]{1,0:T(8,128)S(1)} %add.32), channel_id=1, source_target_pairs={{0,8},{2,10},{4,12},{6,14},{8,0},{10,2},{12,4},{14,6},{16,24},{18,... | collective-permute-start | bytes 196616 | tf_op jit(solution)/shard_map/ppermute | solution.py:52
  131.6 2.0 %collective-permute-done.40 = f32[128,128]{1,0:T(8,128)S(1)} collective-permute-done((f32[128,128]{1,0:T(8,128)S(1)}, f32[128,128]{1,0:T(8,128)S(1)}, u32[]{:S(2)}, u32[]{:S(2)}) %collective-permute-start.40) | collective-permute-done | bytes 65568 | tf_op jit(solution)/shard_map/ppermute | solution.py:52
  136.1 3.2 %collective-permute-done.35.r3 = bf16[128,128]{1,0:T(8,128)(2,1)S(1)} collective-permute-done((bf16[128,128]{1,0:T(8,128)(2,1)S(1)}, bf16[128,128]{1,0:T(8,128)(2,1)S(1)}, u32[]{:S(2)}, u32[]{:S(2)}) %collective-permute-start.35) | collective-permute-done | bytes 32800 | tf_op jit(solution)/shard_map/ppermute | solution.py:52
  (122 shorter events, 47.8 us)
Async XLA Ops:
  0.6 6.5 %collective-permute-start = (bf16[128,128]{1,0:T(8,128)(2,1)}, bf16[128,128]{1,0:T(8,128)(2,1)S(1)}, u32[]{:S(2)}, u32[]{:S(2)}) collective-permute-start(bf16[128,128]{1,0:T(8,128)(2,1)} %anchor_ref.5), channel_id=1, source_target_pairs={{0,8},{2,10},{4,12},{6,14},{8,0},{10,2},{12,4},{14,6},{16,24},{18,... | collective-permute-start | bytes 98312 | tf_op jit(solution)/shard_map/ppermute | solution.py:52
  3.7 5.6 %collective-permute-start.1 = (bf16[128,128]{1,0:T(8,128)(2,1)}, bf16[128,128]{1,0:T(8,128)(2,1)S(1)}, u32[]{:S(2)}, u32[]{:S(2)}) collective-permute-start(bf16[128,128]{1,0:T(8,128)(2,1)} %anchor_ref.5), channel_id=1, source_target_pairs={{0,16},{2,18},{4,20},{6,22},{8,24},{10,26},{12,28},{14,30},{16,0},... | collective-permute-start | bytes 98312 | tf_op jit(solution)/shard_map/ppermute | solution.py:52
  6.3 5.9 %collective-permute-start.2 = (bf16[128,128]{1,0:T(8,128)(2,1)}, bf16[128,128]{1,0:T(8,128)(2,1)S(1)}, u32[]{:S(2)}, u32[]{:S(2)}) collective-permute-start(bf16[128,128]{1,0:T(8,128)(2,1)} %anchor_ref.5), channel_id=1, source_target_pairs={{0,24},{2,26},{4,28},{6,30},{8,16},{10,18},{12,20},{14,22},{16,8},... | collective-permute-start | bytes 98312 | tf_op jit(solution)/shard_map/ppermute | solution.py:52
  13.0 5.0 %collective-permute-start.3 = (bf16[512,128]{1,0:T(8,128)(2,1)S(1)}, bf16[512,128]{1,0:T(8,128)(2,1)S(1)}, u32[]{:S(2)}, u32[]{:S(2)}) collective-permute-start(bf16[512,128]{1,0:T(8,128)(2,1)S(1)} %pad_maximum_fusion), channel_id=1, source_target_pairs={{0,4},{2,6},{4,0},{6,2},{8,12},{10,14},{12,8},{14,10},{16,20},{18,... | collective-permute-start | bytes 393224 | tf_op jit(solution)/shard_map/ppermute | solution.py:52
  18.1 6.8 %collective-permute-start.4 = (bf16[1024,128]{1,0:T(8,128)(2,1)S(1)}, bf16[1024,128]{1,0:T(8,128)(2,1)S(1)}, u32[]{:S(2)}, u32[]{:S(2)}) collective-permute-start(bf16[1024,128]{1,0:T(8,128)(2,1)S(1)} %constant_dynamic-update-slice_fusion.near), channel_id=1, source_target_pairs={{0,2},{2,0},{4,6},{6,4},{8,10},{10,8},{12,14},{14,12},{16,18},{18,... | collective-permute-start | bytes 786440 | tf_op jit(solution)/shard_map/ppermute | solution.py:52
  25.3 4.0 %collective-permute-start.5 = (bf16[128,128]{1,0:T(8,128)(2,1)S(1)}, bf16[128,128]{1,0:T(8,128)(2,1)S(1)}, u32[]{:S(2)}, u32[]{:S(2)}) collective-permute-start(bf16[128,128]{1,0:T(8,128)(2,1)S(1)} %get-tuple-element.29), channel_id=1, source_target_pairs={{0,1},{1,0},{2,3},{3,2},{4,5},{5,4},{6,7},{7,6},{8,9},{9,8},{10,11... | collective-permute-start | bytes 98312 | tf_op jit(solution)/shard_map/ppermute | solution.py:52
  29.5 4.5 %collective-permute-start.6 = (bf16[128,128]{1,0:T(8,128)(2,1)S(1)}, bf16[128,128]{1,0:T(8,128)(2,1)S(1)}, u32[]{:S(2)}, u32[]{:S(2)}) collective-permute-start(bf16[128,128]{1,0:T(8,128)(2,1)S(1)} %shard_map.114), channel_id=1, source_target_pairs={{0,8},{2,10},{4,12},{6,14},{8,0},{10,2},{12,4},{14,6},{16,24},{18,... | collective-permute-start | bytes 98312 | tf_op jit(solution)/shard_map/ppermute | solution.py:52
  29.6 5.1 %collective-permute-start.7 = (bf16[128,128]{1,0:T(8,128)(2,1)S(1)}, bf16[128,128]{1,0:T(8,128)(2,1)S(1)}, u32[]{:S(2)}, u32[]{:S(2)}) collective-permute-start(bf16[128,128]{1,0:T(8,128)(2,1)S(1)} %shard_map.114), channel_id=1, source_target_pairs={{0,16},{2,18},{4,20},{6,22},{8,24},{10,26},{12,28},{14,30},{16,0},... | collective-permute-start | bytes 98312 | tf_op jit(solution)/shard_map/ppermute | solution.py:52
  30.2 6.0 %collective-permute-start.8 = (bf16[128,128]{1,0:T(8,128)(2,1)S(1)}, bf16[128,128]{1,0:T(8,128)(2,1)S(1)}, u32[]{:S(2)}, u32[]{:S(2)}) collective-permute-start(bf16[128,128]{1,0:T(8,128)(2,1)S(1)} %shard_map.114), channel_id=1, source_target_pairs={{0,24},{2,26},{4,28},{6,30},{8,16},{10,18},{12,20},{14,22},{16,8},... | collective-permute-start | bytes 98312 | tf_op jit(solution)/shard_map/ppermute | solution.py:52
  36.2 5.0 %collective-permute-start.9 = (bf16[512,128]{1,0:T(8,128)(2,1)S(1)}, bf16[512,128]{1,0:T(8,128)(2,1)S(1)}, u32[]{:S(2)}, u32[]{:S(2)}) collective-permute-start(bf16[512,128]{1,0:T(8,128)(2,1)S(1)} %pad_maximum_fusion.1), channel_id=1, source_target_pairs={{0,4},{2,6},{4,0},{6,2},{8,12},{10,14},{12,8},{14,10},{16,20},{18,... | collective-permute-start | bytes 393224 | tf_op jit(solution)/shard_map/ppermute | solution.py:52
  47.5 4.5 %collective-permute-start.12 = (bf16[128,128]{1,0:T(8,128)(2,1)S(1)}, bf16[128,128]{1,0:T(8,128)(2,1)S(1)}, u32[]{:S(2)}, u32[]{:S(2)}) collective-permute-start(bf16[128,128]{1,0:T(8,128)(2,1)S(1)} %shard_map.116), channel_id=1, source_target_pairs={{0,8},{2,10},{4,12},{6,14},{8,0},{10,2},{12,4},{14,6},{16,24},{18,... | collective-permute-start | bytes 98312 | tf_op jit(solution)/shard_map/ppermute | solution.py:52
  47.8 5.7 %collective-permute-start.13 = (bf16[128,128]{1,0:T(8,128)(2,1)S(1)}, bf16[128,128]{1,0:T(8,128)(2,1)S(1)}, u32[]{:S(2)}, u32[]{:S(2)}) collective-permute-start(bf16[128,128]{1,0:T(8,128)(2,1)S(1)} %shard_map.116), channel_id=1, source_target_pairs={{0,16},{2,18},{4,20},{6,22},{8,24},{10,26},{12,28},{14,30},{16,0},... | collective-permute-start | bytes 98312 | tf_op jit(solution)/shard_map/ppermute | solution.py:52
  51.6 5.7 %collective-permute-start.14 = (bf16[128,128]{1,0:T(8,128)(2,1)S(1)}, bf16[128,128]{1,0:T(8,128)(2,1)S(1)}, u32[]{:S(2)}, u32[]{:S(2)}) collective-permute-start(bf16[128,128]{1,0:T(8,128)(2,1)S(1)} %shard_map.116), channel_id=1, source_target_pairs={{0,24},{2,26},{4,28},{6,30},{8,16},{10,18},{12,20},{14,22},{16,8},... | collective-permute-start | bytes 98312 | tf_op jit(solution)/shard_map/ppermute | solution.py:52
  57.3 5.0 %collective-permute-start.15 = (bf16[512,128]{1,0:T(8,128)(2,1)S(1)}, bf16[512,128]{1,0:T(8,128)(2,1)S(1)}, u32[]{:S(2)}, u32[]{:S(2)}) collective-permute-start(bf16[512,128]{1,0:T(8,128)(2,1)S(1)} %pad_maximum_fusion.2), channel_id=1, source_target_pairs={{0,4},{2,6},{4,0},{6,2},{8,12},{10,14},{12,8},{14,10},{16,20},{18,... | collective-permute-start | bytes 393224 | tf_op jit(solution)/shard_map/ppermute | solution.py:52
  75.2 5.7 %collective-permute-start.20 = (bf16[512,128]{1,0:T(8,128)(2,1)S(1)}, bf16[512,128]{1,0:T(8,128)(2,1)S(1)}, u32[]{:S(2)}, u32[]{:S(2)}) collective-permute-start(bf16[512,128]{1,0:T(8,128)(2,1)S(1)} %get-tuple-element.40), channel_id=1, source_target_pairs={{0,4},{2,6},{4,0},{6,2},{8,12},{10,14},{12,8},{14,10},{16,20},{18,... | collective-permute-start | bytes 393224 | tf_op jit(solution)/shard_map/ppermute | solution.py:52
  80.9 4.5 %collective-permute-start.21 = (bf16[128,128]{1,0:T(8,128)(2,1)S(1)}, bf16[128,128]{1,0:T(8,128)(2,1)S(1)}, u32[]{:S(2)}, u32[]{:S(2)}) collective-permute-start(bf16[128,128]{1,0:T(8,128)(2,1)S(1)} %get-tuple-element.65), channel_id=1, source_target_pairs={{0,8},{2,10},{4,12},{6,14},{8,0},{10,2},{12,4},{14,6},{16,24},{18,... | collective-permute-start | bytes 98312 | tf_op jit(solution)/shard_map/ppermute | solution.py:52
  81.0 5.1 %collective-permute-start.22 = (bf16[128,128]{1,0:T(8,128)(2,1)S(1)}, bf16[128,128]{1,0:T(8,128)(2,1)S(1)}, u32[]{:S(2)}, u32[]{:S(2)}) collective-permute-start(bf16[128,128]{1,0:T(8,128)(2,1)S(1)} %get-tuple-element.64), channel_id=1, source_target_pairs={{0,16},{2,18},{4,20},{6,22},{8,24},{10,26},{12,28},{14,30},{16,0},... | collective-permute-start | bytes 98312 | tf_op jit(solution)/shard_map/ppermute | solution.py:52
  81.9 5.7 %collective-permute-start.23 = (bf16[128,128]{1,0:T(8,128)(2,1)S(1)}, bf16[128,128]{1,0:T(8,128)(2,1)S(1)}, u32[]{:S(2)}, u32[]{:S(2)}) collective-permute-start(bf16[128,128]{1,0:T(8,128)(2,1)S(1)} %get-tuple-element.63), channel_id=1, source_target_pairs={{0,24},{2,26},{4,28},{6,30},{8,16},{10,18},{12,20},{14,22},{16,8},... | collective-permute-start | bytes 98312 | tf_op jit(solution)/shard_map/ppermute | solution.py:52
  93.9 5.6 %collective-permute-start.26 = (bf16[512,128]{1,0:T(8,128)(2,1)S(1)}, bf16[512,128]{1,0:T(8,128)(2,1)S(1)}, u32[]{:S(2)}, u32[]{:S(2)}) collective-permute-start(bf16[512,128]{1,0:T(8,128)(2,1)S(1)} %get-tuple-element.45), channel_id=1, source_target_pairs={{0,4},{2,6},{4,0},{6,2},{8,12},{10,14},{12,8},{14,10},{16,20},{18,... | collective-permute-start | bytes 393224 | tf_op jit(solution)/shard_map/ppermute | solution.py:52
  99.6 4.5 %collective-permute-start.27 = (bf16[128,128]{1,0:T(8,128)(2,1)S(1)}, bf16[128,128]{1,0:T(8,128)(2,1)S(1)}, u32[]{:S(2)}, u32[]{:S(2)}) collective-permute-start(bf16[128,128]{1,0:T(8,128)(2,1)S(1)} %get-tuple-element.62), channel_id=1, source_target_pairs={{0,8},{2,10},{4,12},{6,14},{8,0},{10,2},{12,4},{14,6},{16,24},{18,... | collective-permute-start | bytes 98312 | tf_op jit(solution)/shard_map/ppermute | solution.py:52
  99.8 5.7 %collective-permute-start.28 = (bf16[128,128]{1,0:T(8,128)(2,1)S(1)}, bf16[128,128]{1,0:T(8,128)(2,1)S(1)}, u32[]{:S(2)}, u32[]{:S(2)}) collective-permute-start(bf16[128,128]{1,0:T(8,128)(2,1)S(1)} %get-tuple-element.61), channel_id=1, source_target_pairs={{0,16},{2,18},{4,20},{6,22},{8,24},{10,26},{12,28},{14,30},{16,0},... | collective-permute-start | bytes 98312 | tf_op jit(solution)/shard_map/ppermute | solution.py:52
  103.6 5.7 %collective-permute-start.29 = (bf16[128,128]{1,0:T(8,128)(2,1)S(1)}, bf16[128,128]{1,0:T(8,128)(2,1)S(1)}, u32[]{:S(2)}, u32[]{:S(2)}) collective-permute-start(bf16[128,128]{1,0:T(8,128)(2,1)S(1)} %get-tuple-element.60), channel_id=1, source_target_pairs={{0,24},{2,26},{4,28},{6,30},{8,16},{10,18},{12,20},{14,22},{16,8},... | collective-permute-start | bytes 98312 | tf_op jit(solution)/shard_map/ppermute | solution.py:52
  113.9 5.1 %collective-permute-start.31 = (bf16[1024,128]{1,0:T(8,128)(2,1)S(1)}, bf16[1024,128]{1,0:T(8,128)(2,1)S(1)}, u32[]{:S(2)}, u32[]{:S(2)}) collective-permute-start(bf16[1024,128]{1,0:T(8,128)(2,1)S(1)} %get-tuple-element.47), channel_id=1, source_target_pairs={{0,2},{2,0},{4,6},{6,4},{8,10},{10,8},{12,14},{14,12},{16,18},{18,... | collective-permute-start | bytes 786440 | tf_op jit(solution)/shard_map/ppermute | solution.py:52
  114.2 4.7 %collective-permute-start.36 = (f32[128,128]{1,0:T(8,128)S(1)}, f32[128,128]{1,0:T(8,128)S(1)}, u32[]{:S(2)}, u32[]{:S(2)}) collective-permute-start(f32[128,128]{1,0:T(8,128)S(1)} %shard_map.128), channel_id=1, source_target_pairs={{0,1},{1,0},{2,3},{3,2},{4,5},{5,4},{6,7},{7,6},{8,9},{9,8},{10,11... | collective-permute-start | bytes 196616 | tf_op jit(solution)/shard_map/ppermute | solution.py:52
  119.1 10.9 %collective-permute-start.32 = (bf16[512,128]{1,0:T(8,128)(2,1)S(1)}, bf16[512,128]{1,0:T(8,128)(2,1)S(1)}, u32[]{:S(2)}, u32[]{:S(2)}) collective-permute-start(bf16[512,128]{1,0:T(8,128)(2,1)S(1)} %get-tuple-element.49), channel_id=1, source_target_pairs={{0,4},{2,6},{4,0},{6,2},{8,12},{10,14},{12,8},{14,10},{16,20},{18,... | collective-permute-start | bytes 393224 | tf_op jit(solution)/shard_map/ppermute | solution.py:52
  120.7 5.7 %collective-permute-start.38 = (f32[128,128]{1,0:T(8,128)S(1)}, f32[128,128]{1,0:T(8,128)S(1)}, u32[]{:S(2)}, u32[]{:S(2)}) collective-permute-start(f32[128,128]{1,0:T(8,128)S(1)} %add.31), channel_id=1, source_target_pairs={{0,4},{2,6},{4,0},{6,2},{8,12},{10,14},{12,8},{14,10},{16,20},{18,... | collective-permute-start | bytes 196616 | tf_op jit(solution)/shard_map/ppermute | solution.py:52
  126.5 7.1 %collective-permute-start.40 = (f32[128,128]{1,0:T(8,128)S(1)}, f32[128,128]{1,0:T(8,128)S(1)}, u32[]{:S(2)}, u32[]{:S(2)}) collective-permute-start(f32[128,128]{1,0:T(8,128)S(1)} %add.32), channel_id=1, source_target_pairs={{0,16},{2,18},{4,20},{6,22},{8,24},{10,26},{12,28},{14,30},{16,0},... | collective-permute-start | bytes 196616 | tf_op jit(solution)/shard_map/ppermute | solution.py:52
  126.6 8.8 %collective-permute-start.41 = (f32[128,128]{1,0:T(8,128)S(1)}, f32[128,128]{1,0:T(8,128)S(1)}, u32[]{:S(2)}, u32[]{:S(2)}) collective-permute-start(f32[128,128]{1,0:T(8,128)S(1)} %add.32), channel_id=1, source_target_pairs={{0,24},{2,26},{4,28},{6,30},{8,16},{10,18},{12,20},{14,22},{16,8},... | collective-permute-start | bytes 196616 | tf_op jit(solution)/shard_map/ppermute | solution.py:52
  127.5 7.9 %collective-permute-start.39 = (f32[128,128]{1,0:T(8,128)S(1)}, f32[128,128]{1,0:T(8,128)S(1)}, u32[]{:S(2)}, u32[]{:S(2)}) collective-permute-start(f32[128,128]{1,0:T(8,128)S(1)} %add.32), channel_id=1, source_target_pairs={{0,8},{2,10},{4,12},{6,14},{8,0},{10,2},{12,4},{14,6},{16,24},{18,... | collective-permute-start | bytes 196616 | tf_op jit(solution)/shard_map/ppermute | solution.py:52
  130.1 6.0 %collective-permute-start.33 = (bf16[128,128]{1,0:T(8,128)(2,1)S(1)}, bf16[128,128]{1,0:T(8,128)(2,1)S(1)}, u32[]{:S(2)}, u32[]{:S(2)}) collective-permute-start(bf16[128,128]{1,0:T(8,128)(2,1)S(1)} %get-tuple-element.59), channel_id=1, source_target_pairs={{0,8},{2,10},{4,12},{6,14},{8,0},{10,2},{12,4},{14,6},{16,24},{18,... | collective-permute-start | bytes 98312 | tf_op jit(solution)/shard_map/ppermute | solution.py:52
  130.2 5.9 %collective-permute-start.34 = (bf16[128,128]{1,0:T(8,128)(2,1)S(1)}, bf16[128,128]{1,0:T(8,128)(2,1)S(1)}, u32[]{:S(2)}, u32[]{:S(2)}) collective-permute-start(bf16[128,128]{1,0:T(8,128)(2,1)S(1)} %get-tuple-element.58), channel_id=1, source_target_pairs={{0,16},{2,18},{4,20},{6,22},{8,24},{10,26},{12,28},{14,30},{16,0},... | collective-permute-start | bytes 98312 | tf_op jit(solution)/shard_map/ppermute | solution.py:52
  133.6 5.7 %collective-permute-start.35 = (bf16[128,128]{1,0:T(8,128)(2,1)S(1)}, bf16[128,128]{1,0:T(8,128)(2,1)S(1)}, u32[]{:S(2)}, u32[]{:S(2)}) collective-permute-start(bf16[128,128]{1,0:T(8,128)(2,1)S(1)} %get-tuple-element.57), channel_id=1, source_target_pairs={{0,24},{2,26},{4,28},{6,30},{8,16},{10,18},{12,20},{14,22},{16,8},... | collective-permute-start | bytes 98312 | tf_op jit(solution)/shard_map/ppermute | solution.py:52
  (18 other events, 142.3 us)

commit v2 on v0

v2 whole, which is shorter than its diff:
```python
import jax
import jax.numpy as jnp
from jax import lax
from jax.experimental import pallas as pl
from jax.experimental.pallas import tpu as pltpu
from jax.sharding import PartitionSpec as P

TILE = 128
ITERS = 3
ADJOINT = 3
LINE = 4
BF16 = jnp.bfloat16
F32 = jnp.float32
VMEM_LIMIT = 48 * 2**20


def vmem_call(body, outs, *args, smem=0, scratch=()):
    specs = [
        pl.BlockSpec(memory_space=pltpu.SMEM if i < smem else pltpu.VMEM) for i in range(len(args))
    ]
    out_specs = [pl.BlockSpec(memory_space=pltpu.VMEM) for _ in outs]
    return pl.pallas_call(
        body,
        out_shape=[jax.ShapeDtypeStruct(shape, dtype) for shape, dtype in outs],
        in_specs=specs,
        out_specs=out_specs,
        scratch_shapes=list(scratch),
        compiler_params=pltpu.CompilerParams(vmem_limit_bytes=VMEM_LIMIT),
    )(*args)


def halves(value):
    high = value.astype(BF16)
    return high, (value - high.astype(F32)).astype(BF16)


def split_dot(value, factor, dims):
    high, low = halves(value)
    return lax.dot_general(high, factor, (dims, ((), ())), preferred_element_type=F32) + lax.dot_general(
        low, factor, (dims, ((), ())), preferred_element_type=F32
    )


def tree_sum(values):
    while len(values) > 1:
        values = [values[i] + values[i + 1] for i in range(0, len(values), 2)]
    return values[0]


def per_device(n_row, n_col, *args):
    anchor, injection, weight, cotangent, node_mask, tile_values, tile_rows, tile_cols, tile_counts = args
    own, hidden = anchor.shape
    assert own == TILE
    slots = tile_values.shape[2]
    z_step = n_row // LINE
    n_y = z_step // 2
    square = [(y, x) for y in range(n_y) for x in range(n_col)]
    line_rows = LINE * TILE
    block = (TILE, hidden)
    where = jnp.stack([lax.axis_index("row"), lax.axis_index("col")]).astype(jnp.int32)

    def exchange(value, row_xor, col_xor=0):
        if col_xor == 0:
            return lax.ppermute(value, "row", [(i, i ^ row_xor) for i in range(n_row)])
        if row_xor == 0:
            return lax.ppermute(value, "col", [(i, i ^ col_xor) for i in range(n_col)])
        pairs = [
            (r * n_col + c, (r ^ row_xor) * n_col + (c ^ col_xor))
            for r in range(n_row)
            for c in range(n_col)
        ]
        return lax.ppermute(value, ("row", "col"), pairs)

    def along_line(values):
        return [exchange(v, z * z_step) for z, v in zip(range(1, LINE), values)]

    def to_square(values):
        return [exchange(v, 2 * y, x) for (y, x), v in zip(square[1:], values)]

    def build(where_ref, rows, cols, count, tiles, *refs):
        parts, turned, acc = refs[:n_y], refs[n_y], refs[n_y + 1]
        acc[...] = jnp.zeros_like(acc)

        def add(k, carry):
            s = cols[k] ^ where_ref[0]
            x = rows[k] ^ where_ref[1]
            y = (s // 2) % n_y
            acc[((y * n_col + x) * 2 + s % 2) * LINE + s // z_step] += tiles[k].astype(F32)
            return carry

        lax.fori_loop(0, count[0], add, 0)
        for y in range(n_y):
            for x in range(n_col):
                for p in range(2 * LINE):
                    tile = acc[(y * n_col + x) * 2 * LINE + p]
                    here, there = slice(x * TILE, (x + 1) * TILE), slice(p * TILE, (p + 1) * TILE)
                    parts[y][here, there] = tile.astype(BF16)
                    if y == 0:
                        turned[there, here] = tile.T.astype(BF16)

    part_shape = (n_col * TILE, 2 * line_rows)
    *parts, turned = vmem_call(
        build,
        [(part_shape, BF16)] * n_y + [(part_shape[::-1], BF16)],
        where,
        tile_rows.reshape(-1),
        tile_cols.reshape(-1),
        tile_counts.reshape(-1),
        tile_values.reshape(slots, TILE, TILE),
        smem=4,
        scratch=[pltpu.VMEM((n_y * n_col * 2 * LINE, TILE, TILE), F32)],
    )
    masked_grad = cotangent.astype(F32) * node_mask.astype(F32)[:, None]

    def first_partial(near, far, *refs):
        a, outs = refs[:n_y], refs[n_y:]
        total = jnp.zeros((n_col * TILE, hidden), F32)
        for y in range(n_y):
            rows = slice(y * line_rows, (y + 1) * line_rows)
            total += jnp.dot(a[y][:, :line_rows], near[rows], preferred_element_type=F32)
            total += jnp.dot(a[y][:, line_rows:], far[rows], preferred_element_type=F32)
        outs[0][...] = total[:TILE]
        for x in range(1, n_col):
            outs[x][...] = total[x * TILE : (x + 1) * TILE].astype(BF16)

    def forward_partial(z0, z1, z2, z3, far, *refs):
        a, outs = refs[:n_y], refs[n_y:]
        near = jnp.concatenate([z0[...], z1[...], z2[...], z3[...]], axis=0)
        for y in range(n_y):
            total = jnp.dot(a[y][:, :line_rows], near, preferred_element_type=F32)
            total += jnp.dot(a[y][:, line_rows:], far[...], preferred_element_type=F32)
            for x in range(n_col):
                out = outs[y * n_col + x]
                out[...] = total[x * TILE : (x + 1) * TILE].astype(out.dtype)

    def advance(beta, last, peers):
        def body(*refs):
            sums, (w, anchor_ref, inject), rest = refs[:peers], refs[peers : peers + 3], refs[peers + 3 :]
            u = tree_sum([s[...].astype(F32) for s in sums])
            pre = split_dot(u, w[...], ((1,), (0,))) + inject[...].astype(F32)
            bent = jnp.tanh(pre)
            outs = rest[1:] if last else rest
            outs[0][...] = (beta * anchor_ref[...].astype(F32) + (1.0 - beta) * bent).astype(BF16)
            if last:
                slope = 1.0 - bent * bent
                outs[1][...] = slope
                outs[2][...] = u
                outs[3][...] = (rest[0][...] * slope).astype(BF16)

        return body

    state = anchor
    for step in range(ITERS):
        line = [state] + along_line([state] * (LINE - 1))
        if step == 0:
            joined = jnp.concatenate(line, axis=0)
            joined, *parts, turned = lax.optimization_barrier((joined, *parts, turned))
            bit = 2
            while bit < z_step:
                joined = jnp.concatenate([joined, exchange(joined, bit)], axis=0)
                bit *= 2
            joined, *sent = lax.optimization_barrier((joined, *parts[1:]))
            far = exchange(joined, 1)
            outs = [(block, F32)] + [(block, BF16)] * (n_col - 1)
            mine, *sends = vmem_call(first_partial, outs, joined, far, *parts)
            parts = [parts[0]] + [exchange(p, 2 * (i + 1)) for i, p in enumerate(sent)]
            got = [exchange(v, 0, x + 1) for x, v in enumerate(sends)]
        else:
            far = exchange(jnp.concatenate(line, axis=0), 1)
            outs = [(block, F32)] + [(block, BF16)] * (len(square) - 1)
            mine, *sends = vmem_call(forward_partial, outs, *line, far, *parts)
            got = to_square(sends)
        last = step == ITERS - 1
        results = [(block, BF16)] + ([(block, F32), (block, F32), (block, BF16)] if last else [])
        state, *rest = vmem_call(
            advance(1.0 / (step + 2.0), last, 1 + len(got)),
            results,
            mine,
            *got,
            weight,
            anchor,
            injection,
            *([masked_grad] if last else []),
        )
    slope, mixed, scaled = rest

    def turn(*refs):
        for part, out in zip(refs[: n_y - 1], refs[n_y - 1 :]):
            for x in range(n_col):
                for p in range(2 * LINE):
                    here, there = slice(x * TILE, (x + 1) * TILE), slice(p * TILE, (p + 1) * TILE)
                    out[there, here] = part[here, there].T

    turned = [turned] + list(vmem_call(turn, [(part_shape[::-1], BF16)] * (n_y - 1), *parts[1:]))

    def backward_partial(last):
        def body(*refs):
            n = len(square)
            h, a_t, (near, far, *term) = refs[:n], refs[n : n + n_y], refs[n + n_y :]
            total = None
            for y in range(n_y):
                joined = jnp.concatenate([h[y * n_col + x][:TILE] for x in range(n_col)], axis=0)
                product = jnp.dot(a_t[y][...], joined, preferred_element_type=F32)
                total = product if total is None else total + product
            near[...] = total[:line_rows]
            far[:line_rows] = total[line_rows:].astype(BF16)
            if last:
                whole = tree_sum([v[TILE:].astype(F32) for v in h])
                high, low = halves(whole)
                far[line_rows : line_rows + hidden] = high
                far[line_rows + hidden :] = low
                term[0][...] = high.astype(F32) + low.astype(F32)

        return body

    def fold(last):
        def body(held, got, *refs):
            outs = refs[1:] if last else refs
            for z in range(LINE):
                rows = slice(z * TILE, (z + 1) * TILE)
                value = held[rows] + got[rows].astype(F32)
                if z == 0:
                    outs[0][...] = value
                else:
                    outs[z][:TILE] = value.astype(BF16)
            if last:
                high, low = got[line_rows : line_rows + hidden], got[line_rows + hidden :]
                term = (refs[0][...] + (high.astype(F32) + low.astype(F32))).astype(BF16)
                outs[LINE][...] = term.astype(F32)
                for z in range(1, LINE):
                    outs[z][TILE:] = term

        return body

    def pull(last, ride):
        def body(held, *refs):
            got, rest = refs[: LINE - 1], refs[LINE - 1 :]
            v = tree_sum([held[...]] + [r[:TILE].astype(F32) for r in got])
            base, w, slope_ref = rest[:3]
            g = base[...] + split_dot(v, w[...], ((1,), (1,)))
            if last:
                term, adjoint_out, grad_out = rest[3:]
                adjoint_out[...] = g
                whole = tree_sum([term[...]] + [r[TILE:].astype(F32) for r in got])
                grad_out[...] = whole / (own * n_col)
            else:
                out = rest[-1]
                h = (g * slope_ref[...]).astype(BF16)
                out[:TILE] = h
                if ride:
                    out[TILE:] = split_dot(rest[3][...], h, ((0,), (0,))).astype(BF16)

        return body

    for step in range(ADJOINT):
        last, ride = step == ADJOINT - 1, step == ADJOINT - 2
        states = [scaled] + to_square([scaled] * (len(square) - 1))
        extra = 2 * hidden if last else 0
        near, far, *term = vmem_call(
            backward_partial(last),
            [((line_rows, hidden), F32), ((line_rows + extra, hidden), BF16)]
            + ([((hidden, hidden), F32)] if last else []),
            *states,
            *turned,
        )
        got = exchange(far, 1)
        extra = hidden if last else 0
        held, *sends = vmem_call(
            fold(last),
            [(block, F32)]
            + [((TILE + extra, hidden), BF16)] * (LINE - 1)
            + ([((hidden, hidden), F32)] if last else []),
            near,
            got,
            *term,
        )
        if last:
            *sends, total = sends
        got = along_line(sends)
        inputs = (held, *got, masked_grad, weight, slope)
        if last:
            adjoint, weight_grad = vmem_call(
                pull(True, False), [(block, F32), ((hidden, hidden), F32)], *inputs, total
            )
        else:
            rows = TILE + (hidden if ride else 0)
            (scaled,) = vmem_call(
                pull(False, ride), [((rows, hidden), BF16)], *inputs, *([mixed] if ride else [])
            )
    return state, adjoint, weight_grad


def solution(mesh):
    in_specs = (
        P(("row", "col"), None),
        P(("row", "col"), None),
        P(),
        P(("row", "col"), None),
        P(("row", "col")),
        P("row", "col", None, None, None),
        P("row", "col", None),
        P("row", "col", None),
        P("row", "col"),
    )
    out_specs = (P(("row", "col"), None), P(("row", "col"), None), P())

    def whole(*args):
        return per_device(mesh.shape["row"], mesh.shape["col"], *args)

    return jax.shard_map(whole, mesh=mesh, in_specs=in_specs, out_specs=out_specs, check_vma=False)
```

time: 585 us -> 114 us (0.19)
  waiting for transfers between devices: 379 us -> 50.8 us
  blocking collectives: 84 us -> 0 us
  other arithmetic: 57.4 us -> 0.2 us
  starting transfers between devices: 0.29 us -> 51.1 us
  matrix products: 23.6 us -> 0 us
  local copies, waits for them, and re-layouts: 20.4 us -> 2.92 us
  between operations: 15 us -> 1.56 us
  Pallas kernels: 0 us -> 7.25 us
    reduce_scatter x6 -> x0, waiting for transfers between devices: 259 us -> none  [the longest x3 196 us: per_device(): lax.psum_scatter(partial_value, 'row', scatter_dimension=0, tiled=True)]
    psum x1 -> x0, waiting for transfers between devices: 120 us -> none  [per_device(): weight_grad = lax.psum(local_grad, ('row', 'col'))]
    all_gather x6 -> x0, blocking collectives: 84 us -> none  [the longest x3 70.3 us: per_device(): column_states = lax.all_gather(projected, 'row', axis=0, tiled=True)]
    ppermute x0 -> x42, starting transfers between devices: none -> 51.1 us  [the longest x31 37.9 us: exchange(): return lax.ppermute(value, 'row', [(i, i ^ row_xor) for i in range(n_row)])]
    ppermute x0 -> x42, waiting for transfers between devices: none -> 50.8 us  [the longest x31 35.9 us: exchange(): return lax.ppermute(value, 'row', [(i, i ^ row_xor) for i in range(n_row)])]
    scatter-add x12 -> x0, other arithmetic: 50 us -> none  [one_block(): total.at[some_out].add(product.reshape(block, -1) * some_alive[:, None])]
    dot_general x19 -> x0, matrix products: 23.6 us -> none  [the longest x12 16.1 us: one_block(): jnp.einsum(pattern, some_tiles, shaped[some_index], preferred_element_typ...]
    gather x12 -> x0, local copies, waits for them, and re-layouts: 7.77 us -> none  [one_block(): shaped[some_index]]
  transfers between devices with their start and end apart: 7 -> 42, of which waited for: 7 -> 33; matrix products, arithmetic and copies ran while one was open for 1% -> 0% of each run, Pallas kernels for 0% -> 2%
where the time goes in v2:
time: 114 us
  starting transfers between devices  51.1 us (45%)
  waiting for transfers between devices  50.8 us (45%)
  Pallas kernels  7.25 us (6%)
  local copies, waits for them, and re-layouts  2.92 us (3%)
  between operations  1.56 us (1%)
    ppermute x31, starting transfers between devices, exchange(): return lax.ppermute(value, 'row', [(i, i ^ row_xor) for i in range(n_row)])  37.9 us
    ppermute x31, waiting for transfers between devices, exchange(): return lax.ppermute(value, 'row', [(i, i ^ row_xor) for i in range(n_row)])  35.9 us
    ppermute x5, waiting for transfers between devices, exchange(): return lax.ppermute(value, ('row', 'col'), pairs)  9.62 us
    pallas_call x17, Pallas kernels, vmem_call(): pl.pallas_call(body, out_shape=[jax.ShapeDtypeStruct(shape, dtype) for sh...  7.25 us
    ppermute x5, starting transfers between devices, exchange(): return lax.ppermute(value, ('row', 'col'), pairs)  6.74 us
    ppermute x6, starting transfers between devices, exchange(): return lax.ppermute(value, 'col', [(i, i ^ col_xor) for i in range(n_col)])  6.52 us
    ppermute x6, waiting for transfers between devices, exchange(): return lax.ppermute(value, 'col', [(i, i ^ col_xor) for i in range(n_col)])  5.24 us
    unnamed x16, local copies, waits for them, and re-layouts  2.92 us
  transfers between devices with their start and end apart: 42, of which 33 were waited for; matrix products, arithmetic and copies ran while one was open for 0% of the time, Pallas kernels for 2%

profile of v2, /device:TPU:0, one launch (start us, length us, event | category | flops | bytes accessed | tf_op | source)
XLA Modules:
  0.0 113.9 jit_solution(17282939423125253184)
XLA Ops:
  0.6 3.1 %collective-permute-start = (bf16[128,128]{1,0:T(8,128)(2,1)}, bf16[128,128]{1,0:T(8,128)(2,1)S(1)}, u32[]{:S(2)}, u32[]{:S(2)}) collective-permute-start(bf16[128,128]{1,0:T(8,128)(2,1)} %refs_5_.3), channel_id=1, source_target_pairs={{0,8},{2,10},{4,12},{6,14},{8,0},{10,2},{12,4},{14,6},{16,24},{18,... | collective-permute-start | bytes 98312 | tf_op jit(solution)/shard_map/ppermute | solution.py:64
  3.7 2.6 %collective-permute-start.1 = (bf16[128,128]{1,0:T(8,128)(2,1)}, bf16[128,128]{1,0:T(8,128)(2,1)S(1)}, u32[]{:S(2)}, u32[]{:S(2)}) collective-permute-start(bf16[128,128]{1,0:T(8,128)(2,1)} %refs_5_.3), channel_id=1, source_target_pairs={{0,16},{2,18},{4,20},{6,22},{8,24},{10,26},{12,28},{14,30},{16,0},... | collective-permute-start | bytes 98312 | tf_op jit(solution)/shard_map/ppermute | solution.py:64
  7.0 1.6 %copy-done = bf16[1,1,64,128,128]{4,3,2,1,0:T(8,128)(2,1)S(1)} copy-done((bf16[1,1,64,128,128]{4,3,2,1,0:T(8,128)(2,1)S(1)}, bf16[1,1,64,128,128]{4,3,2,1,0:T(8,128)(2,1)}, u32[]{:S(2)}) %copy-start) | copy-done | bytes 2097176
  10.0 2.0 %shard_map.112 = (bf16[256,1024]{1,0:T(8,128)(2,1)S(1)}, bf16[256,1024]{1,0:T(8,128)(2,1)S(1)}, bf16[1024,256]{1,0:T(8,128)(2,1)S(1)}) custom-call(s32[2]{0:T(128)S(1)} %pad_add_fusion.where_ref, s32[64]{0:T(128)S(1)} %bitcast.8, s32[64]{0:T(128)S(1)} %bitcast.9, s32[1]{0:T(128)} %bitcast.6.count, bf16[64,128,128]{2,1,0:T(8,128)(2,1)S(1)} %bitcast.7), custom_call_target="tpu_custom_call" | custom-call | tf_op jit(solution)/shard_map/pallas_call | solution.py:22
  12.2 1.9 %collective-permute-start.3 = (bf16[512,128]{1,0:T(8,128)(2,1)S(1)}, bf16[512,128]{1,0:T(8,128)(2,1)S(1)}, u32[]{:S(2)}, u32[]{:S(2)}) collective-permute-start(bf16[512,128]{1,0:T(8,128)(2,1)S(1)} %pad_maximum_fusion.1), channel_id=1, source_target_pairs={{0,4},{2,6},{4,0},{6,2},{8,12},{10,14},{12,8},{14,10},{16,20},{18,... | collective-permute-start | bytes 393224 | tf_op jit(solution)/shard_map/ppermute | solution.py:64
  14.2 3.1 %collective-permute-done.3 = bf16[512,128]{1,0:T(8,128)(2,1)S(1)} collective-permute-done((bf16[512,128]{1,0:T(8,128)(2,1)S(1)}, bf16[512,128]{1,0:T(8,128)(2,1)S(1)}, u32[]{:S(2)}, u32[]{:S(2)}) %collective-permute-start.3) | collective-permute-done | bytes 131104 | tf_op jit(solution)/shard_map/ppermute | solution.py:64
  17.4 1.9 %collective-permute-start.10 = (bf16[256,1024]{1,0:T(8,128)(2,1)S(1)}, bf16[256,1024]{1,0:T(8,128)(2,1)S(1)}, u32[]{:S(2)}, u32[]{:S(2)}) collective-permute-start(bf16[256,1024]{1,0:T(8,128)(2,1)S(1)} %get-tuple-element.57.refs_1_), channel_id=1, source_target_pairs={{0,4},{2,6},{4,0},{6,2},{8,12},{10,14},{12,8},{14,10},{16,20},{18,... | collective-permute-start | bytes 1572872 | tf_op jit(solution)/shard_map/ppermute | solution.py:64
  21.0 2.8 %collective-permute-done.5.refs_1_ = bf16[128,128]{1,0:T(8,128)(2,1)S(1)} collective-permute-done((bf16[128,128]{1,0:T(8,128)(2,1)S(1)}, bf16[128,128]{1,0:T(8,128)(2,1)S(1)}, u32[]{:S(2)}, u32[]{:S(2)}) %collective-permute-start.5) | collective-permute-done | bytes 32800 | tf_op jit(solution)/shard_map/ppermute | solution.py:66
  24.2 3.6 %collective-permute-start.7 = (bf16[128,128]{1,0:T(8,128)(2,1)S(1)}, bf16[128,128]{1,0:T(8,128)(2,1)S(1)}, u32[]{:S(2)}, u32[]{:S(2)}) collective-permute-start(bf16[128,128]{1,0:T(8,128)(2,1)S(1)} %shard_map.114.z0), channel_id=1, source_target_pairs={{0,16},{2,18},{4,20},{6,22},{8,24},{10,26},{12,28},{14,30},{16,0},... | collective-permute-start | bytes 98312 | tf_op jit(solution)/shard_map/ppermute | solution.py:64
  29.6 3.8 %collective-permute-done.8.z3 = bf16[128,128]{1,0:T(8,128)(2,1)S(1)} collective-permute-done((bf16[128,128]{1,0:T(8,128)(2,1)S(1)}, bf16[128,128]{1,0:T(8,128)(2,1)S(1)}, u32[]{:S(2)}, u32[]{:S(2)}) %collective-permute-start.8) | collective-permute-done | bytes 32800 | tf_op jit(solution)/shard_map/ppermute | solution.py:64
  33.5 1.3 %collective-permute-done.9.far = bf16[512,128]{1,0:T(8,128)(2,1)S(1)} collective-permute-done((bf16[512,128]{1,0:T(8,128)(2,1)S(1)}, bf16[512,128]{1,0:T(8,128)(2,1)S(1)}, u32[]{:S(2)}, u32[]{:S(2)}) %collective-permute-start.9) | collective-permute-done | bytes 131104 | tf_op jit(solution)/shard_map/ppermute | solution.py:64
  36.3 1.5 %collective-permute-start.12 = (bf16[128,128]{1,0:T(8,128)(2,1)S(1)}, bf16[128,128]{1,0:T(8,128)(2,1)S(1)}, u32[]{:S(2)}, u32[]{:S(2)}) collective-permute-start(bf16[128,128]{1,0:T(8,128)(2,1)S(1)} %get-tuple-element.60), channel_id=1, source_target_pairs={{0,4},{2,6},{4,0},{6,2},{8,12},{10,14},{12,8},{14,10},{16,20},{18,... | collective-permute-start | bytes 98312 | tf_op jit(solution)/shard_map/ppermute | solution.py:64
  40.2 2.4 %collective-permute-done.13.refs_3_ = bf16[128,128]{1,0:T(8,128)(2,1)S(1)} collective-permute-done((bf16[128,128]{1,0:T(8,128)(2,1)S(1)}, bf16[128,128]{1,0:T(8,128)(2,1)S(1)}, u32[]{:S(2)}, u32[]{:S(2)}) %collective-permute-start.13) | collective-permute-done | bytes 32800 | tf_op jit(solution)/shard_map/ppermute | solution.py:72
  42.8 1.4 %collective-permute-start.15 = (bf16[128,128]{1,0:T(8,128)(2,1)S(1)}, bf16[128,128]{1,0:T(8,128)(2,1)S(1)}, u32[]{:S(2)}, u32[]{:S(2)}) collective-permute-start(bf16[128,128]{1,0:T(8,128)(2,1)S(1)} %shard_map.116.z0), channel_id=1, source_target_pairs={{0,16},{2,18},{4,20},{6,22},{8,24},{10,26},{12,28},{14,30},{16,0},... | collective-permute-start | bytes 98312 | tf_op jit(solution)/shard_map/ppermute | solution.py:64
  44.2 3.0 %collective-permute-start.16 = (bf16[128,128]{1,0:T(8,128)(2,1)S(1)}, bf16[128,128]{1,0:T(8,128)(2,1)S(1)}, u32[]{:S(2)}, u32[]{:S(2)}) collective-permute-start(bf16[128,128]{1,0:T(8,128)(2,1)S(1)} %shard_map.116.z0), channel_id=1, source_target_pairs={{0,24},{2,26},{4,28},{6,30},{8,16},{10,18},{12,20},{14,22},{16,8},... | collective-permute-start | bytes 98312 | tf_op jit(solution)/shard_map/ppermute | solution.py:64
  47.7 2.2 %collective-permute-done.16.z3 = bf16[128,128]{1,0:T(8,128)(2,1)S(1)} collective-permute-done((bf16[128,128]{1,0:T(8,128)(2,1)S(1)}, bf16[128,128]{1,0:T(8,128)(2,1)S(1)}, u32[]{:S(2)}, u32[]{:S(2)}) %collective-permute-start.16) | collective-permute-done | bytes 32800 | tf_op jit(solution)/shard_map/ppermute | solution.py:64
  53.3 2.0 %collective-permute-start.20 = (bf16[128,128]{1,0:T(8,128)(2,1)S(1)}, bf16[128,128]{1,0:T(8,128)(2,1)S(1)}, u32[]{:S(2)}, u32[]{:S(2)}) collective-permute-start(bf16[128,128]{1,0:T(8,128)(2,1)S(1)} %get-tuple-element.65), channel_id=1, source_target_pairs={{0,5},{1,4},{2,7},{3,6},{4,1},{5,0},{6,3},{7,2},{8,13},{9,12},{10,... | collective-permute-start | bytes 98312 | tf_op jit(solution)/shard_map/ppermute | solution.py:72
  60.1 1.5 %collective-permute-start.22 = (bf16[128,128]{1,0:T(8,128)(2,1)S(1)}, bf16[128,128]{1,0:T(8,128)(2,1)S(1)}, u32[]{:S(2)}, u32[]{:S(2)}) collective-permute-start(bf16[128,128]{1,0:T(8,128)(2,1)S(1)} %get-tuple-element.67.refs_0_), channel_id=1, source_target_pairs={{0,4},{2,6},{4,0},{6,2},{8,12},{10,14},{12,8},{14,10},{16,20},{18,... | collective-permute-start | bytes 98312 | tf_op jit(solution)/shard_map/ppermute | solution.py:64
  64.0 2.4 %collective-permute-done.23.refs_3_ = bf16[128,128]{1,0:T(8,128)(2,1)S(1)} collective-permute-done((bf16[128,128]{1,0:T(8,128)(2,1)S(1)}, bf16[128,128]{1,0:T(8,128)(2,1)S(1)}, u32[]{:S(2)}, u32[]{:S(2)}) %collective-permute-start.23) | collective-permute-done | bytes 32800 | tf_op jit(solution)/shard_map/ppermute | solution.py:72
  66.8 1.3 %collective-permute-done.24.got = bf16[512,128]{1,0:T(8,128)(2,1)S(1)} collective-permute-done((bf16[512,128]{1,0:T(8,128)(2,1)S(1)}, bf16[512,128]{1,0:T(8,128)(2,1)S(1)}, u32[]{:S(2)}, u32[]{:S(2)}) %collective-permute-start.24) | collective-permute-done | bytes 131104 | tf_op jit(solution)/shard_map/ppermute | solution.py:64
  68.3 3.5 %collective-permute-start.26 = (bf16[128,128]{1,0:T(8,128)(2,1)S(1)}, bf16[128,128]{1,0:T(8,128)(2,1)S(1)}, u32[]{:S(2)}, u32[]{:S(2)}) collective-permute-start(bf16[128,128]{1,0:T(8,128)(2,1)S(1)} %get-tuple-element.73), channel_id=1, source_target_pairs={{0,16},{2,18},{4,20},{6,22},{8,24},{10,26},{12,28},{14,30},{16,0},... | collective-permute-start | bytes 98312 | tf_op jit(solution)/shard_map/ppermute | solution.py:64
  73.9 3.6 %collective-permute-done.27.refs_2_ = bf16[128,128]{1,0:T(8,128)(2,1)S(1)} collective-permute-done((bf16[128,128]{1,0:T(8,128)(2,1)S(1)}, bf16[128,128]{1,0:T(8,128)(2,1)S(1)}, u32[]{:S(2)}, u32[]{:S(2)}) %collective-permute-start.27) | collective-permute-done | bytes 32800 | tf_op jit(solution)/shard_map/ppermute | solution.py:64
  79.4 1.9 %collective-permute-start.30 = (bf16[128,128]{1,0:T(8,128)(2,1)S(1)}, bf16[128,128]{1,0:T(8,128)(2,1)S(1)}, u32[]{:S(2)}, u32[]{:S(2)}) collective-permute-start(bf16[128,128]{1,0:T(8,128)(2,1)S(1)} %shard_map.122.refs_0_), channel_id=1, source_target_pairs={{0,5},{1,4},{2,7},{3,6},{4,1},{5,0},{6,3},{7,2},{8,13},{9,12},{10,... | collective-permute-start | bytes 98312 | tf_op jit(solution)/shard_map/ppermute | solution.py:72
  82.6 1.6 %collective-permute-done.30.refs_3_ = bf16[128,128]{1,0:T(8,128)(2,1)S(1)} collective-permute-done((bf16[128,128]{1,0:T(8,128)(2,1)S(1)}, bf16[128,128]{1,0:T(8,128)(2,1)S(1)}, u32[]{:S(2)}, u32[]{:S(2)}) %collective-permute-start.30) | collective-permute-done | bytes 32800 | tf_op jit(solution)/shard_map/ppermute | solution.py:72
  87.4 3.1 %collective-permute-start.34 = (bf16[128,128]{1,0:T(8,128)(2,1)S(1)}, bf16[128,128]{1,0:T(8,128)(2,1)S(1)}, u32[]{:S(2)}, u32[]{:S(2)}) collective-permute-start(bf16[128,128]{1,0:T(8,128)(2,1)S(1)} %get-tuple-element.81), channel_id=1, source_target_pairs={{0,24},{2,26},{4,28},{6,30},{8,16},{10,18},{12,20},{14,22},{16,8},... | collective-permute-start | bytes 98312 | tf_op jit(solution)/shard_map/ppermute | solution.py:64
  91.1 2.0 %collective-permute-done.34.refs_2_ = bf16[128,128]{1,0:T(8,128)(2,1)S(1)} collective-permute-done((bf16[128,128]{1,0:T(8,128)(2,1)S(1)}, bf16[128,128]{1,0:T(8,128)(2,1)S(1)}, u32[]{:S(2)}, u32[]{:S(2)}) %collective-permute-start.34) | collective-permute-done | bytes 32800 | tf_op jit(solution)/shard_map/ppermute | solution.py:64
  94.7 1.5 %collective-permute-start.36 = (bf16[256,128]{1,0:T(8,128)(2,1)S(1)}, bf16[256,128]{1,0:T(8,128)(2,1)S(1)}, u32[]{:S(2)}, u32[]{:S(2)}) collective-permute-start(bf16[256,128]{1,0:T(8,128)(2,1)S(1)} %shard_map.125.refs_0_), channel_id=1, source_target_pairs={{0,4},{2,6},{4,0},{6,2},{8,12},{10,14},{12,8},{14,10},{16,20},{18,... | collective-permute-start | bytes 196616 | tf_op jit(solution)/shard_map/ppermute | solution.py:64
  99.1 2.2 %collective-permute-done.37.refs_3_ = bf16[256,128]{1,0:T(8,128)(2,1)S(1)} collective-permute-done((bf16[256,128]{1,0:T(8,128)(2,1)S(1)}, bf16[256,128]{1,0:T(8,128)(2,1)S(1)}, u32[]{:S(2)}, u32[]{:S(2)}) %collective-permute-start.37) | collective-permute-done | bytes 65568 | tf_op jit(solution)/shard_map/ppermute | solution.py:72
  101.8 1.4 %collective-permute-done.38.got = bf16[768,128]{1,0:T(8,128)(2,1)S(1)} collective-permute-done((bf16[768,128]{1,0:T(8,128)(2,1)S(1)}, bf16[768,128]{1,0:T(8,128)(2,1)S(1)}, u32[]{:S(2)}, u32[]{:S(2)}) %collective-permute-start.38) | collective-permute-done | bytes 196640 | tf_op jit(solution)/shard_map/ppermute | solution.py:64
  103.4 3.5 %collective-permute-start.40 = (bf16[256,128]{1,0:T(8,128)(2,1)S(1)}, bf16[256,128]{1,0:T(8,128)(2,1)S(1)}, u32[]{:S(2)}, u32[]{:S(2)}) collective-permute-start(bf16[256,128]{1,0:T(8,128)(2,1)S(1)} %get-tuple-element.88), channel_id=1, source_target_pairs={{0,16},{2,18},{4,20},{6,22},{8,24},{10,26},{12,28},{14,30},{16,0},... | collective-permute-start | bytes 196616 | tf_op jit(solution)/shard_map/ppermute | solution.py:64
  107.7 3.2 %collective-permute-done.40.refs_1_ = bf16[256,128]{1,0:T(8,128)(2,1)S(1)} collective-permute-done((bf16[256,128]{1,0:T(8,128)(2,1)S(1)}, bf16[256,128]{1,0:T(8,128)(2,1)S(1)}, u32[]{:S(2)}, u32[]{:S(2)}) %collective-permute-start.40) | collective-permute-done | bytes 65568 | tf_op jit(solution)/shard_map/ppermute | solution.py:64
  110.9 2.1 %collective-permute-done.41.refs_2_ = bf16[256,128]{1,0:T(8,128)(2,1)S(1)} collective-permute-done((bf16[256,128]{1,0:T(8,128)(2,1)S(1)}, bf16[256,128]{1,0:T(8,128)(2,1)S(1)}, u32[]{:S(2)}, u32[]{:S(2)}) %collective-permute-start.41) | collective-permute-done | bytes 65568 | tf_op jit(solution)/shard_map/ppermute | solution.py:64
  (92 shorter events, 37.3 us)
Async XLA Ops:
  0.6 11.3 %collective-permute-start = (bf16[128,128]{1,0:T(8,128)(2,1)}, bf16[128,128]{1,0:T(8,128)(2,1)S(1)}, u32[]{:S(2)}, u32[]{:S(2)}) collective-permute-start(bf16[128,128]{1,0:T(8,128)(2,1)} %refs_5_.3), channel_id=1, source_target_pairs={{0,8},{2,10},{4,12},{6,14},{8,0},{10,2},{12,4},{14,6},{16,24},{18,... | collective-permute-start | bytes 98312 | tf_op jit(solution)/shard_map/ppermute | solution.py:64
  3.7 8.2 %collective-permute-start.1 = (bf16[128,128]{1,0:T(8,128)(2,1)}, bf16[128,128]{1,0:T(8,128)(2,1)S(1)}, u32[]{:S(2)}, u32[]{:S(2)}) collective-permute-start(bf16[128,128]{1,0:T(8,128)(2,1)} %refs_5_.3), channel_id=1, source_target_pairs={{0,16},{2,18},{4,20},{6,22},{8,24},{10,26},{12,28},{14,30},{16,0},... | collective-permute-start | bytes 98312 | tf_op jit(solution)/shard_map/ppermute | solution.py:64
  6.3 5.9 %collective-permute-start.2 = (bf16[128,128]{1,0:T(8,128)(2,1)}, bf16[128,128]{1,0:T(8,128)(2,1)S(1)}, u32[]{:S(2)}, u32[]{:S(2)}) collective-permute-start(bf16[128,128]{1,0:T(8,128)(2,1)} %refs_5_.3), channel_id=1, source_target_pairs={{0,24},{2,26},{4,28},{6,30},{8,16},{10,18},{12,20},{14,22},{16,8},... | collective-permute-start | bytes 98312 | tf_op jit(solution)/shard_map/ppermute | solution.py:64
  12.2 5.0 %collective-permute-start.3 = (bf16[512,128]{1,0:T(8,128)(2,1)S(1)}, bf16[512,128]{1,0:T(8,128)(2,1)S(1)}, u32[]{:S(2)}, u32[]{:S(2)}) collective-permute-start(bf16[512,128]{1,0:T(8,128)(2,1)S(1)} %pad_maximum_fusion.1), channel_id=1, source_target_pairs={{0,4},{2,6},{4,0},{6,2},{8,12},{10,14},{12,8},{14,10},{16,20},{18,... | collective-permute-start | bytes 393224 | tf_op jit(solution)/shard_map/ppermute | solution.py:64
  17.4 17.5 %collective-permute-start.10 = (bf16[256,1024]{1,0:T(8,128)(2,1)S(1)}, bf16[256,1024]{1,0:T(8,128)(2,1)S(1)}, u32[]{:S(2)}, u32[]{:S(2)}) collective-permute-start(bf16[256,1024]{1,0:T(8,128)(2,1)S(1)} %get-tuple-element.57.refs_1_), channel_id=1, source_target_pairs={{0,4},{2,6},{4,0},{6,2},{8,12},{10,14},{12,8},{14,10},{16,20},{18,... | collective-permute-start | bytes 1572872 | tf_op jit(solution)/shard_map/ppermute | solution.py:64
  19.8 4.0 %collective-permute-start.5 = (bf16[128,128]{1,0:T(8,128)(2,1)S(1)}, bf16[128,128]{1,0:T(8,128)(2,1)S(1)}, u32[]{:S(2)}, u32[]{:S(2)}) collective-permute-start(bf16[128,128]{1,0:T(8,128)(2,1)S(1)} %get-tuple-element.56), channel_id=1, source_target_pairs={{0,1},{1,0},{2,3},{3,2},{4,5},{5,4},{6,7},{7,6},{8,9},{9,8},{10,11... | collective-permute-start | bytes 98312 | tf_op jit(solution)/shard_map/ppermute | solution.py:66
  23.9 4.5 %collective-permute-start.6 = (bf16[128,128]{1,0:T(8,128)(2,1)S(1)}, bf16[128,128]{1,0:T(8,128)(2,1)S(1)}, u32[]{:S(2)}, u32[]{:S(2)}) collective-permute-start(bf16[128,128]{1,0:T(8,128)(2,1)S(1)} %shard_map.114.z0), channel_id=1, source_target_pairs={{0,8},{2,10},{4,12},{6,14},{8,0},{10,2},{12,4},{14,6},{16,24},{18,... | collective-permute-start | bytes 98312 | tf_op jit(solution)/shard_map/ppermute | solution.py:64
  24.2 5.4 %collective-permute-start.7 = (bf16[128,128]{1,0:T(8,128)(2,1)S(1)}, bf16[128,128]{1,0:T(8,128)(2,1)S(1)}, u32[]{:S(2)}, u32[]{:S(2)}) collective-permute-start(bf16[128,128]{1,0:T(8,128)(2,1)S(1)} %shard_map.114.z0), channel_id=1, source_target_pairs={{0,16},{2,18},{4,20},{6,22},{8,24},{10,26},{12,28},{14,30},{16,0},... | collective-permute-start | bytes 98312 | tf_op jit(solution)/shard_map/ppermute | solution.py:64
  27.7 5.7 %collective-permute-start.8 = (bf16[128,128]{1,0:T(8,128)(2,1)S(1)}, bf16[128,128]{1,0:T(8,128)(2,1)S(1)}, u32[]{:S(2)}, u32[]{:S(2)}) collective-permute-start(bf16[128,128]{1,0:T(8,128)(2,1)S(1)} %shard_map.114.z0), channel_id=1, source_target_pairs={{0,24},{2,26},{4,28},{6,30},{8,16},{10,18},{12,20},{14,22},{16,8},... | collective-permute-start | bytes 98312 | tf_op jit(solution)/shard_map/ppermute | solution.py:64
  35.3 4.0 %collective-permute-start.11 = (bf16[128,128]{1,0:T(8,128)(2,1)S(1)}, bf16[128,128]{1,0:T(8,128)(2,1)S(1)}, u32[]{:S(2)}, u32[]{:S(2)}) collective-permute-start(bf16[128,128]{1,0:T(8,128)(2,1)S(1)} %get-tuple-element.59), channel_id=1, source_target_pairs={{0,1},{1,0},{2,3},{3,2},{4,5},{5,4},{6,7},{7,6},{8,9},{9,8},{10,11... | collective-permute-start | bytes 98312 | tf_op jit(solution)/shard_map/ppermute | solution.py:66
  37.8 4.8 %collective-permute-start.13 = (bf16[128,128]{1,0:T(8,128)(2,1)S(1)}, bf16[128,128]{1,0:T(8,128)(2,1)S(1)}, u32[]{:S(2)}, u32[]{:S(2)}) collective-permute-start(bf16[128,128]{1,0:T(8,128)(2,1)S(1)} %get-tuple-element.61), channel_id=1, source_target_pairs={{0,5},{1,4},{2,7},{3,6},{4,1},{5,0},{6,3},{7,2},{8,13},{9,12},{10,... | collective-permute-start | bytes 98312 | tf_op jit(solution)/shard_map/ppermute | solution.py:72
  42.8 4.5 %collective-permute-start.14 = (bf16[128,128]{1,0:T(8,128)(2,1)S(1)}, bf16[128,128]{1,0:T(8,128)(2,1)S(1)}, u32[]{:S(2)}, u32[]{:S(2)}) collective-permute-start(bf16[128,128]{1,0:T(8,128)(2,1)S(1)} %shard_map.116.z0), channel_id=1, source_target_pairs={{0,8},{2,10},{4,12},{6,14},{8,0},{10,2},{12,4},{14,6},{16,24},{18,... | collective-permute-start | bytes 98312 | tf_op jit(solution)/shard_map/ppermute | solution.py:64
  42.8 4.9 %collective-permute-start.15 = (bf16[128,128]{1,0:T(8,128)(2,1)S(1)}, bf16[128,128]{1,0:T(8,128)(2,1)S(1)}, u32[]{:S(2)}, u32[]{:S(2)}) collective-permute-start(bf16[128,128]{1,0:T(8,128)(2,1)S(1)} %shard_map.116.z0), channel_id=1, source_target_pairs={{0,16},{2,18},{4,20},{6,22},{8,24},{10,26},{12,28},{14,30},{16,0},... | collective-permute-start | bytes 98312 | tf_op jit(solution)/shard_map/ppermute | solution.py:64
  44.2 5.7 %collective-permute-start.16 = (bf16[128,128]{1,0:T(8,128)(2,1)S(1)}, bf16[128,128]{1,0:T(8,128)(2,1)S(1)}, u32[]{:S(2)}, u32[]{:S(2)}) collective-permute-start(bf16[128,128]{1,0:T(8,128)(2,1)S(1)} %shard_map.116.z0), channel_id=1, source_target_pairs={{0,24},{2,26},{4,28},{6,30},{8,16},{10,18},{12,20},{14,22},{16,8},... | collective-permute-start | bytes 98312 | tf_op jit(solution)/shard_map/ppermute | solution.py:64
  51.8 4.0 %collective-permute-start.18 = (bf16[128,128]{1,0:T(8,128)(2,1)S(1)}, bf16[128,128]{1,0:T(8,128)(2,1)S(1)}, u32[]{:S(2)}, u32[]{:S(2)}) collective-permute-start(bf16[128,128]{1,0:T(8,128)(2,1)S(1)} %get-tuple-element.63), channel_id=1, source_target_pairs={{0,1},{1,0},{2,3},{3,2},{4,5},{5,4},{6,7},{7,6},{8,9},{9,8},{10,11... | collective-permute-start | bytes 98312 | tf_op jit(solution)/shard_map/ppermute | solution.py:66
  52.8 4.3 %collective-permute-start.19 = (bf16[128,128]{1,0:T(8,128)(2,1)S(1)}, bf16[128,128]{1,0:T(8,128)(2,1)S(1)}, u32[]{:S(2)}, u32[]{:S(2)}) collective-permute-start(bf16[128,128]{1,0:T(8,128)(2,1)S(1)} %get-tuple-element.64), channel_id=1, source_target_pairs={{0,4},{2,6},{4,0},{6,2},{8,12},{10,14},{12,8},{14,10},{16,20},{18,... | collective-permute-start | bytes 98312 | tf_op jit(solution)/shard_map/ppermute | solution.py:64
  53.3 4.8 %collective-permute-start.20 = (bf16[128,128]{1,0:T(8,128)(2,1)S(1)}, bf16[128,128]{1,0:T(8,128)(2,1)S(1)}, u32[]{:S(2)}, u32[]{:S(2)}) collective-permute-start(bf16[128,128]{1,0:T(8,128)(2,1)S(1)} %get-tuple-element.65), channel_id=1, source_target_pairs={{0,5},{1,4},{2,7},{3,6},{4,1},{5,0},{6,3},{7,2},{8,13},{9,12},{10,... | collective-permute-start | bytes 98312 | tf_op jit(solution)/shard_map/ppermute | solution.py:72
  61.5 4.8 %collective-permute-start.23 = (bf16[128,128]{1,0:T(8,128)(2,1)S(1)}, bf16[128,128]{1,0:T(8,128)(2,1)S(1)}, u32[]{:S(2)}, u32[]{:S(2)}) collective-permute-start(bf16[128,128]{1,0:T(8,128)(2,1)S(1)} %get-tuple-element.67.refs_0_), channel_id=1, source_target_pairs={{0,5},{1,4},{2,7},{3,6},{4,1},{5,0},{6,3},{7,2},{8,13},{9,12},{10,... | collective-permute-start | bytes 98312 | tf_op jit(solution)/shard_map/ppermute | solution.py:72
  68.2 4.5 %collective-permute-start.25 = (bf16[128,128]{1,0:T(8,128)(2,1)S(1)}, bf16[128,128]{1,0:T(8,128)(2,1)S(1)}, u32[]{:S(2)}, u32[]{:S(2)}) collective-permute-start(bf16[128,128]{1,0:T(8,128)(2,1)S(1)} %get-tuple-element.72), channel_id=1, source_target_pairs={{0,8},{2,10},{4,12},{6,14},{8,0},{10,2},{12,4},{14,6},{16,24},{18,... | collective-permute-start | bytes 98312 | tf_op jit(solution)/shard_map/ppermute | solution.py:64
  68.3 5.6 %collective-permute-start.26 = (bf16[128,128]{1,0:T(8,128)(2,1)S(1)}, bf16[128,128]{1,0:T(8,128)(2,1)S(1)}, u32[]{:S(2)}, u32[]{:S(2)}) collective-permute-start(bf16[128,128]{1,0:T(8,128)(2,1)S(1)} %get-tuple-element.73), channel_id=1, source_target_pairs={{0,16},{2,18},{4,20},{6,22},{8,24},{10,26},{12,28},{14,30},{16,0},... | collective-permute-start | bytes 98312 | tf_op jit(solution)/shard_map/ppermute | solution.py:64
  71.8 5.7 %collective-permute-start.27 = (bf16[128,128]{1,0:T(8,128)(2,1)S(1)}, bf16[128,128]{1,0:T(8,128)(2,1)S(1)}, u32[]{:S(2)}, u32[]{:S(2)}) collective-permute-start(bf16[128,128]{1,0:T(8,128)(2,1)S(1)} %get-tuple-element.74), channel_id=1, source_target_pairs={{0,24},{2,26},{4,28},{6,30},{8,16},{10,18},{12,20},{14,22},{16,8},... | collective-permute-start | bytes 98312 | tf_op jit(solution)/shard_map/ppermute | solution.py:64
  77.7 4.0 %collective-permute-start.28 = (bf16[128,128]{1,0:T(8,128)(2,1)S(1)}, bf16[128,128]{1,0:T(8,128)(2,1)S(1)}, u32[]{:S(2)}, u32[]{:S(2)}) collective-permute-start(bf16[128,128]{1,0:T(8,128)(2,1)S(1)} %shard_map.122.refs_0_), channel_id=1, source_target_pairs={{0,1},{1,0},{2,3},{3,2},{4,5},{5,4},{6,7},{7,6},{8,9},{9,8},{10,11... | collective-permute-start | bytes 98312 | tf_op jit(solution)/shard_map/ppermute | solution.py:66
  79.4 4.8 %collective-permute-start.30 = (bf16[128,128]{1,0:T(8,128)(2,1)S(1)}, bf16[128,128]{1,0:T(8,128)(2,1)S(1)}, u32[]{:S(2)}, u32[]{:S(2)}) collective-permute-start(bf16[128,128]{1,0:T(8,128)(2,1)S(1)} %shard_map.122.refs_0_), channel_id=1, source_target_pairs={{0,5},{1,4},{2,7},{3,6},{4,1},{5,0},{6,3},{7,2},{8,13},{9,12},{10,... | collective-permute-start | bytes 98312 | tf_op jit(solution)/shard_map/ppermute | solution.py:72
  86.1 4.5 %collective-permute-start.32 = (bf16[128,128]{1,0:T(8,128)(2,1)S(1)}, bf16[128,128]{1,0:T(8,128)(2,1)S(1)}, u32[]{:S(2)}, u32[]{:S(2)}) collective-permute-start(bf16[128,128]{1,0:T(8,128)(2,1)S(1)} %get-tuple-element.79), channel_id=1, source_target_pairs={{0,8},{2,10},{4,12},{6,14},{8,0},{10,2},{12,4},{14,6},{16,24},{18,... | collective-permute-start | bytes 98312 | tf_op jit(solution)/shard_map/ppermute | solution.py:64
  86.2 4.9 %collective-permute-start.33 = (bf16[128,128]{1,0:T(8,128)(2,1)S(1)}, bf16[128,128]{1,0:T(8,128)(2,1)S(1)}, u32[]{:S(2)}, u32[]{:S(2)}) collective-permute-start(bf16[128,128]{1,0:T(8,128)(2,1)S(1)} %get-tuple-element.80), channel_id=1, source_target_pairs={{0,16},{2,18},{4,20},{6,22},{8,24},{10,26},{12,28},{14,30},{16,0},... | collective-permute-start | bytes 98312 | tf_op jit(solution)/shard_map/ppermute | solution.py:64
  87.4 5.7 %collective-permute-start.34 = (bf16[128,128]{1,0:T(8,128)(2,1)S(1)}, bf16[128,128]{1,0:T(8,128)(2,1)S(1)}, u32[]{:S(2)}, u32[]{:S(2)}) collective-permute-start(bf16[128,128]{1,0:T(8,128)(2,1)S(1)} %get-tuple-element.81), channel_id=1, source_target_pairs={{0,24},{2,26},{4,28},{6,30},{8,16},{10,18},{12,20},{14,22},{16,8},... | collective-permute-start | bytes 98312 | tf_op jit(solution)/shard_map/ppermute | solution.py:64
  93.5 4.6 %collective-permute-start.35 = (bf16[256,128]{1,0:T(8,128)(2,1)S(1)}, bf16[256,128]{1,0:T(8,128)(2,1)S(1)}, u32[]{:S(2)}, u32[]{:S(2)}) collective-permute-start(bf16[256,128]{1,0:T(8,128)(2,1)S(1)} %shard_map.125.refs_0_), channel_id=1, source_target_pairs={{0,1},{1,0},{2,3},{3,2},{4,5},{5,4},{6,7},{7,6},{8,9},{9,8},{10,11... | collective-permute-start | bytes 196616 | tf_op jit(solution)/shard_map/ppermute | solution.py:66
  94.7 4.4 %collective-permute-start.36 = (bf16[256,128]{1,0:T(8,128)(2,1)S(1)}, bf16[256,128]{1,0:T(8,128)(2,1)S(1)}, u32[]{:S(2)}, u32[]{:S(2)}) collective-permute-start(bf16[256,128]{1,0:T(8,128)(2,1)S(1)} %shard_map.125.refs_0_), channel_id=1, source_target_pairs={{0,4},{2,6},{4,0},{6,2},{8,12},{10,14},{12,8},{14,10},{16,20},{18,... | collective-permute-start | bytes 196616 | tf_op jit(solution)/shard_map/ppermute | solution.py:64
  96.1 5.2 %collective-permute-start.37 = (bf16[256,128]{1,0:T(8,128)(2,1)S(1)}, bf16[256,128]{1,0:T(8,128)(2,1)S(1)}, u32[]{:S(2)}, u32[]{:S(2)}) collective-permute-start(bf16[256,128]{1,0:T(8,128)(2,1)S(1)} %shard_map.125.refs_0_), channel_id=1, source_target_pairs={{0,5},{1,4},{2,7},{3,6},{4,1},{5,0},{6,3},{7,2},{8,13},{9,12},{10,... | collective-permute-start | bytes 196616 | tf_op jit(solution)/shard_map/ppermute | solution.py:72
  103.3 4.5 %collective-permute-start.39 = (bf16[256,128]{1,0:T(8,128)(2,1)S(1)}, bf16[256,128]{1,0:T(8,128)(2,1)S(1)}, u32[]{:S(2)}, u32[]{:S(2)}) collective-permute-start(bf16[256,128]{1,0:T(8,128)(2,1)S(1)} %get-tuple-element.87), channel_id=1, source_target_pairs={{0,8},{2,10},{4,12},{6,14},{8,0},{10,2},{12,4},{14,6},{16,24},{18,... | collective-permute-start | bytes 196616 | tf_op jit(solution)/shard_map/ppermute | solution.py:64
  103.4 7.6 %collective-permute-start.40 = (bf16[256,128]{1,0:T(8,128)(2,1)S(1)}, bf16[256,128]{1,0:T(8,128)(2,1)S(1)}, u32[]{:S(2)}, u32[]{:S(2)}) collective-permute-start(bf16[256,128]{1,0:T(8,128)(2,1)S(1)} %get-tuple-element.88), channel_id=1, source_target_pairs={{0,16},{2,18},{4,20},{6,22},{8,24},{10,26},{12,28},{14,30},{16,0},... | collective-permute-start | bytes 196616 | tf_op jit(solution)/shard_map/ppermute | solution.py:64
  106.9 6.2 %collective-permute-start.41 = (bf16[256,128]{1,0:T(8,128)(2,1)S(1)}, bf16[256,128]{1,0:T(8,128)(2,1)S(1)}, u32[]{:S(2)}, u32[]{:S(2)}) collective-permute-start(bf16[256,128]{1,0:T(8,128)(2,1)S(1)} %get-tuple-element.89), channel_id=1, source_target_pairs={{0,24},{2,26},{4,28},{6,30},{8,16},{10,18},{12,20},{14,22},{16,8},... | collective-permute-start | bytes 196616 | tf_op jit(solution)/shard_map/ppermute | solution.py:64
  (18 other events, 126.0 us)

commit v3 on v2

--- a/solution.py
+++ b/solution.py
@@ -14,10 +14,8 @@
 VMEM_LIMIT = 48 * 2**20
 
 
-def vmem_call(body, outs, *args, smem=0, scratch=()):
-    specs = [
-        pl.BlockSpec(memory_space=pltpu.SMEM if i < smem else pltpu.VMEM) for i in range(len(args))
-    ]
+def vmem_call(body, outs, *args, spaces=None, scratch=()):
+    specs = [pl.BlockSpec(memory_space=space) for space in spaces or [pltpu.VMEM] * len(args)]
     out_specs = [pl.BlockSpec(memory_space=pltpu.VMEM) for _ in outs]
     return pl.pallas_call(
         body,
@@ -77,18 +75,41 @@
     def to_square(values):
         return [exchange(v, 2 * y, x) for (y, x), v in zip(square[1:], values)]
 
-    def build(where_ref, rows, cols, count, tiles, *refs):
-        parts, turned, acc = refs[:n_y], refs[n_y], refs[n_y + 1]
+    chunk = min(16, slots)
+    n_chunks = slots // chunk
+    assert slots % chunk == 0
+
+    def build(where_ref, count, rows_hbm, cols_hbm, tiles_hbm, inject, cotan, mask, *refs):
+        parts, turned, fixed_out = refs[:n_y], refs[n_y], refs[n_y + 1]
+        rows, cols, tiles, acc, index_sem, tile_sem = refs[n_y + 2 :]
+        copies = [
+            pltpu.make_async_copy(rows_hbm, rows, index_sem.at[0]),
+            pltpu.make_async_copy(cols_hbm, cols, index_sem.at[1]),
+        ]
+        pieces = [slice(c * chunk, (c + 1) * chunk) for c in range(n_chunks)]
+        loads = [
+            pltpu.make_async_copy(tiles_hbm.at[0, 0, piece], tiles.at[piece], tile_sem.at[c])
+            for c, piece in enumerate(pieces)
+        ]
+        for copy in copies + loads:
+            copy.start()
         acc[...] = jnp.zeros_like(acc)
+        fixed_out[:TILE] = inject[...]
+        kept_nodes = jnp.broadcast_to(mask[...].astype(F32), (TILE, TILE)).T[:, :1]
+        fixed_out[TILE:] = (cotan[...].astype(F32) * kept_nodes).astype(BF16)
+        for copy in copies:
+            copy.wait()
 
         def add(k, carry):
-            s = cols[k] ^ where_ref[0]
-            x = rows[k] ^ where_ref[1]
+            s = cols[0, 0, k] ^ where_ref[0]
+            x = rows[0, 0, k] ^ where_ref[1]
             y = (s // 2) % n_y
             acc[((y * n_col + x) * 2 + s % 2) * LINE + s // z_step] += tiles[k].astype(F32)
             return carry
 
-        lax.fori_loop(0, count[0], add, 0)
+        for c, load in enumerate(loads):
+            load.wait()
+            lax.fori_loop(c * chunk, jnp.clip(count[0, 0], c * chunk, (c + 1) * chunk), add, 0)
         for y in range(n_y):
             for x in range(n_col):
                 for p in range(2 * LINE):
@@ -97,20 +118,34 @@
                     parts[y][here, there] = tile.astype(BF16)
                     if y == 0:
                         turned[there, here] = tile.T.astype(BF16)
-
+            if y > 0:
+                parts[y][: 2 * TILE, 2 * line_rows :] = fixed_out[...]
+                if n_col > 2:
+                    parts[y][2 * TILE :, 2 * line_rows :] = jnp.zeros(((n_col - 2) * TILE, hidden), BF16)
+
+    assert n_col >= 2
     part_shape = (n_col * TILE, 2 * line_rows)
-    *parts, turned = vmem_call(
+    sent_shape = (n_col * TILE, 2 * line_rows + hidden)
+    *parts, turned, fixed = vmem_call(
         build,
-        [(part_shape, BF16)] * n_y + [(part_shape[::-1], BF16)],
+        [(part_shape, BF16)] + [(sent_shape, BF16)] * (n_y - 1)
+        + [(part_shape[::-1], BF16), ((2 * TILE, hidden), BF16)],
         where,
-        tile_rows.reshape(-1),
-        tile_cols.reshape(-1),
-        tile_counts.reshape(-1),
-        tile_values.reshape(slots, TILE, TILE),
-        smem=4,
-        scratch=[pltpu.VMEM((n_y * n_col * 2 * LINE, TILE, TILE), F32)],
+        tile_counts,
+        *[pltpu.with_memory_space_constraint(v, pltpu.HBM) for v in (tile_rows, tile_cols, tile_values)],
+        injection,
+        cotangent,
+        node_mask.reshape(1, -1),
+        spaces=[pltpu.SMEM] * 2 + [pltpu.HBM] * 3 + [pltpu.VMEM] * 3,
+        scratch=[
+            pltpu.SMEM(tile_rows.shape, jnp.int32),
+            pltpu.SMEM(tile_cols.shape, jnp.int32),
+            pltpu.VMEM((slots, TILE, TILE), BF16),
+            pltpu.VMEM((n_y * n_col * 2 * LINE, TILE, TILE), F32),
+            pltpu.SemaphoreType.DMA((2,)),
+            pltpu.SemaphoreType.DMA((n_chunks,)),
+        ],
     )
-    masked_grad = cotangent.astype(F32) * node_mask.astype(F32)[:, None]
 
     def first_partial(near, far, *refs):
         a, outs = refs[:n_y], refs[n_y:]
@@ -118,40 +153,96 @@
         for y in range(n_y):
             rows = slice(y * line_rows, (y + 1) * line_rows)
             total += jnp.dot(a[y][:, :line_rows], near[rows], preferred_element_type=F32)
-            total += jnp.dot(a[y][:, line_rows:], far[rows], preferred_element_type=F32)
+            total += jnp.dot(a[y][:, line_rows : 2 * line_rows], far[rows], preferred_element_type=F32)
         outs[0][...] = total[:TILE]
         for x in range(1, n_col):
             outs[x][...] = total[x * TILE : (x + 1) * TILE].astype(BF16)
 
-    def forward_partial(z0, z1, z2, z3, far, *refs):
+    n_square = len(square)
+    square_rows = n_square * TILE
+
+    def forward_near(z0, z1, z2, z3, *refs):
+        a, out = refs[:n_y], refs[n_y]
+        near = jnp.concatenate([z0[...], z1[...], z2[...], z3[...]], axis=0)
+        rows = n_col * TILE
+        for y in range(n_y):
+            out[y * rows : (y + 1) * rows] = jnp.dot(a[y][:, :line_rows], near, preferred_element_type=F32)
+
+    def far_product(held, far, a, y):
+        rows = slice(y * n_col * TILE, (y + 1) * n_col * TILE)
+        return held[rows] + jnp.dot(a[y][:, line_rows : 2 * line_rows], far[...], preferred_element_type=F32)
+
+    def forward_far(held, far, *refs):
         a, outs = refs[:n_y], refs[n_y:]
-        near = jnp.concatenate([z0[...], z1[...], z2[...], z3[...]], axis=0)
-        for y in range(n_y):
-            total = jnp.dot(a[y][:, :line_rows], near, preferred_element_type=F32)
-            total += jnp.dot(a[y][:, line_rows:], far[...], preferred_element_type=F32)
+        for y in range(n_y):
+            total = far_product(held, far, a, y)
             for x in range(n_col):
                 out = outs[y * n_col + x]
                 out[...] = total[x * TILE : (x + 1) * TILE].astype(out.dtype)
 
-    def advance(beta, last, peers):
+    def forward_far_all(held, far, *refs):
+        a, (kept, sent) = refs[:n_y], refs[n_y:]
+        for y in range(n_y):
+            rows = slice(y * n_col * TILE, (y + 1) * n_col * TILE)
+            total = far_product(held, far, a, y)
+            kept[rows] = total
+            sent[rows] = total.astype(BF16)
+
+    def advance(beta, peers):
         def body(*refs):
-            sums, (w, anchor_ref, inject), rest = refs[:peers], refs[peers : peers + 3], refs[peers + 3 :]
+            sums, (w, anchor_ref, inject, out) = refs[:peers], refs[peers:]
             u = tree_sum([s[...].astype(F32) for s in sums])
-            pre = split_dot(u, w[...], ((1,), (0,))) + inject[...].astype(F32)
-            bent = jnp.tanh(pre)
-            outs = rest[1:] if last else rest
-            outs[0][...] = (beta * anchor_ref[...].astype(F32) + (1.0 - beta) * bent).astype(BF16)
-            if last:
-                slope = 1.0 - bent * bent
-                outs[1][...] = slope
-                outs[2][...] = u
-                outs[3][...] = (rest[0][...] * slope).astype(BF16)
+            bent = jnp.tanh(split_dot(u, w[...], ((1,), (0,))) + inject[...].astype(F32))
+            out[...] = (beta * anchor_ref[...].astype(F32) + (1.0 - beta) * bent).astype(BF16)
 
         return body
+
+    def meet(kept, *refs):
+        got, refs = refs[: n_square - 1], refs[n_square - 1 :]
+        fixed_refs, (w, bent_out, slope_out, u_out, h_out) = refs[:n_col], refs[n_col:]
+        fixed = [fixed_refs[x].at[2 * y * TILE : 2 * (y + 1) * TILE] for y, x in square]
+        u = jnp.concatenate(
+            [
+                tree_sum(
+                    [kept[j * TILE : (j + 1) * TILE]]
+                    + [
+                        got[i - 1][(i ^ j) * TILE : ((i ^ j) + 1) * TILE].astype(F32)
+                        for i in range(1, n_square)
+                    ]
+                )
+                for j in range(n_square)
+            ],
+            axis=0,
+        )
+        inject = jnp.concatenate([f[:TILE] for f in fixed], axis=0).astype(F32)
+        bent = jnp.tanh(split_dot(u, w[...], ((1,), (0,))) + inject)
+        slope = 1.0 - bent * bent
+        base = jnp.concatenate([f[TILE:] for f in fixed], axis=0).astype(F32)
+        h_out[...] = (base * slope).astype(BF16)
+        bent_out[...] = bent[:TILE]
+        slope_out[...] = slope[:TILE]
+        u_out[...] = u[:TILE]
+
+    def turn(fixed_ref, *refs):
+        came, outs, fixed_out = refs[: n_y - 1], refs[n_y - 1 : -1], refs[-1]
+        fixed_out[: 2 * TILE] = fixed_ref[...]
+        for y in range(1, n_y):
+            part, out = came[y - 1], outs[y - 1]
+            fixed_out[2 * y * TILE : 2 * (y + 1) * TILE] = part[: 2 * TILE, 2 * line_rows :]
+            for x in range(n_col):
+                for p in range(2 * LINE):
+                    here, there = slice(x * TILE, (x + 1) * TILE), slice(p * TILE, (p + 1) * TILE)
+                    out[there, here] = part[here, there].T
 
     state = anchor
     for step in range(ITERS):
+        beta = 1.0 / (step + 2.0)
+        if step == 2:
+            state, fixed_y = lax.optimization_barrier((state, fixed_y))
         line = [state] + along_line([state] * (LINE - 1))
+        if step == 2:
+            fixed = [fixed_y] + [exchange(fixed_y, 0, x) for x in range(1, n_col)]
+            line, fixed = lax.optimization_barrier((line, fixed))
         if step == 0:
             joined = jnp.concatenate(line, axis=0)
             joined, *parts, turned = lax.optimization_barrier((joined, *parts, turned))
@@ -159,7 +250,7 @@
             while bit < z_step:
                 joined = jnp.concatenate([joined, exchange(joined, bit)], axis=0)
                 bit *= 2
-            joined, *sent = lax.optimization_barrier((joined, *parts[1:]))
+            joined, sent = lax.optimization_barrier((joined, parts[1:]))
             far = exchange(joined, 1)
             outs = [(block, F32)] + [(block, BF16)] * (n_col - 1)
             mine, *sends = vmem_call(first_partial, outs, joined, far, *parts)
@@ -167,43 +258,56 @@
             got = [exchange(v, 0, x + 1) for x, v in enumerate(sends)]
         else:
             far = exchange(jnp.concatenate(line, axis=0), 1)
-            outs = [(block, F32)] + [(block, BF16)] * (len(square) - 1)
-            mine, *sends = vmem_call(forward_partial, outs, *line, far, *parts)
+            (held,) = vmem_call(forward_near, [((square_rows, hidden), F32)], *line, *parts)
+            if step == ITERS - 1:
+                outs = [((square_rows, hidden), F32), ((square_rows, hidden), BF16)]
+                kept, sent = vmem_call(forward_far_all, outs, held, far, *parts)
+                got = to_square([sent] * (n_square - 1))
+                bent, slope, mixed, h_all = vmem_call(
+                    meet, [(block, F32)] * 3 + [((square_rows, hidden), BF16)], kept, *got, *fixed, weight
+                )
+                break
+            outs = [(block, F32)] + [(block, BF16)] * (n_square - 1)
+            mine, *sends = vmem_call(forward_far, outs, held, far, *parts)
             got = to_square(sends)
-        last = step == ITERS - 1
-        results = [(block, BF16)] + ([(block, F32), (block, F32), (block, BF16)] if last else [])
-        state, *rest = vmem_call(
-            advance(1.0 / (step + 2.0), last, 1 + len(got)),
-            results,
-            mine,
-            *got,
-            weight,
-            anchor,
-            injection,
-            *([masked_grad] if last else []),
+        if step == 1:
+            *more, fixed_y = vmem_call(
+                turn,
+                [(part_shape[::-1], BF16)] * (n_y - 1) + [((2 * n_y * TILE, hidden), BF16)],
+                fixed,
+                *parts[1:],
+            )
+            turned = [turned] + more
+        (state,) = vmem_call(
+            advance(beta, 1 + len(got)), [(block, BF16)], mine, *got, weight, anchor, injection
         )
-    slope, mixed, scaled = rest
-
-    def turn(*refs):
-        for part, out in zip(refs[: n_y - 1], refs[n_y - 1 :]):
-            for x in range(n_col):
-                for p in range(2 * LINE):
-                    here, there = slice(x * TILE, (x + 1) * TILE), slice(p * TILE, (p + 1) * TILE)
-                    out[there, here] = part[here, there].T
-
-    turned = [turned] + list(vmem_call(turn, [(part_shape[::-1], BF16)] * (n_y - 1), *parts[1:]))
-
-    def backward_partial(last):
+
+    def finish(bent_ref, anchor_ref, out):
+        out[...] = (beta * anchor_ref[...].astype(F32) + (1.0 - beta) * bent_ref[...]).astype(BF16)
+
+    (state,) = vmem_call(finish, [(block, BF16)], bent, anchor)
+
+    def line_product(h, a_t, rows):
+        total = None
+        for y in range(n_y):
+            if len(h) == 1:
+                joined = h[0][y * n_col * TILE : (y + 1) * n_col * TILE]
+            else:
+                joined = jnp.concatenate([h[y * n_col + x][:TILE] for x in range(n_col)], axis=0)
+            product = jnp.dot(a_t[y][rows], joined, preferred_element_type=F32)
+            total = product if total is None else total + product
+        return total
+
+    def backward_near(n):
         def body(*refs):
-            n = len(square)
-            h, a_t, (near, far, *term) = refs[:n], refs[n : n + n_y], refs[n + n_y :]
-            total = None
-            for y in range(n_y):
-                joined = jnp.concatenate([h[y * n_col + x][:TILE] for x in range(n_col)], axis=0)
-                product = jnp.dot(a_t[y][...], joined, preferred_element_type=F32)
-                total = product if total is None else total + product
-            near[...] = total[:line_rows]
-            far[:line_rows] = total[line_rows:].astype(BF16)
+            refs[-1][...] = line_product(refs[:n], refs[n:-1], slice(0, line_rows))
+
+        return body
+
+    def backward_far(n, last):
+        def body(*refs):
+            h, a_t, (far, *term) = refs[:n], refs[n : n + n_y], refs[n + n_y :]
+            far[:line_rows] = line_product(h, a_t, slice(line_rows, 2 * line_rows)).astype(BF16)
             if last:
                 whole = tree_sum([v[TILE:].astype(F32) for v in h])
                 high, low = halves(whole)
@@ -237,7 +341,7 @@
             got, rest = refs[: LINE - 1], refs[LINE - 1 :]
             v = tree_sum([held[...]] + [r[:TILE].astype(F32) for r in got])
             base, w, slope_ref = rest[:3]
-            g = base[...] + split_dot(v, w[...], ((1,), (1,)))
+            g = base[TILE : 2 * TILE].astype(F32) + split_dot(v, w[...], ((1,), (1,)))
             if last:
                 term, adjoint_out, grad_out = rest[3:]
                 adjoint_out[...] = g
@@ -254,14 +358,16 @@
 
     for step in range(ADJOINT):
         last, ride = step == ADJOINT - 1, step == ADJOINT - 2
-        states = [scaled] + to_square([scaled] * (len(square) - 1))
+        states = [h_all] if step == 0 else [scaled] + to_square([scaled] * (n_square - 1))
         extra = 2 * hidden if last else 0
-        near, far, *term = vmem_call(
-            backward_partial(last),
-            [((line_rows, hidden), F32), ((line_rows + extra, hidden), BF16)]
-            + ([((hidden, hidden), F32)] if last else []),
+        far, *term = vmem_call(
+            backward_far(len(states), last),
+            [((line_rows + extra, hidden), BF16)] + ([((hidden, hidden), F32)] if last else []),
             *states,
             *turned,
+        )
+        (near,) = vmem_call(
+            backward_near(len(states)), [((line_rows, hidden), F32)], *states, *turned
         )
         got = exchange(far, 1)
         extra = hidden if last else 0
@@ -277,7 +383,7 @@
         if last:
             *sends, total = sends
         got = along_line(sends)
-        inputs = (held, *got, masked_grad, weight, slope)
+        inputs = (held, *got, fixed[0], weight, slope)
         if last:
             adjoint, weight_grad = vmem_call(
                 pull(True, False), [(block, F32), ((hidden, hidden), F32)], *inputs, total

time: 114 us -> 107 us (0.939)
  waiting for transfers between devices: 50.8 us -> 45.6 us
  starting transfers between devices: 51.1 us -> 48.3 us
  Pallas kernels: 7.25 us -> 9.19 us
    ppermute x31 -> x30, starting transfers between devices: 37.9 us -> 34.4 us  [exchange(): return lax.ppermute(value, 'row', [(i, i ^ row_xor) for i in range(n_row)])]
    ppermute x31 -> x30, waiting for transfers between devices: 35.9 us -> 32.7 us  [exchange(): return lax.ppermute(value, 'row', [(i, i ^ row_xor) for i in range(n_row)])]
    pallas_call x17 -> x23, Pallas kernels: 7.25 us -> 9.19 us  [vmem_call(): pl.pallas_call(body, out_shape=[jax.ShapeDtypeStruct(shape, dtype) for sh...]
    ppermute x5 -> x4, waiting for transfers between devices: 9.62 us -> 7.9 us  [exchange(): return lax.ppermute(value, ('row', 'col'), pairs)]
    ppermute x5 -> x4, starting transfers between devices: 6.74 us -> 7.64 us  [exchange(): return lax.ppermute(value, ('row', 'col'), pairs)]
    unnamed x16 -> x12, local copies, waits for them, and re-layouts: 2.92 us -> 2.18 us
  transfers between devices with their start and end apart: 42 -> 40, of which waited for: 33 -> 32; matrix products, arithmetic and copies ran while one was open for 0% -> 0% of each run, Pallas kernels for 2% -> 6%
where the time goes in v3:
time: 107 us
  starting transfers between devices  48.3 us (45%)
  waiting for transfers between devices  45.6 us (43%)
  Pallas kernels  9.19 us (9%)
  local copies, waits for them, and re-layouts  2.18 us (2%)
  between operations  1.57 us (1%)
    ppermute x30, starting transfers between devices, exchange(): return lax.ppermute(value, 'row', [(i, i ^ row_xor) for i in range(n_row)])  34.4 us
    ppermute x30, waiting for transfers between devices, exchange(): return lax.ppermute(value, 'row', [(i, i ^ row_xor) for i in range(n_row)])  32.7 us
    pallas_call x23, Pallas kernels, vmem_call(): pl.pallas_call(body, out_shape=[jax.ShapeDtypeStruct(shape, dtype) for sh...  9.19 us
    ppermute x4, waiting for transfers between devices, exchange(): return lax.ppermute(value, ('row', 'col'), pairs)  7.9 us
    ppermute x4, starting transfers between devices, exchange(): return lax.ppermute(value, ('row', 'col'), pairs)  7.64 us
    ppermute x6, starting transfers between devices, exchange(): return lax.ppermute(value, 'col', [(i, i ^ col_xor) for i in range(n_col)])  6.32 us
    ppermute x6, waiting for transfers between devices, exchange(): return lax.ppermute(value, 'col', [(i, i ^ col_xor) for i in range(n_col)])  5.02 us
    unnamed x12, local copies, waits for them, and re-layouts  2.18 us
  transfers between devices with their start and end apart: 40, of which 32 were waited for; matrix products, arithmetic and copies ran while one was open for 0% of the time, Pallas kernels for 6%

profile of v3, /device:TPU:0, one launch (start us, length us, event | category | flops | bytes accessed | tf_op | source)
XLA Modules:
  0.0 107.0 jit_solution(13935230000043573231)
XLA Ops:
  0.6 5.1 %collective-permute-start.2 = (bf16[128,128]{1,0:T(8,128)(2,1)}, bf16[128,128]{1,0:T(8,128)(2,1)S(1)}, u32[]{:S(2)}, u32[]{:S(2)}) collective-permute-start(bf16[128,128]{1,0:T(8,128)(2,1)} %anchor_ref.1), channel_id=1, source_target_pairs={{0,24},{2,26},{4,28},{6,30},{8,16},{10,18},{12,20},{14,22},{16,8},... | collective-permute-start | bytes 98312 | tf_op jit(solution)/shard_map/ppermute | solution.py:62
  9.3 3.1 %shard_map.112 = (bf16[256,1024]{1,0:T(8,128)(2,1)S(1)}, bf16[256,1152]{1,0:T(8,128)(2,1)S(1)}, bf16[1024,256]{1,0:T(8,128)(2,1)S(1)}, bf16[256,128]{1,0:T(8,128)(2,1)S(1)}) custom-call(s32[2]{0:T(128)S(1)} %pad_add_fusion.where_ref, s32[1,1]{1,0:T(1,128)S(6)} %copy.12.count, s32[1,1,64]{2,1,0:T(1,128)} %rows_hbm.1, s32[1,1,64]{2,1,0:T(1,128)} %cols_hbm.1, ...), custom_call_target="tpu_custom_call" | custom-call | tf_op jit(solution)/shard_map/pallas_call | solution.py:20
  12.5 1.4 %collective-permute-start.3 = (bf16[512,128]{1,0:T(8,128)(2,1)S(1)}, bf16[512,128]{1,0:T(8,128)(2,1)S(1)}, u32[]{:S(2)}, u32[]{:S(2)}) collective-permute-start(bf16[512,128]{1,0:T(8,128)(2,1)S(1)} %pad_maximum_fusion.1), channel_id=1, source_target_pairs={{0,4},{2,6},{4,0},{6,2},{8,12},{10,14},{12,8},{14,10},{16,20},{18,... | collective-permute-start | bytes 393224 | tf_op jit(solution)/shard_map/ppermute | solution.py:62
  13.9 3.6 %collective-permute-done.3 = bf16[512,128]{1,0:T(8,128)(2,1)S(1)} collective-permute-done((bf16[512,128]{1,0:T(8,128)(2,1)S(1)}, bf16[512,128]{1,0:T(8,128)(2,1)S(1)}, u32[]{:S(2)}, u32[]{:S(2)}) %collective-permute-start.3) | collective-permute-done | bytes 131104 | tf_op jit(solution)/shard_map/ppermute | solution.py:62
  17.5 1.4 %collective-permute-start.9 = (bf16[256,1152]{1,0:T(8,128)(2,1)S(1)}, bf16[256,1152]{1,0:T(8,128)(2,1)S(1)}, u32[]{:S(2)}, u32[]{:S(2)}) collective-permute-start(bf16[256,1152]{1,0:T(8,128)(2,1)S(1)} %get-tuple-element.61.refs_1_), channel_id=1, source_target_pairs={{0,4},{2,6},{4,0},{6,2},{8,12},{10,14},{12,8},{14,10},{16,20},{18,... | collective-permute-start | bytes 1769480 | tf_op jit(solution)/shard_map/ppermute | solution.py:62
  18.9 1.5 %collective-permute-done.4.far = bf16[1024,128]{1,0:T(8,128)(2,1)S(1)} collective-permute-done((bf16[1024,128]{1,0:T(8,128)(2,1)S(1)}, bf16[1024,128]{1,0:T(8,128)(2,1)S(1)}, u32[]{:S(2)}, u32[]{:S(2)}) %collective-permute-start.4) | collective-permute-done | bytes 262176 | tf_op jit(solution)/shard_map/ppermute | solution.py:62
  20.9 1.6 %collective-permute-start.5 = (bf16[128,128]{1,0:T(8,128)(2,1)S(1)}, bf16[128,128]{1,0:T(8,128)(2,1)S(1)}, u32[]{:S(2)}, u32[]{:S(2)}) collective-permute-start(bf16[128,128]{1,0:T(8,128)(2,1)S(1)} %get-tuple-element.60), channel_id=1, source_target_pairs={{0,1},{1,0},{2,3},{3,2},{4,5},{5,4},{6,7},{7,6},{8,9},{9,8},{10,11... | collective-permute-start | bytes 98312 | tf_op jit(solution)/shard_map/ppermute | solution.py:64
  22.4 2.4 %collective-permute-done.5.refs_1_ = bf16[128,128]{1,0:T(8,128)(2,1)S(1)} collective-permute-done((bf16[128,128]{1,0:T(8,128)(2,1)S(1)}, bf16[128,128]{1,0:T(8,128)(2,1)S(1)}, u32[]{:S(2)}, u32[]{:S(2)}) %collective-permute-start.5) | collective-permute-done | bytes 32800 | tf_op jit(solution)/shard_map/ppermute | solution.py:64
  25.0 4.2 %collective-permute-start.8 = (bf16[128,128]{1,0:T(8,128)(2,1)S(1)}, bf16[128,128]{1,0:T(8,128)(2,1)S(1)}, u32[]{:S(2)}, u32[]{:S(2)}) collective-permute-start(bf16[128,128]{1,0:T(8,128)(2,1)S(1)} %shard_map.114.z0), channel_id=1, source_target_pairs={{0,24},{2,26},{4,28},{6,30},{8,16},{10,18},{12,20},{14,22},{16,8},... | collective-permute-start | bytes 98312 | tf_op jit(solution)/shard_map/ppermute | solution.py:62
  31.1 2.9 %collective-permute-done.7.z2 = bf16[128,128]{1,0:T(8,128)(2,1)S(1)} collective-permute-done((bf16[128,128]{1,0:T(8,128)(2,1)S(1)}, bf16[128,128]{1,0:T(8,128)(2,1)S(1)}, u32[]{:S(2)}, u32[]{:S(2)}) %collective-permute-start.7) | collective-permute-done | bytes 32800 | tf_op jit(solution)/shard_map/ppermute | solution.py:62
  36.9 2.4 %collective-permute-start.13 = (bf16[128,128]{1,0:T(8,128)(2,1)S(1)}, bf16[128,128]{1,0:T(8,128)(2,1)S(1)}, u32[]{:S(2)}, u32[]{:S(2)}) collective-permute-start(bf16[128,128]{1,0:T(8,128)(2,1)S(1)} %get-tuple-element.65), channel_id=1, source_target_pairs={{0,5},{1,4},{2,7},{3,6},{4,1},{5,0},{6,3},{7,2},{8,13},{9,12},{10,... | collective-permute-start | bytes 98312 | tf_op jit(solution)/shard_map/ppermute | solution.py:70
  43.0 1.5 %collective-permute-start.16 = (bf16[128,128]{1,0:T(8,128)(2,1)S(1)}, bf16[128,128]{1,0:T(8,128)(2,1)S(1)}, u32[]{:S(2)}, u32[]{:S(2)}) collective-permute-start(bf16[128,128]{1,0:T(8,128)(2,1)S(1)} %shard_map.117.z0), channel_id=1, source_target_pairs={{0,24},{2,26},{4,28},{6,30},{8,16},{10,18},{12,20},{14,22},{16,8},... | collective-permute-start | bytes 98312 | tf_op jit(solution)/shard_map/ppermute | solution.py:62
  45.0 2.4 %collective-permute-start.14 = (bf16[128,128]{1,0:T(8,128)(2,1)S(1)}, bf16[128,128]{1,0:T(8,128)(2,1)S(1)}, u32[]{:S(2)}, u32[]{:S(2)}) collective-permute-start(bf16[128,128]{1,0:T(8,128)(2,1)S(1)} %shard_map.117.z0), channel_id=1, source_target_pairs={{0,8},{2,10},{4,12},{6,14},{8,0},{10,2},{12,4},{14,6},{16,24},{18,... | collective-permute-start | bytes 98312 | tf_op jit(solution)/shard_map/ppermute | solution.py:62
  51.3 2.0 %collective-permute-start.21 = (bf16[512,128]{1,0:T(8,128)(2,1)S(1)}, bf16[512,128]{1,0:T(8,128)(2,1)S(1)}, u32[]{:S(2)}, u32[]{:S(2)}) collective-permute-start(bf16[512,128]{1,0:T(8,128)(2,1)S(1)} %get-tuple-element.75), channel_id=1, source_target_pairs={{0,5},{1,4},{2,7},{3,6},{4,1},{5,0},{6,3},{7,2},{8,13},{9,12},{10,... | collective-permute-start | bytes 393224 | tf_op jit(solution)/shard_map/ppermute | solution.py:70
  54.9 3.7 %collective-permute-done.21.refs_2_ = bf16[512,128]{1,0:T(8,128)(2,1)S(1)} collective-permute-done((bf16[512,128]{1,0:T(8,128)(2,1)S(1)}, bf16[512,128]{1,0:T(8,128)(2,1)S(1)}, u32[]{:S(2)}, u32[]{:S(2)}) %collective-permute-start.21) | collective-permute-done | bytes 131104 | tf_op jit(solution)/shard_map/ppermute | solution.py:70
  58.6 2.0 %collective-permute-done.20.refs_1_ = bf16[512,128]{1,0:T(8,128)(2,1)S(1)} collective-permute-done((bf16[512,128]{1,0:T(8,128)(2,1)S(1)}, bf16[512,128]{1,0:T(8,128)(2,1)S(1)}, u32[]{:S(2)}, u32[]{:S(2)}) %collective-permute-start.20) | collective-permute-done | bytes 131104 | tf_op jit(solution)/shard_map/ppermute | solution.py:62
  63.2 1.7 %collective-permute-start.23 = (bf16[128,128]{1,0:T(8,128)(2,1)S(1)}, bf16[128,128]{1,0:T(8,128)(2,1)S(1)}, u32[]{:S(2)}, u32[]{:S(2)}) collective-permute-start(bf16[128,128]{1,0:T(8,128)(2,1)S(1)} %get-tuple-element.83), channel_id=1, source_target_pairs={{0,8},{2,10},{4,12},{6,14},{8,0},{10,2},{12,4},{14,6},{16,24},{18,... | collective-permute-start | bytes 98312 | tf_op jit(solution)/shard_map/ppermute | solution.py:62
  66.2 1.5 %collective-permute-start.25 = (bf16[128,128]{1,0:T(8,128)(2,1)S(1)}, bf16[128,128]{1,0:T(8,128)(2,1)S(1)}, u32[]{:S(2)}, u32[]{:S(2)}) collective-permute-start(bf16[128,128]{1,0:T(8,128)(2,1)S(1)} %get-tuple-element.85), channel_id=1, source_target_pairs={{0,24},{2,26},{4,28},{6,30},{8,16},{10,18},{12,20},{14,22},{16,8},... | collective-permute-start | bytes 98312 | tf_op jit(solution)/shard_map/ppermute | solution.py:62
  67.6 2.3 %collective-permute-done.24.refs_1_ = bf16[128,128]{1,0:T(8,128)(2,1)S(1)} collective-permute-done((bf16[128,128]{1,0:T(8,128)(2,1)S(1)}, bf16[128,128]{1,0:T(8,128)(2,1)S(1)}, u32[]{:S(2)}, u32[]{:S(2)}) %collective-permute-start.24) | collective-permute-done | bytes 32800 | tf_op jit(solution)/shard_map/ppermute | solution.py:62
  69.9 1.9 %collective-permute-done.25.refs_2_ = bf16[128,128]{1,0:T(8,128)(2,1)S(1)} collective-permute-done((bf16[128,128]{1,0:T(8,128)(2,1)S(1)}, bf16[128,128]{1,0:T(8,128)(2,1)S(1)}, u32[]{:S(2)}, u32[]{:S(2)}) %collective-permute-start.25) | collective-permute-done | bytes 32800 | tf_op jit(solution)/shard_map/ppermute | solution.py:62
  72.0 1.5 %collective-permute-start.28 = (bf16[128,128]{1,0:T(8,128)(2,1)S(1)}, bf16[128,128]{1,0:T(8,128)(2,1)S(1)}, u32[]{:S(2)}, u32[]{:S(2)}) collective-permute-start(bf16[128,128]{1,0:T(8,128)(2,1)S(1)} %shard_map.126.refs_0_), channel_id=1, source_target_pairs={{0,5},{1,4},{2,7},{3,6},{4,1},{5,0},{6,3},{7,2},{8,13},{9,12},{10,... | collective-permute-start | bytes 98312 | tf_op jit(solution)/shard_map/ppermute | solution.py:70
  74.2 1.4 %collective-permute-start.26 = (bf16[128,128]{1,0:T(8,128)(2,1)S(1)}, bf16[128,128]{1,0:T(8,128)(2,1)S(1)}, u32[]{:S(2)}, u32[]{:S(2)}) collective-permute-start(bf16[128,128]{1,0:T(8,128)(2,1)S(1)} %shard_map.126.refs_0_), channel_id=1, source_target_pairs={{0,1},{1,0},{2,3},{3,2},{4,5},{5,4},{6,7},{7,6},{8,9},{9,8},{10,11... | collective-permute-start | bytes 98312 | tf_op jit(solution)/shard_map/ppermute | solution.py:64
  75.6 1.3 %collective-permute-done.28.refs_3_ = bf16[128,128]{1,0:T(8,128)(2,1)S(1)} collective-permute-done((bf16[128,128]{1,0:T(8,128)(2,1)S(1)}, bf16[128,128]{1,0:T(8,128)(2,1)S(1)}, u32[]{:S(2)}, u32[]{:S(2)}) %collective-permute-start.28) | collective-permute-done | bytes 32800 | tf_op jit(solution)/shard_map/ppermute | solution.py:70
  79.9 2.0 %collective-permute-start.31 = (bf16[128,128]{1,0:T(8,128)(2,1)S(1)}, bf16[128,128]{1,0:T(8,128)(2,1)S(1)}, u32[]{:S(2)}, u32[]{:S(2)}) collective-permute-start(bf16[128,128]{1,0:T(8,128)(2,1)S(1)} %get-tuple-element.89), channel_id=1, source_target_pairs={{0,16},{2,18},{4,20},{6,22},{8,24},{10,26},{12,28},{14,30},{16,0},... | collective-permute-start | bytes 98312 | tf_op jit(solution)/shard_map/ppermute | solution.py:62
  81.9 2.4 %collective-permute-start.32 = (bf16[128,128]{1,0:T(8,128)(2,1)S(1)}, bf16[128,128]{1,0:T(8,128)(2,1)S(1)}, u32[]{:S(2)}, u32[]{:S(2)}) collective-permute-start(bf16[128,128]{1,0:T(8,128)(2,1)S(1)} %get-tuple-element.90), channel_id=1, source_target_pairs={{0,24},{2,26},{4,28},{6,30},{8,16},{10,18},{12,20},{14,22},{16,8},... | collective-permute-start | bytes 98312 | tf_op jit(solution)/shard_map/ppermute | solution.py:62
  84.8 2.8 %collective-permute-done.32.refs_2_ = bf16[128,128]{1,0:T(8,128)(2,1)S(1)} collective-permute-done((bf16[128,128]{1,0:T(8,128)(2,1)S(1)}, bf16[128,128]{1,0:T(8,128)(2,1)S(1)}, u32[]{:S(2)}, u32[]{:S(2)}) %collective-permute-start.32) | collective-permute-done | bytes 32800 | tf_op jit(solution)/shard_map/ppermute | solution.py:62
  88.0 1.7 %collective-permute-start.35 = (bf16[256,128]{1,0:T(8,128)(2,1)S(1)}, bf16[256,128]{1,0:T(8,128)(2,1)S(1)}, u32[]{:S(2)}, u32[]{:S(2)}) collective-permute-start(bf16[256,128]{1,0:T(8,128)(2,1)S(1)} %shard_map.130.refs_0_), channel_id=1, source_target_pairs={{0,5},{1,4},{2,7},{3,6},{4,1},{5,0},{6,3},{7,2},{8,13},{9,12},{10,... | collective-permute-start | bytes 196616 | tf_op jit(solution)/shard_map/ppermute | solution.py:70
  91.5 1.8 %collective-permute-done.35.refs_3_ = bf16[256,128]{1,0:T(8,128)(2,1)S(1)} collective-permute-done((bf16[256,128]{1,0:T(8,128)(2,1)S(1)}, bf16[256,128]{1,0:T(8,128)(2,1)S(1)}, u32[]{:S(2)}, u32[]{:S(2)}) %collective-permute-start.35) | collective-permute-done | bytes 65568 | tf_op jit(solution)/shard_map/ppermute | solution.py:70
  97.1 2.9 %collective-permute-start.38 = (bf16[256,128]{1,0:T(8,128)(2,1)S(1)}, bf16[256,128]{1,0:T(8,128)(2,1)S(1)}, u32[]{:S(2)}, u32[]{:S(2)}) collective-permute-start(bf16[256,128]{1,0:T(8,128)(2,1)S(1)} %get-tuple-element.96), channel_id=1, source_target_pairs={{0,16},{2,18},{4,20},{6,22},{8,24},{10,26},{12,28},{14,30},{16,0},... | collective-permute-start | bytes 196616 | tf_op jit(solution)/shard_map/ppermute | solution.py:62
  100.0 1.5 %collective-permute-start.39 = (bf16[256,128]{1,0:T(8,128)(2,1)S(1)}, bf16[256,128]{1,0:T(8,128)(2,1)S(1)}, u32[]{:S(2)}, u32[]{:S(2)}) collective-permute-start(bf16[256,128]{1,0:T(8,128)(2,1)S(1)} %get-tuple-element.97), channel_id=1, source_target_pairs={{0,24},{2,26},{4,28},{6,30},{8,16},{10,18},{12,20},{14,22},{16,8},... | collective-permute-start | bytes 196616 | tf_op jit(solution)/shard_map/ppermute | solution.py:62
  102.4 2.4 %collective-permute-done.38.refs_1_ = bf16[256,128]{1,0:T(8,128)(2,1)S(1)} collective-permute-done((bf16[256,128]{1,0:T(8,128)(2,1)S(1)}, bf16[256,128]{1,0:T(8,128)(2,1)S(1)}, u32[]{:S(2)}, u32[]{:S(2)}) %collective-permute-start.38) | collective-permute-done | bytes 65568 | tf_op jit(solution)/shard_map/ppermute | solution.py:62
  104.8 1.4 %collective-permute-done.39.refs_2_ = bf16[256,128]{1,0:T(8,128)(2,1)S(1)} collective-permute-done((bf16[256,128]{1,0:T(8,128)(2,1)S(1)}, bf16[256,128]{1,0:T(8,128)(2,1)S(1)}, u32[]{:S(2)}, u32[]{:S(2)}) %collective-permute-start.39) | collective-permute-done | bytes 65568 | tf_op jit(solution)/shard_map/ppermute | solution.py:62
  (88 shorter events, 33.7 us)
Async XLA Ops:
  0.6 11.8 %collective-permute-start.2 = (bf16[128,128]{1,0:T(8,128)(2,1)}, bf16[128,128]{1,0:T(8,128)(2,1)S(1)}, u32[]{:S(2)}, u32[]{:S(2)}) collective-permute-start(bf16[128,128]{1,0:T(8,128)(2,1)} %anchor_ref.1), channel_id=1, source_target_pairs={{0,24},{2,26},{4,28},{6,30},{8,16},{10,18},{12,20},{14,22},{16,8},... | collective-permute-start | bytes 98312 | tf_op jit(solution)/shard_map/ppermute | solution.py:62
  5.8 6.7 %collective-permute-start.1 = (bf16[128,128]{1,0:T(8,128)(2,1)}, bf16[128,128]{1,0:T(8,128)(2,1)S(1)}, u32[]{:S(2)}, u32[]{:S(2)}) collective-permute-start(bf16[128,128]{1,0:T(8,128)(2,1)} %anchor_ref.1), channel_id=1, source_target_pairs={{0,16},{2,18},{4,20},{6,22},{8,24},{10,26},{12,28},{14,30},{16,0},... | collective-permute-start | bytes 98312 | tf_op jit(solution)/shard_map/ppermute | solution.py:62
  5.8 6.7 %collective-permute-start = (bf16[128,128]{1,0:T(8,128)(2,1)}, bf16[128,128]{1,0:T(8,128)(2,1)S(1)}, u32[]{:S(2)}, u32[]{:S(2)}) collective-permute-start(bf16[128,128]{1,0:T(8,128)(2,1)} %anchor_ref.1), channel_id=1, source_target_pairs={{0,8},{2,10},{4,12},{6,14},{8,0},{10,2},{12,4},{14,6},{16,24},{18,... | collective-permute-start | bytes 98312 | tf_op jit(solution)/shard_map/ppermute | solution.py:62
  12.5 5.0 %collective-permute-start.3 = (bf16[512,128]{1,0:T(8,128)(2,1)S(1)}, bf16[512,128]{1,0:T(8,128)(2,1)S(1)}, u32[]{:S(2)}, u32[]{:S(2)}) collective-permute-start(bf16[512,128]{1,0:T(8,128)(2,1)S(1)} %pad_maximum_fusion.1), channel_id=1, source_target_pairs={{0,4},{2,6},{4,0},{6,2},{8,12},{10,14},{12,8},{14,10},{16,20},{18,... | collective-permute-start | bytes 393224 | tf_op jit(solution)/shard_map/ppermute | solution.py:62
  17.5 16.6 %collective-permute-start.9 = (bf16[256,1152]{1,0:T(8,128)(2,1)S(1)}, bf16[256,1152]{1,0:T(8,128)(2,1)S(1)}, u32[]{:S(2)}, u32[]{:S(2)}) collective-permute-start(bf16[256,1152]{1,0:T(8,128)(2,1)S(1)} %get-tuple-element.61.refs_1_), channel_id=1, source_target_pairs={{0,4},{2,6},{4,0},{6,2},{8,12},{10,14},{12,8},{14,10},{16,20},{18,... | collective-permute-start | bytes 1769480 | tf_op jit(solution)/shard_map/ppermute | solution.py:62
  20.9 4.0 %collective-permute-start.5 = (bf16[128,128]{1,0:T(8,128)(2,1)S(1)}, bf16[128,128]{1,0:T(8,128)(2,1)S(1)}, u32[]{:S(2)}, u32[]{:S(2)}) collective-permute-start(bf16[128,128]{1,0:T(8,128)(2,1)S(1)} %get-tuple-element.60), channel_id=1, source_target_pairs={{0,1},{1,0},{2,3},{3,2},{4,5},{5,4},{6,7},{7,6},{8,9},{9,8},{10,11... | collective-permute-start | bytes 98312 | tf_op jit(solution)/shard_map/ppermute | solution.py:64
  25.0 6.1 %collective-permute-start.8 = (bf16[128,128]{1,0:T(8,128)(2,1)S(1)}, bf16[128,128]{1,0:T(8,128)(2,1)S(1)}, u32[]{:S(2)}, u32[]{:S(2)}) collective-permute-start(bf16[128,128]{1,0:T(8,128)(2,1)S(1)} %shard_map.114.z0), channel_id=1, source_target_pairs={{0,24},{2,26},{4,28},{6,30},{8,16},{10,18},{12,20},{14,22},{16,8},... | collective-permute-start | bytes 98312 | tf_op jit(solution)/shard_map/ppermute | solution.py:62
  29.2 4.8 %collective-permute-start.7 = (bf16[128,128]{1,0:T(8,128)(2,1)S(1)}, bf16[128,128]{1,0:T(8,128)(2,1)S(1)}, u32[]{:S(2)}, u32[]{:S(2)}) collective-permute-start(bf16[128,128]{1,0:T(8,128)(2,1)S(1)} %shard_map.114.z0), channel_id=1, source_target_pairs={{0,16},{2,18},{4,20},{6,22},{8,24},{10,26},{12,28},{14,30},{16,0},... | collective-permute-start | bytes 98312 | tf_op jit(solution)/shard_map/ppermute | solution.py:62
  29.2 4.8 %collective-permute-start.6 = (bf16[128,128]{1,0:T(8,128)(2,1)S(1)}, bf16[128,128]{1,0:T(8,128)(2,1)S(1)}, u32[]{:S(2)}, u32[]{:S(2)}) collective-permute-start(bf16[128,128]{1,0:T(8,128)(2,1)S(1)} %shard_map.114.z0), channel_id=1, source_target_pairs={{0,8},{2,10},{4,12},{6,14},{8,0},{10,2},{12,4},{14,6},{16,24},{18,... | collective-permute-start | bytes 98312 | tf_op jit(solution)/shard_map/ppermute | solution.py:62
  35.8 4.0 %collective-permute-start.11 = (bf16[128,128]{1,0:T(8,128)(2,1)S(1)}, bf16[128,128]{1,0:T(8,128)(2,1)S(1)}, u32[]{:S(2)}, u32[]{:S(2)}) collective-permute-start(bf16[128,128]{1,0:T(8,128)(2,1)S(1)} %get-tuple-element.63), channel_id=1, source_target_pairs={{0,1},{1,0},{2,3},{3,2},{4,5},{5,4},{6,7},{7,6},{8,9},{9,8},{10,11... | collective-permute-start | bytes 98312 | tf_op jit(solution)/shard_map/ppermute | solution.py:64
  36.4 4.3 %collective-permute-start.12 = (bf16[128,128]{1,0:T(8,128)(2,1)S(1)}, bf16[128,128]{1,0:T(8,128)(2,1)S(1)}, u32[]{:S(2)}, u32[]{:S(2)}) collective-permute-start(bf16[128,128]{1,0:T(8,128)(2,1)S(1)} %get-tuple-element.64), channel_id=1, source_target_pairs={{0,4},{2,6},{4,0},{6,2},{8,12},{10,14},{12,8},{14,10},{16,20},{18,... | collective-permute-start | bytes 98312 | tf_op jit(solution)/shard_map/ppermute | solution.py:62
  36.9 4.8 %collective-permute-start.13 = (bf16[128,128]{1,0:T(8,128)(2,1)S(1)}, bf16[128,128]{1,0:T(8,128)(2,1)S(1)}, u32[]{:S(2)}, u32[]{:S(2)}) collective-permute-start(bf16[128,128]{1,0:T(8,128)(2,1)S(1)} %get-tuple-element.65), channel_id=1, source_target_pairs={{0,5},{1,4},{2,7},{3,6},{4,1},{5,0},{6,3},{7,2},{8,13},{9,12},{10,... | collective-permute-start | bytes 98312 | tf_op jit(solution)/shard_map/ppermute | solution.py:70
  41.9 7.7 %collective-permute-start.17 = (bf16[512,128]{1,0:T(8,128)(2,1)S(1)}, bf16[512,128]{1,0:T(8,128)(2,1)S(1)}, u32[]{:S(2)}, u32[]{:S(2)}) collective-permute-start(bf16[512,128]{1,0:T(8,128)(2,1)S(1)} %get-tuple-element.76.refs_3_), channel_id=1, source_target_pairs={{0,1},{1,0},{2,3},{3,2},{4,5},{5,4},{6,7},{7,6},{8,9},{9,8},{10,11... | collective-permute-start | bytes 393224 | tf_op jit(solution)/shard_map/ppermute | solution.py:64
  43.0 5.7 %collective-permute-start.16 = (bf16[128,128]{1,0:T(8,128)(2,1)S(1)}, bf16[128,128]{1,0:T(8,128)(2,1)S(1)}, u32[]{:S(2)}, u32[]{:S(2)}) collective-permute-start(bf16[128,128]{1,0:T(8,128)(2,1)S(1)} %shard_map.117.z0), channel_id=1, source_target_pairs={{0,24},{2,26},{4,28},{6,30},{8,16},{10,18},{12,20},{14,22},{16,8},... | collective-permute-start | bytes 98312 | tf_op jit(solution)/shard_map/ppermute | solution.py:62
  44.4 4.8 %collective-permute-start.15 = (bf16[128,128]{1,0:T(8,128)(2,1)S(1)}, bf16[128,128]{1,0:T(8,128)(2,1)S(1)}, u32[]{:S(2)}, u32[]{:S(2)}) collective-permute-start(bf16[128,128]{1,0:T(8,128)(2,1)S(1)} %shard_map.117.z0), channel_id=1, source_target_pairs={{0,16},{2,18},{4,20},{6,22},{8,24},{10,26},{12,28},{14,30},{16,0},... | collective-permute-start | bytes 98312 | tf_op jit(solution)/shard_map/ppermute | solution.py:62
  45.0 4.6 %collective-permute-start.14 = (bf16[128,128]{1,0:T(8,128)(2,1)S(1)}, bf16[128,128]{1,0:T(8,128)(2,1)S(1)}, u32[]{:S(2)}, u32[]{:S(2)}) collective-permute-start(bf16[128,128]{1,0:T(8,128)(2,1)S(1)} %shard_map.117.z0), channel_id=1, source_target_pairs={{0,8},{2,10},{4,12},{6,14},{8,0},{10,2},{12,4},{14,6},{16,24},{18,... | collective-permute-start | bytes 98312 | tf_op jit(solution)/shard_map/ppermute | solution.py:62
  51.3 7.3 %collective-permute-start.21 = (bf16[512,128]{1,0:T(8,128)(2,1)S(1)}, bf16[512,128]{1,0:T(8,128)(2,1)S(1)}, u32[]{:S(2)}, u32[]{:S(2)}) collective-permute-start(bf16[512,128]{1,0:T(8,128)(2,1)S(1)} %get-tuple-element.75), channel_id=1, source_target_pairs={{0,5},{1,4},{2,7},{3,6},{4,1},{5,0},{6,3},{7,2},{8,13},{9,12},{10,... | collective-permute-start | bytes 393224 | tf_op jit(solution)/shard_map/ppermute | solution.py:70
  53.4 7.3 %collective-permute-start.20 = (bf16[512,128]{1,0:T(8,128)(2,1)S(1)}, bf16[512,128]{1,0:T(8,128)(2,1)S(1)}, u32[]{:S(2)}, u32[]{:S(2)}) collective-permute-start(bf16[512,128]{1,0:T(8,128)(2,1)S(1)} %get-tuple-element.75), channel_id=1, source_target_pairs={{0,4},{2,6},{4,0},{6,2},{8,12},{10,14},{12,8},{14,10},{16,20},{18,... | collective-permute-start | bytes 393224 | tf_op jit(solution)/shard_map/ppermute | solution.py:62
  53.9 7.3 %collective-permute-start.19 = (bf16[512,128]{1,0:T(8,128)(2,1)S(1)}, bf16[512,128]{1,0:T(8,128)(2,1)S(1)}, u32[]{:S(2)}, u32[]{:S(2)}) collective-permute-start(bf16[512,128]{1,0:T(8,128)(2,1)S(1)} %get-tuple-element.75), channel_id=1, source_target_pairs={{0,1},{1,0},{2,3},{3,2},{4,5},{5,4},{6,7},{7,6},{8,9},{9,8},{10,11... | collective-permute-start | bytes 393224 | tf_op jit(solution)/shard_map/ppermute | solution.py:64
  63.2 4.5 %collective-permute-start.23 = (bf16[128,128]{1,0:T(8,128)(2,1)S(1)}, bf16[128,128]{1,0:T(8,128)(2,1)S(1)}, u32[]{:S(2)}, u32[]{:S(2)}) collective-permute-start(bf16[128,128]{1,0:T(8,128)(2,1)S(1)} %get-tuple-element.83), channel_id=1, source_target_pairs={{0,8},{2,10},{4,12},{6,14},{8,0},{10,2},{12,4},{14,6},{16,24},{18,... | collective-permute-start | bytes 98312 | tf_op jit(solution)/shard_map/ppermute | solution.py:62
  64.9 5.0 %collective-permute-start.24 = (bf16[128,128]{1,0:T(8,128)(2,1)S(1)}, bf16[128,128]{1,0:T(8,128)(2,1)S(1)}, u32[]{:S(2)}, u32[]{:S(2)}) collective-permute-start(bf16[128,128]{1,0:T(8,128)(2,1)S(1)} %get-tuple-element.84), channel_id=1, source_target_pairs={{0,16},{2,18},{4,20},{6,22},{8,24},{10,26},{12,28},{14,30},{16,0},... | collective-permute-start | bytes 98312 | tf_op jit(solution)/shard_map/ppermute | solution.py:62
  66.2 5.7 %collective-permute-start.25 = (bf16[128,128]{1,0:T(8,128)(2,1)S(1)}, bf16[128,128]{1,0:T(8,128)(2,1)S(1)}, u32[]{:S(2)}, u32[]{:S(2)}) collective-permute-start(bf16[128,128]{1,0:T(8,128)(2,1)S(1)} %get-tuple-element.85), channel_id=1, source_target_pairs={{0,24},{2,26},{4,28},{6,30},{8,16},{10,18},{12,20},{14,22},{16,8},... | collective-permute-start | bytes 98312 | tf_op jit(solution)/shard_map/ppermute | solution.py:62
  72.0 4.9 %collective-permute-start.28 = (bf16[128,128]{1,0:T(8,128)(2,1)S(1)}, bf16[128,128]{1,0:T(8,128)(2,1)S(1)}, u32[]{:S(2)}, u32[]{:S(2)}) collective-permute-start(bf16[128,128]{1,0:T(8,128)(2,1)S(1)} %shard_map.126.refs_0_), channel_id=1, source_target_pairs={{0,5},{1,4},{2,7},{3,6},{4,1},{5,0},{6,3},{7,2},{8,13},{9,12},{10,... | collective-permute-start | bytes 98312 | tf_op jit(solution)/shard_map/ppermute | solution.py:70
  79.8 4.5 %collective-permute-start.30 = (bf16[128,128]{1,0:T(8,128)(2,1)S(1)}, bf16[128,128]{1,0:T(8,128)(2,1)S(1)}, u32[]{:S(2)}, u32[]{:S(2)}) collective-permute-start(bf16[128,128]{1,0:T(8,128)(2,1)S(1)} %get-tuple-element.88), channel_id=1, source_target_pairs={{0,8},{2,10},{4,12},{6,14},{8,0},{10,2},{12,4},{14,6},{16,24},{18,... | collective-permute-start | bytes 98312 | tf_op jit(solution)/shard_map/ppermute | solution.py:62
  79.9 4.9 %collective-permute-start.31 = (bf16[128,128]{1,0:T(8,128)(2,1)S(1)}, bf16[128,128]{1,0:T(8,128)(2,1)S(1)}, u32[]{:S(2)}, u32[]{:S(2)}) collective-permute-start(bf16[128,128]{1,0:T(8,128)(2,1)S(1)} %get-tuple-element.89), channel_id=1, source_target_pairs={{0,16},{2,18},{4,20},{6,22},{8,24},{10,26},{12,28},{14,30},{16,0},... | collective-permute-start | bytes 98312 | tf_op jit(solution)/shard_map/ppermute | solution.py:62
  81.9 5.7 %collective-permute-start.32 = (bf16[128,128]{1,0:T(8,128)(2,1)S(1)}, bf16[128,128]{1,0:T(8,128)(2,1)S(1)}, u32[]{:S(2)}, u32[]{:S(2)}) collective-permute-start(bf16[128,128]{1,0:T(8,128)(2,1)S(1)} %get-tuple-element.90), channel_id=1, source_target_pairs={{0,24},{2,26},{4,28},{6,30},{8,16},{10,18},{12,20},{14,22},{16,8},... | collective-permute-start | bytes 98312 | tf_op jit(solution)/shard_map/ppermute | solution.py:62
  88.0 5.3 %collective-permute-start.35 = (bf16[256,128]{1,0:T(8,128)(2,1)S(1)}, bf16[256,128]{1,0:T(8,128)(2,1)S(1)}, u32[]{:S(2)}, u32[]{:S(2)}) collective-permute-start(bf16[256,128]{1,0:T(8,128)(2,1)S(1)} %shard_map.130.refs_0_), channel_id=1, source_target_pairs={{0,5},{1,4},{2,7},{3,6},{4,1},{5,0},{6,3},{7,2},{8,13},{9,12},{10,... | collective-permute-start | bytes 196616 | tf_op jit(solution)/shard_map/ppermute | solution.py:70
  89.7 4.3 %collective-permute-start.34 = (bf16[256,128]{1,0:T(8,128)(2,1)S(1)}, bf16[256,128]{1,0:T(8,128)(2,1)S(1)}, u32[]{:S(2)}, u32[]{:S(2)}) collective-permute-start(bf16[256,128]{1,0:T(8,128)(2,1)S(1)} %shard_map.130.refs_0_), channel_id=1, source_target_pairs={{0,4},{2,6},{4,0},{6,2},{8,12},{10,14},{12,8},{14,10},{16,20},{18,... | collective-permute-start | bytes 196616 | tf_op jit(solution)/shard_map/ppermute | solution.py:62
  90.9 4.3 %collective-permute-start.33 = (bf16[256,128]{1,0:T(8,128)(2,1)S(1)}, bf16[256,128]{1,0:T(8,128)(2,1)S(1)}, u32[]{:S(2)}, u32[]{:S(2)}) collective-permute-start(bf16[256,128]{1,0:T(8,128)(2,1)S(1)} %shard_map.130.refs_0_), channel_id=1, source_target_pairs={{0,1},{1,0},{2,3},{3,2},{4,5},{5,4},{6,7},{7,6},{8,9},{9,8},{10,11... | collective-permute-start | bytes 196616 | tf_op jit(solution)/shard_map/ppermute | solution.py:64
  97.1 5.4 %collective-permute-start.37 = (bf16[256,128]{1,0:T(8,128)(2,1)S(1)}, bf16[256,128]{1,0:T(8,128)(2,1)S(1)}, u32[]{:S(2)}, u32[]{:S(2)}) collective-permute-start(bf16[256,128]{1,0:T(8,128)(2,1)S(1)} %get-tuple-element.95), channel_id=1, source_target_pairs={{0,8},{2,10},{4,12},{6,14},{8,0},{10,2},{12,4},{14,6},{16,24},{18,... | collective-permute-start | bytes 196616 | tf_op jit(solution)/shard_map/ppermute | solution.py:62
  97.1 7.7 %collective-permute-start.38 = (bf16[256,128]{1,0:T(8,128)(2,1)S(1)}, bf16[256,128]{1,0:T(8,128)(2,1)S(1)}, u32[]{:S(2)}, u32[]{:S(2)}) collective-permute-start(bf16[256,128]{1,0:T(8,128)(2,1)S(1)} %get-tuple-element.96), channel_id=1, source_target_pairs={{0,16},{2,18},{4,20},{6,22},{8,24},{10,26},{12,28},{14,30},{16,0},... | collective-permute-start | bytes 196616 | tf_op jit(solution)/shard_map/ppermute | solution.py:62
  100.0 6.2 %collective-permute-start.39 = (bf16[256,128]{1,0:T(8,128)(2,1)S(1)}, bf16[256,128]{1,0:T(8,128)(2,1)S(1)}, u32[]{:S(2)}, u32[]{:S(2)}) collective-permute-start(bf16[256,128]{1,0:T(8,128)(2,1)S(1)} %get-tuple-element.97), channel_id=1, source_target_pairs={{0,24},{2,26},{4,28},{6,30},{8,16},{10,18},{12,20},{14,22},{16,8},... | collective-permute-start | bytes 196616 | tf_op jit(solution)/shard_map/ppermute | solution.py:62
  (14 other events, 61.7 us)

commit v4 on v3

--- a/solution.py
+++ b/solution.py
@@ -79,12 +79,14 @@
     n_chunks = slots // chunk
     assert slots % chunk == 0
 
-    def build(where_ref, count, rows_hbm, cols_hbm, tiles_hbm, inject, cotan, mask, *refs):
+    def build(where_ref, count, *refs):
+        small_hbm, tiles_hbm, refs = refs[:5], refs[5], refs[6:]
         parts, turned, fixed_out = refs[:n_y], refs[n_y], refs[n_y + 1]
-        rows, cols, tiles, acc, index_sem, tile_sem = refs[n_y + 2 :]
+        small, (tiles, acc, small_sem, tile_sem) = refs[n_y + 2 : n_y + 7], refs[n_y + 7 :]
+        rows, cols, inject, cotan, mask = small
         copies = [
-            pltpu.make_async_copy(rows_hbm, rows, index_sem.at[0]),
-            pltpu.make_async_copy(cols_hbm, cols, index_sem.at[1]),
+            pltpu.make_async_copy(source, target, small_sem.at[i])
+            for i, (source, target) in enumerate(zip(small_hbm, small))
         ]
         pieces = [slice(c * chunk, (c + 1) * chunk) for c in range(n_chunks)]
         loads = [
@@ -94,11 +96,11 @@
         for copy in copies + loads:
             copy.start()
         acc[...] = jnp.zeros_like(acc)
+        for copy in copies:
+            copy.wait()
         fixed_out[:TILE] = inject[...]
         kept_nodes = jnp.broadcast_to(mask[...].astype(F32), (TILE, TILE)).T[:, :1]
         fixed_out[TILE:] = (cotan[...].astype(F32) * kept_nodes).astype(BF16)
-        for copy in copies:
-            copy.wait()
 
         def add(k, carry):
             s = cols[0, 0, k] ^ where_ref[0]
@@ -126,23 +128,21 @@
     assert n_col >= 2
     part_shape = (n_col * TILE, 2 * line_rows)
     sent_shape = (n_col * TILE, 2 * line_rows + hidden)
+    small = (tile_rows, tile_cols, injection, cotangent, node_mask.reshape(1, -1))
     *parts, turned, fixed = vmem_call(
         build,
         [(part_shape, BF16)] + [(sent_shape, BF16)] * (n_y - 1)
         + [(part_shape[::-1], BF16), ((2 * TILE, hidden), BF16)],
         where,
         tile_counts,
-        *[pltpu.with_memory_space_constraint(v, pltpu.HBM) for v in (tile_rows, tile_cols, tile_values)],
-        injection,
-        cotangent,
-        node_mask.reshape(1, -1),
-        spaces=[pltpu.SMEM] * 2 + [pltpu.HBM] * 3 + [pltpu.VMEM] * 3,
+        *[pltpu.with_memory_space_constraint(v, pltpu.HBM) for v in (*small, tile_values)],
+        spaces=[pltpu.SMEM] * 2 + [pltpu.HBM] * 6,
         scratch=[
-            pltpu.SMEM(tile_rows.shape, jnp.int32),
-            pltpu.SMEM(tile_cols.shape, jnp.int32),
+            *[pltpu.SMEM(v.shape, v.dtype) for v in small[:2]],
+            *[pltpu.VMEM(v.shape, v.dtype) for v in small[2:]],
             pltpu.VMEM((slots, TILE, TILE), BF16),
             pltpu.VMEM((n_y * n_col * 2 * LINE, TILE, TILE), F32),
-            pltpu.SemaphoreType.DMA((2,)),
+            pltpu.SemaphoreType.DMA((5,)),
             pltpu.SemaphoreType.DMA((n_chunks,)),
         ],
     )
@@ -250,7 +250,7 @@
             while bit < z_step:
                 joined = jnp.concatenate([joined, exchange(joined, bit)], axis=0)
                 bit *= 2
-            joined, sent = lax.optimization_barrier((joined, parts[1:]))
+            sent = parts[1:]
             far = exchange(joined, 1)
             outs = [(block, F32)] + [(block, BF16)] * (n_col - 1)
             mine, *sends = vmem_call(first_partial, outs, joined, far, *parts)

time: 107 us -> 105 us (0.981)
  local copies, waits for them, and re-layouts: 2.18 us -> 0.04 us
  waiting for transfers between devices: 45.6 us -> 47.6 us
  starting transfers between devices: 48.3 us -> 46.6 us
    ppermute x4, starting transfers between devices: 7.64 us -> 4.92 us  [exchange(): return lax.ppermute(value, ('row', 'col'), pairs)]
    unnamed x12 -> x7, local copies, waits for them, and re-layouts: 2.18 us -> 0.03 us
    ppermute x4, waiting for transfers between devices: 7.9 us -> 9.71 us  [exchange(): return lax.ppermute(value, ('row', 'col'), pairs)]
    ppermute x30, starting transfers between devices: 34.4 us -> 36.1 us  [exchange(): return lax.ppermute(value, 'row', [(i, i ^ row_xor) for i in range(n_row)])]
  transfers between devices with their start and end apart: 40 -> 40, of which waited for: 32 -> 31; matrix products, arithmetic and copies ran while one was open for 0% -> 0% of each run, Pallas kernels for 6% -> 6%
where the time goes in v4:
time: 105 us
  waiting for transfers between devices  47.6 us (45%)
  starting transfers between devices  46.6 us (44%)
  Pallas kernels  9.25 us (9%)
  between operations  1.56 us (1%)
    ppermute x30, starting transfers between devices, exchange(): return lax.ppermute(value, 'row', [(i, i ^ row_xor) for i in range(n_row)])  36.1 us
    ppermute x30, waiting for transfers between devices, exchange(): return lax.ppermute(value, 'row', [(i, i ^ row_xor) for i in range(n_row)])  33.4 us
    ppermute x4, waiting for transfers between devices, exchange(): return lax.ppermute(value, ('row', 'col'), pairs)  9.71 us
    pallas_call x23, Pallas kernels, vmem_call(): pl.pallas_call(body, out_shape=[jax.ShapeDtypeStruct(shape, dtype) for sh...  9.25 us
    ppermute x6, starting transfers between devices, exchange(): return lax.ppermute(value, 'col', [(i, i ^ col_xor) for i in range(n_col)])  5.6 us
    ppermute x4, starting transfers between devices, exchange(): return lax.ppermute(value, ('row', 'col'), pairs)  4.92 us
    ppermute x6, waiting for transfers between devices, exchange(): return lax.ppermute(value, 'col', [(i, i ^ col_xor) for i in range(n_col)])  4.51 us
  transfers between devices with their start and end apart: 40, of which 31 were waited for; matrix products, arithmetic and copies ran while one was open for 0% of the time, Pallas kernels for 6%

profile of v4, /device:TPU:0, one launch (start us, length us, event | category | flops | bytes accessed | tf_op | source)
XLA Modules:
  0.0 105.2 jit_solution(16439757444072491899)
XLA Ops:
  0.6 5.1 %collective-permute-start.2 = (bf16[128,128]{1,0:T(8,128)(2,1)}, bf16[128,128]{1,0:T(8,128)(2,1)S(1)}, u32[]{:S(2)}, u32[]{:S(2)}) collective-permute-start(bf16[128,128]{1,0:T(8,128)(2,1)} %anchor_ref.1), channel_id=1, source_target_pairs={{0,24},{2,26},{4,28},{6,30},{8,16},{10,18},{12,20},{14,22},{16,8},... | collective-permute-start | bytes 98312 | tf_op jit(solution)/shard_map/ppermute | solution.py:62
  7.1 3.2 %shard_map.112 = (bf16[256,1024]{1,0:T(8,128)(2,1)S(1)}, bf16[256,1152]{1,0:T(8,128)(2,1)S(1)}, bf16[1024,256]{1,0:T(8,128)(2,1)S(1)}, bf16[256,128]{1,0:T(8,128)(2,1)S(1)}) custom-call(s32[2]{0:T(128)S(1)} %pad_add_fusion.where_ref, s32[1,1]{1,0:T(1,128)S(6)} %copy.13.count, s32[1,1,64]{2,1,0:T(1,128)} %refs_0_.1, s32[1,1,64]{2,1,0:T(1,128)} %refs_1_.1, ...), custom_call_target="tpu_custom_call" | custom-call | tf_op jit(solution)/shard_map/pallas_call | solution.py:20
  10.8 1.6 %collective-permute-start.3 = (bf16[512,128]{1,0:T(8,128)(2,1)S(1)}, bf16[512,128]{1,0:T(8,128)(2,1)S(1)}, u32[]{:S(2)}, u32[]{:S(2)}) collective-permute-start(bf16[512,128]{1,0:T(8,128)(2,1)S(1)} %pad_maximum_fusion), channel_id=1, source_target_pairs={{0,4},{2,6},{4,0},{6,2},{8,12},{10,14},{12,8},{14,10},{16,20},{18,... | collective-permute-start | bytes 393224 | tf_op jit(solution)/shard_map/ppermute | solution.py:62
  12.9 4.4 %collective-permute-done.3 = bf16[512,128]{1,0:T(8,128)(2,1)S(1)} collective-permute-done((bf16[512,128]{1,0:T(8,128)(2,1)S(1)}, bf16[512,128]{1,0:T(8,128)(2,1)S(1)}, u32[]{:S(2)}, u32[]{:S(2)}) %collective-permute-start.3) | collective-permute-done | bytes 131104 | tf_op jit(solution)/shard_map/ppermute | solution.py:62
  17.4 1.5 %collective-permute-done.4.far = bf16[1024,128]{1,0:T(8,128)(2,1)S(1)} collective-permute-done((bf16[1024,128]{1,0:T(8,128)(2,1)S(1)}, bf16[1024,128]{1,0:T(8,128)(2,1)S(1)}, u32[]{:S(2)}, u32[]{:S(2)}) %collective-permute-start.4) | collective-permute-done | bytes 262176 | tf_op jit(solution)/shard_map/ppermute | solution.py:62
  19.3 1.6 %collective-permute-start.5 = (bf16[128,128]{1,0:T(8,128)(2,1)S(1)}, bf16[128,128]{1,0:T(8,128)(2,1)S(1)}, u32[]{:S(2)}, u32[]{:S(2)}) collective-permute-start(bf16[128,128]{1,0:T(8,128)(2,1)S(1)} %get-tuple-element.57), channel_id=1, source_target_pairs={{0,1},{1,0},{2,3},{3,2},{4,5},{5,4},{6,7},{7,6},{8,9},{9,8},{10,11... | collective-permute-start | bytes 98312 | tf_op jit(solution)/shard_map/ppermute | solution.py:64
  20.9 2.4 %collective-permute-done.5.refs_1_ = bf16[128,128]{1,0:T(8,128)(2,1)S(1)} collective-permute-done((bf16[128,128]{1,0:T(8,128)(2,1)S(1)}, bf16[128,128]{1,0:T(8,128)(2,1)S(1)}, u32[]{:S(2)}, u32[]{:S(2)}) %collective-permute-start.5) | collective-permute-done | bytes 32800 | tf_op jit(solution)/shard_map/ppermute | solution.py:64
  23.5 3.1 %collective-permute-start.8 = (bf16[128,128]{1,0:T(8,128)(2,1)S(1)}, bf16[128,128]{1,0:T(8,128)(2,1)S(1)}, u32[]{:S(2)}, u32[]{:S(2)}) collective-permute-start(bf16[128,128]{1,0:T(8,128)(2,1)S(1)} %shard_map.114.z0), channel_id=1, source_target_pairs={{0,24},{2,26},{4,28},{6,30},{8,16},{10,18},{12,20},{14,22},{16,8},... | collective-permute-start | bytes 98312 | tf_op jit(solution)/shard_map/ppermute | solution.py:62
  26.6 1.4 %collective-permute-start.6 = (bf16[128,128]{1,0:T(8,128)(2,1)S(1)}, bf16[128,128]{1,0:T(8,128)(2,1)S(1)}, u32[]{:S(2)}, u32[]{:S(2)}) collective-permute-start(bf16[128,128]{1,0:T(8,128)(2,1)S(1)} %shard_map.114.z0), channel_id=1, source_target_pairs={{0,8},{2,10},{4,12},{6,14},{8,0},{10,2},{12,4},{14,6},{16,24},{18,... | collective-permute-start | bytes 98312 | tf_op jit(solution)/shard_map/ppermute | solution.py:62
  28.0 1.3 %collective-permute-done.8.z3 = bf16[128,128]{1,0:T(8,128)(2,1)S(1)} collective-permute-done((bf16[128,128]{1,0:T(8,128)(2,1)S(1)}, bf16[128,128]{1,0:T(8,128)(2,1)S(1)}, u32[]{:S(2)}, u32[]{:S(2)}) %collective-permute-start.8) | collective-permute-done | bytes 32800 | tf_op jit(solution)/shard_map/ppermute | solution.py:62
  29.3 2.1 %collective-permute-done.7.z2 = bf16[128,128]{1,0:T(8,128)(2,1)S(1)} collective-permute-done((bf16[128,128]{1,0:T(8,128)(2,1)S(1)}, bf16[128,128]{1,0:T(8,128)(2,1)S(1)}, u32[]{:S(2)}, u32[]{:S(2)}) %collective-permute-start.7) | collective-permute-done | bytes 32800 | tf_op jit(solution)/shard_map/ppermute | solution.py:62
  34.3 2.0 %collective-permute-start.12 = (bf16[128,128]{1,0:T(8,128)(2,1)S(1)}, bf16[128,128]{1,0:T(8,128)(2,1)S(1)}, u32[]{:S(2)}, u32[]{:S(2)}) collective-permute-start(bf16[128,128]{1,0:T(8,128)(2,1)S(1)} %get-tuple-element.60), channel_id=1, source_target_pairs={{0,4},{2,6},{4,0},{6,2},{8,12},{10,14},{12,8},{14,10},{16,20},{18,... | collective-permute-start | bytes 98312 | tf_op jit(solution)/shard_map/ppermute | solution.py:62
  38.2 2.9 %collective-permute-done.13.refs_3_ = bf16[128,128]{1,0:T(8,128)(2,1)S(1)} collective-permute-done((bf16[128,128]{1,0:T(8,128)(2,1)S(1)}, bf16[128,128]{1,0:T(8,128)(2,1)S(1)}, u32[]{:S(2)}, u32[]{:S(2)}) %collective-permute-start.13) | collective-permute-done | bytes 32800 | tf_op jit(solution)/shard_map/ppermute | solution.py:70
  41.7 1.9 %collective-permute-start.16 = (bf16[128,128]{1,0:T(8,128)(2,1)S(1)}, bf16[128,128]{1,0:T(8,128)(2,1)S(1)}, u32[]{:S(2)}, u32[]{:S(2)}) collective-permute-start(bf16[128,128]{1,0:T(8,128)(2,1)S(1)} %shard_map.117.z0), channel_id=1, source_target_pairs={{0,24},{2,26},{4,28},{6,30},{8,16},{10,18},{12,20},{14,22},{16,8},... | collective-permute-start | bytes 98312 | tf_op jit(solution)/shard_map/ppermute | solution.py:62
  43.7 2.3 %collective-permute-start.14 = (bf16[128,128]{1,0:T(8,128)(2,1)S(1)}, bf16[128,128]{1,0:T(8,128)(2,1)S(1)}, u32[]{:S(2)}, u32[]{:S(2)}) collective-permute-start(bf16[128,128]{1,0:T(8,128)(2,1)S(1)} %shard_map.117.z0), channel_id=1, source_target_pairs={{0,8},{2,10},{4,12},{6,14},{8,0},{10,2},{12,4},{14,6},{16,24},{18,... | collective-permute-start | bytes 98312 | tf_op jit(solution)/shard_map/ppermute | solution.py:62
  47.4 1.3 %collective-permute-done.15.z2 = bf16[128,128]{1,0:T(8,128)(2,1)S(1)} collective-permute-done((bf16[128,128]{1,0:T(8,128)(2,1)S(1)}, bf16[128,128]{1,0:T(8,128)(2,1)S(1)}, u32[]{:S(2)}, u32[]{:S(2)}) %collective-permute-start.15) | collective-permute-done | bytes 32800 | tf_op jit(solution)/shard_map/ppermute | solution.py:62
  51.6 1.7 %collective-permute-start.20 = (bf16[512,128]{1,0:T(8,128)(2,1)S(1)}, bf16[512,128]{1,0:T(8,128)(2,1)S(1)}, u32[]{:S(2)}, u32[]{:S(2)}) collective-permute-start(bf16[512,128]{1,0:T(8,128)(2,1)S(1)} %get-tuple-element.71), channel_id=1, source_target_pairs={{0,4},{2,6},{4,0},{6,2},{8,12},{10,14},{12,8},{14,10},{16,20},{18,... | collective-permute-start | bytes 393224 | tf_op jit(solution)/shard_map/ppermute | solution.py:62
  54.0 3.8 %collective-permute-done.21.refs_2_ = bf16[512,128]{1,0:T(8,128)(2,1)S(1)} collective-permute-done((bf16[512,128]{1,0:T(8,128)(2,1)S(1)}, bf16[512,128]{1,0:T(8,128)(2,1)S(1)}, u32[]{:S(2)}, u32[]{:S(2)}) %collective-permute-start.21) | collective-permute-done | bytes 131104 | tf_op jit(solution)/shard_map/ppermute | solution.py:70
  57.8 1.9 %collective-permute-done.20.refs_1_ = bf16[512,128]{1,0:T(8,128)(2,1)S(1)} collective-permute-done((bf16[512,128]{1,0:T(8,128)(2,1)S(1)}, bf16[512,128]{1,0:T(8,128)(2,1)S(1)}, u32[]{:S(2)}, u32[]{:S(2)}) %collective-permute-start.20) | collective-permute-done | bytes 131104 | tf_op jit(solution)/shard_map/ppermute | solution.py:62
  61.6 1.4 %collective-permute-start.23 = (bf16[128,128]{1,0:T(8,128)(2,1)S(1)}, bf16[128,128]{1,0:T(8,128)(2,1)S(1)}, u32[]{:S(2)}, u32[]{:S(2)}) collective-permute-start(bf16[128,128]{1,0:T(8,128)(2,1)S(1)} %get-tuple-element.79), channel_id=1, source_target_pairs={{0,8},{2,10},{4,12},{6,14},{8,0},{10,2},{12,4},{14,6},{16,24},{18,... | collective-permute-start | bytes 98312 | tf_op jit(solution)/shard_map/ppermute | solution.py:62
  64.3 1.8 %collective-permute-start.25 = (bf16[128,128]{1,0:T(8,128)(2,1)S(1)}, bf16[128,128]{1,0:T(8,128)(2,1)S(1)}, u32[]{:S(2)}, u32[]{:S(2)}) collective-permute-start(bf16[128,128]{1,0:T(8,128)(2,1)S(1)} %get-tuple-element.81), channel_id=1, source_target_pairs={{0,24},{2,26},{4,28},{6,30},{8,16},{10,18},{12,20},{14,22},{16,8},... | collective-permute-start | bytes 98312 | tf_op jit(solution)/shard_map/ppermute | solution.py:62
  66.1 2.1 %collective-permute-done.24.refs_1_ = bf16[128,128]{1,0:T(8,128)(2,1)S(1)} collective-permute-done((bf16[128,128]{1,0:T(8,128)(2,1)S(1)}, bf16[128,128]{1,0:T(8,128)(2,1)S(1)}, u32[]{:S(2)}, u32[]{:S(2)}) %collective-permute-start.24) | collective-permute-done | bytes 32800 | tf_op jit(solution)/shard_map/ppermute | solution.py:62
  68.2 1.8 %collective-permute-done.25.refs_2_ = bf16[128,128]{1,0:T(8,128)(2,1)S(1)} collective-permute-done((bf16[128,128]{1,0:T(8,128)(2,1)S(1)}, bf16[128,128]{1,0:T(8,128)(2,1)S(1)}, u32[]{:S(2)}, u32[]{:S(2)}) %collective-permute-start.25) | collective-permute-done | bytes 32800 | tf_op jit(solution)/shard_map/ppermute | solution.py:62
  70.2 1.8 %collective-permute-start.28 = (bf16[128,128]{1,0:T(8,128)(2,1)S(1)}, bf16[128,128]{1,0:T(8,128)(2,1)S(1)}, u32[]{:S(2)}, u32[]{:S(2)}) collective-permute-start(bf16[128,128]{1,0:T(8,128)(2,1)S(1)} %shard_map.126.refs_0_), channel_id=1, source_target_pairs={{0,5},{1,4},{2,7},{3,6},{4,1},{5,0},{6,3},{7,2},{8,13},{9,12},{10,... | collective-permute-start | bytes 98312 | tf_op jit(solution)/shard_map/ppermute | solution.py:70
  78.4 2.1 %collective-permute-start.31 = (bf16[128,128]{1,0:T(8,128)(2,1)S(1)}, bf16[128,128]{1,0:T(8,128)(2,1)S(1)}, u32[]{:S(2)}, u32[]{:S(2)}) collective-permute-start(bf16[128,128]{1,0:T(8,128)(2,1)S(1)} %get-tuple-element.85), channel_id=1, source_target_pairs={{0,16},{2,18},{4,20},{6,22},{8,24},{10,26},{12,28},{14,30},{16,0},... | collective-permute-start | bytes 98312 | tf_op jit(solution)/shard_map/ppermute | solution.py:62
  80.4 2.3 %collective-permute-start.32 = (bf16[128,128]{1,0:T(8,128)(2,1)S(1)}, bf16[128,128]{1,0:T(8,128)(2,1)S(1)}, u32[]{:S(2)}, u32[]{:S(2)}) collective-permute-start(bf16[128,128]{1,0:T(8,128)(2,1)S(1)} %get-tuple-element.86), channel_id=1, source_target_pairs={{0,24},{2,26},{4,28},{6,30},{8,16},{10,18},{12,20},{14,22},{16,8},... | collective-permute-start | bytes 98312 | tf_op jit(solution)/shard_map/ppermute | solution.py:62
  83.3 2.9 %collective-permute-done.32.refs_2_ = bf16[128,128]{1,0:T(8,128)(2,1)S(1)} collective-permute-done((bf16[128,128]{1,0:T(8,128)(2,1)S(1)}, bf16[128,128]{1,0:T(8,128)(2,1)S(1)}, u32[]{:S(2)}, u32[]{:S(2)}) %collective-permute-start.32) | collective-permute-done | bytes 32800 | tf_op jit(solution)/shard_map/ppermute | solution.py:62
  86.5 1.6 %collective-permute-start.35 = (bf16[256,128]{1,0:T(8,128)(2,1)S(1)}, bf16[256,128]{1,0:T(8,128)(2,1)S(1)}, u32[]{:S(2)}, u32[]{:S(2)}) collective-permute-start(bf16[256,128]{1,0:T(8,128)(2,1)S(1)} %shard_map.130.refs_0_), channel_id=1, source_target_pairs={{0,5},{1,4},{2,7},{3,6},{4,1},{5,0},{6,3},{7,2},{8,13},{9,12},{10,... | collective-permute-start | bytes 196616 | tf_op jit(solution)/shard_map/ppermute | solution.py:70
  90.1 1.7 %collective-permute-done.35.refs_3_ = bf16[256,128]{1,0:T(8,128)(2,1)S(1)} collective-permute-done((bf16[256,128]{1,0:T(8,128)(2,1)S(1)}, bf16[256,128]{1,0:T(8,128)(2,1)S(1)}, u32[]{:S(2)}, u32[]{:S(2)}) %collective-permute-start.35) | collective-permute-done | bytes 65568 | tf_op jit(solution)/shard_map/ppermute | solution.py:70
  95.6 2.6 %collective-permute-start.38 = (bf16[256,128]{1,0:T(8,128)(2,1)S(1)}, bf16[256,128]{1,0:T(8,128)(2,1)S(1)}, u32[]{:S(2)}, u32[]{:S(2)}) collective-permute-start(bf16[256,128]{1,0:T(8,128)(2,1)S(1)} %get-tuple-element.92), channel_id=1, source_target_pairs={{0,16},{2,18},{4,20},{6,22},{8,24},{10,26},{12,28},{14,30},{16,0},... | collective-permute-start | bytes 196616 | tf_op jit(solution)/shard_map/ppermute | solution.py:62
  98.2 1.8 %collective-permute-start.39 = (bf16[256,128]{1,0:T(8,128)(2,1)S(1)}, bf16[256,128]{1,0:T(8,128)(2,1)S(1)}, u32[]{:S(2)}, u32[]{:S(2)}) collective-permute-start(bf16[256,128]{1,0:T(8,128)(2,1)S(1)} %get-tuple-element.93), channel_id=1, source_target_pairs={{0,24},{2,26},{4,28},{6,30},{8,16},{10,18},{12,20},{14,22},{16,8},... | collective-permute-start | bytes 196616 | tf_op jit(solution)/shard_map/ppermute | solution.py:62
  100.8 2.9 %collective-permute-done.38.refs_1_ = bf16[256,128]{1,0:T(8,128)(2,1)S(1)} collective-permute-done((bf16[256,128]{1,0:T(8,128)(2,1)S(1)}, bf16[256,128]{1,0:T(8,128)(2,1)S(1)}, u32[]{:S(2)}, u32[]{:S(2)}) %collective-permute-start.38) | collective-permute-done | bytes 65568 | tf_op jit(solution)/shard_map/ppermute | solution.py:62
  (83 shorter events, 31.5 us)
Async XLA Ops:
  0.6 9.7 %collective-permute-start.2 = (bf16[128,128]{1,0:T(8,128)(2,1)}, bf16[128,128]{1,0:T(8,128)(2,1)S(1)}, u32[]{:S(2)}, u32[]{:S(2)}) collective-permute-start(bf16[128,128]{1,0:T(8,128)(2,1)} %anchor_ref.1), channel_id=1, source_target_pairs={{0,24},{2,26},{4,28},{6,30},{8,16},{10,18},{12,20},{14,22},{16,8},... | collective-permute-start | bytes 98312 | tf_op jit(solution)/shard_map/ppermute | solution.py:62
  5.8 5.0 %collective-permute-start.1 = (bf16[128,128]{1,0:T(8,128)(2,1)}, bf16[128,128]{1,0:T(8,128)(2,1)S(1)}, u32[]{:S(2)}, u32[]{:S(2)}) collective-permute-start(bf16[128,128]{1,0:T(8,128)(2,1)} %anchor_ref.1), channel_id=1, source_target_pairs={{0,16},{2,18},{4,20},{6,22},{8,24},{10,26},{12,28},{14,30},{16,0},... | collective-permute-start | bytes 98312 | tf_op jit(solution)/shard_map/ppermute | solution.py:62
  5.8 5.0 %collective-permute-start = (bf16[128,128]{1,0:T(8,128)(2,1)}, bf16[128,128]{1,0:T(8,128)(2,1)S(1)}, u32[]{:S(2)}, u32[]{:S(2)}) collective-permute-start(bf16[128,128]{1,0:T(8,128)(2,1)} %anchor_ref.1), channel_id=1, source_target_pairs={{0,8},{2,10},{4,12},{6,14},{8,0},{10,2},{12,4},{14,6},{16,24},{18,... | collective-permute-start | bytes 98312 | tf_op jit(solution)/shard_map/ppermute | solution.py:62
  10.8 6.5 %collective-permute-start.3 = (bf16[512,128]{1,0:T(8,128)(2,1)S(1)}, bf16[512,128]{1,0:T(8,128)(2,1)S(1)}, u32[]{:S(2)}, u32[]{:S(2)}) collective-permute-start(bf16[512,128]{1,0:T(8,128)(2,1)S(1)} %pad_maximum_fusion), channel_id=1, source_target_pairs={{0,4},{2,6},{4,0},{6,2},{8,12},{10,14},{12,8},{14,10},{16,20},{18,... | collective-permute-start | bytes 393224 | tf_op jit(solution)/shard_map/ppermute | solution.py:62
  12.4 19.1 %collective-permute-start.9 = (bf16[256,1152]{1,0:T(8,128)(2,1)S(1)}, bf16[256,1152]{1,0:T(8,128)(2,1)S(1)}, u32[]{:S(2)}, u32[]{:S(2)}) collective-permute-start(bf16[256,1152]{1,0:T(8,128)(2,1)S(1)} %get-tuple-element.55.refs_1_), channel_id=1, source_target_pairs={{0,4},{2,6},{4,0},{6,2},{8,12},{10,14},{12,8},{14,10},{16,20},{18,... | collective-permute-start | bytes 1769480 | tf_op jit(solution)/shard_map/ppermute | solution.py:62
  19.3 4.0 %collective-permute-start.5 = (bf16[128,128]{1,0:T(8,128)(2,1)S(1)}, bf16[128,128]{1,0:T(8,128)(2,1)S(1)}, u32[]{:S(2)}, u32[]{:S(2)}) collective-permute-start(bf16[128,128]{1,0:T(8,128)(2,1)S(1)} %get-tuple-element.57), channel_id=1, source_target_pairs={{0,1},{1,0},{2,3},{3,2},{4,5},{5,4},{6,7},{7,6},{8,9},{9,8},{10,11... | collective-permute-start | bytes 98312 | tf_op jit(solution)/shard_map/ppermute | solution.py:64
  23.5 5.8 %collective-permute-start.8 = (bf16[128,128]{1,0:T(8,128)(2,1)S(1)}, bf16[128,128]{1,0:T(8,128)(2,1)S(1)}, u32[]{:S(2)}, u32[]{:S(2)}) collective-permute-start(bf16[128,128]{1,0:T(8,128)(2,1)S(1)} %shard_map.114.z0), channel_id=1, source_target_pairs={{0,24},{2,26},{4,28},{6,30},{8,16},{10,18},{12,20},{14,22},{16,8},... | collective-permute-start | bytes 98312 | tf_op jit(solution)/shard_map/ppermute | solution.py:62
  26.6 4.8 %collective-permute-start.7 = (bf16[128,128]{1,0:T(8,128)(2,1)S(1)}, bf16[128,128]{1,0:T(8,128)(2,1)S(1)}, u32[]{:S(2)}, u32[]{:S(2)}) collective-permute-start(bf16[128,128]{1,0:T(8,128)(2,1)S(1)} %shard_map.114.z0), channel_id=1, source_target_pairs={{0,16},{2,18},{4,20},{6,22},{8,24},{10,26},{12,28},{14,30},{16,0},... | collective-permute-start | bytes 98312 | tf_op jit(solution)/shard_map/ppermute | solution.py:62
  26.6 4.8 %collective-permute-start.6 = (bf16[128,128]{1,0:T(8,128)(2,1)S(1)}, bf16[128,128]{1,0:T(8,128)(2,1)S(1)}, u32[]{:S(2)}, u32[]{:S(2)}) collective-permute-start(bf16[128,128]{1,0:T(8,128)(2,1)S(1)} %shard_map.114.z0), channel_id=1, source_target_pairs={{0,8},{2,10},{4,12},{6,14},{8,0},{10,2},{12,4},{14,6},{16,24},{18,... | collective-permute-start | bytes 98312 | tf_op jit(solution)/shard_map/ppermute | solution.py:62
  33.1 4.0 %collective-permute-start.11 = (bf16[128,128]{1,0:T(8,128)(2,1)S(1)}, bf16[128,128]{1,0:T(8,128)(2,1)S(1)}, u32[]{:S(2)}, u32[]{:S(2)}) collective-permute-start(bf16[128,128]{1,0:T(8,128)(2,1)S(1)} %get-tuple-element.59), channel_id=1, source_target_pairs={{0,1},{1,0},{2,3},{3,2},{4,5},{5,4},{6,7},{7,6},{8,9},{9,8},{10,11... | collective-permute-start | bytes 98312 | tf_op jit(solution)/shard_map/ppermute | solution.py:64
  34.3 3.9 %collective-permute-start.12 = (bf16[128,128]{1,0:T(8,128)(2,1)S(1)}, bf16[128,128]{1,0:T(8,128)(2,1)S(1)}, u32[]{:S(2)}, u32[]{:S(2)}) collective-permute-start(bf16[128,128]{1,0:T(8,128)(2,1)S(1)} %get-tuple-element.60), channel_id=1, source_target_pairs={{0,4},{2,6},{4,0},{6,2},{8,12},{10,14},{12,8},{14,10},{16,20},{18,... | collective-permute-start | bytes 98312 | tf_op jit(solution)/shard_map/ppermute | solution.py:62
  36.3 4.8 %collective-permute-start.13 = (bf16[128,128]{1,0:T(8,128)(2,1)S(1)}, bf16[128,128]{1,0:T(8,128)(2,1)S(1)}, u32[]{:S(2)}, u32[]{:S(2)}) collective-permute-start(bf16[128,128]{1,0:T(8,128)(2,1)S(1)} %get-tuple-element.61), channel_id=1, source_target_pairs={{0,5},{1,4},{2,7},{3,6},{4,1},{5,0},{6,3},{7,2},{8,13},{9,12},{10,... | collective-permute-start | bytes 98312 | tf_op jit(solution)/shard_map/ppermute | solution.py:70
  41.3 7.4 %collective-permute-start.17 = (bf16[512,128]{1,0:T(8,128)(2,1)S(1)}, bf16[512,128]{1,0:T(8,128)(2,1)S(1)}, u32[]{:S(2)}, u32[]{:S(2)}) collective-permute-start(bf16[512,128]{1,0:T(8,128)(2,1)S(1)} %get-tuple-element.72.refs_3_), channel_id=1, source_target_pairs={{0,1},{1,0},{2,3},{3,2},{4,5},{5,4},{6,7},{7,6},{8,9},{9,8},{10,11... | collective-permute-start | bytes 393224 | tf_op jit(solution)/shard_map/ppermute | solution.py:64
  41.7 5.7 %collective-permute-start.16 = (bf16[128,128]{1,0:T(8,128)(2,1)S(1)}, bf16[128,128]{1,0:T(8,128)(2,1)S(1)}, u32[]{:S(2)}, u32[]{:S(2)}) collective-permute-start(bf16[128,128]{1,0:T(8,128)(2,1)S(1)} %shard_map.117.z0), channel_id=1, source_target_pairs={{0,24},{2,26},{4,28},{6,30},{8,16},{10,18},{12,20},{14,22},{16,8},... | collective-permute-start | bytes 98312 | tf_op jit(solution)/shard_map/ppermute | solution.py:62
  43.5 5.2 %collective-permute-start.15 = (bf16[128,128]{1,0:T(8,128)(2,1)S(1)}, bf16[128,128]{1,0:T(8,128)(2,1)S(1)}, u32[]{:S(2)}, u32[]{:S(2)}) collective-permute-start(bf16[128,128]{1,0:T(8,128)(2,1)S(1)} %shard_map.117.z0), channel_id=1, source_target_pairs={{0,16},{2,18},{4,20},{6,22},{8,24},{10,26},{12,28},{14,30},{16,0},... | collective-permute-start | bytes 98312 | tf_op jit(solution)/shard_map/ppermute | solution.py:62
  43.7 5.0 %collective-permute-start.14 = (bf16[128,128]{1,0:T(8,128)(2,1)S(1)}, bf16[128,128]{1,0:T(8,128)(2,1)S(1)}, u32[]{:S(2)}, u32[]{:S(2)}) collective-permute-start(bf16[128,128]{1,0:T(8,128)(2,1)S(1)} %shard_map.117.z0), channel_id=1, source_target_pairs={{0,8},{2,10},{4,12},{6,14},{8,0},{10,2},{12,4},{14,6},{16,24},{18,... | collective-permute-start | bytes 98312 | tf_op jit(solution)/shard_map/ppermute | solution.py:62
  50.4 7.4 %collective-permute-start.21 = (bf16[512,128]{1,0:T(8,128)(2,1)S(1)}, bf16[512,128]{1,0:T(8,128)(2,1)S(1)}, u32[]{:S(2)}, u32[]{:S(2)}) collective-permute-start(bf16[512,128]{1,0:T(8,128)(2,1)S(1)} %get-tuple-element.71), channel_id=1, source_target_pairs={{0,5},{1,4},{2,7},{3,6},{4,1},{5,0},{6,3},{7,2},{8,13},{9,12},{10,... | collective-permute-start | bytes 393224 | tf_op jit(solution)/shard_map/ppermute | solution.py:70
  51.6 8.1 %collective-permute-start.20 = (bf16[512,128]{1,0:T(8,128)(2,1)S(1)}, bf16[512,128]{1,0:T(8,128)(2,1)S(1)}, u32[]{:S(2)}, u32[]{:S(2)}) collective-permute-start(bf16[512,128]{1,0:T(8,128)(2,1)S(1)} %get-tuple-element.71), channel_id=1, source_target_pairs={{0,4},{2,6},{4,0},{6,2},{8,12},{10,14},{12,8},{14,10},{16,20},{18,... | collective-permute-start | bytes 393224 | tf_op jit(solution)/shard_map/ppermute | solution.py:62
  53.3 6.4 %collective-permute-start.19 = (bf16[512,128]{1,0:T(8,128)(2,1)S(1)}, bf16[512,128]{1,0:T(8,128)(2,1)S(1)}, u32[]{:S(2)}, u32[]{:S(2)}) collective-permute-start(bf16[512,128]{1,0:T(8,128)(2,1)S(1)} %get-tuple-element.71), channel_id=1, source_target_pairs={{0,1},{1,0},{2,3},{3,2},{4,5},{5,4},{6,7},{7,6},{8,9},{9,8},{10,11... | collective-permute-start | bytes 393224 | tf_op jit(solution)/shard_map/ppermute | solution.py:64
  61.6 4.5 %collective-permute-start.23 = (bf16[128,128]{1,0:T(8,128)(2,1)S(1)}, bf16[128,128]{1,0:T(8,128)(2,1)S(1)}, u32[]{:S(2)}, u32[]{:S(2)}) collective-permute-start(bf16[128,128]{1,0:T(8,128)(2,1)S(1)} %get-tuple-element.79), channel_id=1, source_target_pairs={{0,8},{2,10},{4,12},{6,14},{8,0},{10,2},{12,4},{14,6},{16,24},{18,... | collective-permute-start | bytes 98312 | tf_op jit(solution)/shard_map/ppermute | solution.py:62
  63.1 5.2 %collective-permute-start.24 = (bf16[128,128]{1,0:T(8,128)(2,1)S(1)}, bf16[128,128]{1,0:T(8,128)(2,1)S(1)}, u32[]{:S(2)}, u32[]{:S(2)}) collective-permute-start(bf16[128,128]{1,0:T(8,128)(2,1)S(1)} %get-tuple-element.80), channel_id=1, source_target_pairs={{0,16},{2,18},{4,20},{6,22},{8,24},{10,26},{12,28},{14,30},{16,0},... | collective-permute-start | bytes 98312 | tf_op jit(solution)/shard_map/ppermute | solution.py:62
  64.3 5.7 %collective-permute-start.25 = (bf16[128,128]{1,0:T(8,128)(2,1)S(1)}, bf16[128,128]{1,0:T(8,128)(2,1)S(1)}, u32[]{:S(2)}, u32[]{:S(2)}) collective-permute-start(bf16[128,128]{1,0:T(8,128)(2,1)S(1)} %get-tuple-element.81), channel_id=1, source_target_pairs={{0,24},{2,26},{4,28},{6,30},{8,16},{10,18},{12,20},{14,22},{16,8},... | collective-permute-start | bytes 98312 | tf_op jit(solution)/shard_map/ppermute | solution.py:62
  70.2 4.9 %collective-permute-start.28 = (bf16[128,128]{1,0:T(8,128)(2,1)S(1)}, bf16[128,128]{1,0:T(8,128)(2,1)S(1)}, u32[]{:S(2)}, u32[]{:S(2)}) collective-permute-start(bf16[128,128]{1,0:T(8,128)(2,1)S(1)} %shard_map.126.refs_0_), channel_id=1, source_target_pairs={{0,5},{1,4},{2,7},{3,6},{4,1},{5,0},{6,3},{7,2},{8,13},{9,12},{10,... | collective-permute-start | bytes 98312 | tf_op jit(solution)/shard_map/ppermute | solution.py:70
  78.3 4.5 %collective-permute-start.30 = (bf16[128,128]{1,0:T(8,128)(2,1)S(1)}, bf16[128,128]{1,0:T(8,128)(2,1)S(1)}, u32[]{:S(2)}, u32[]{:S(2)}) collective-permute-start(bf16[128,128]{1,0:T(8,128)(2,1)S(1)} %get-tuple-element.84), channel_id=1, source_target_pairs={{0,8},{2,10},{4,12},{6,14},{8,0},{10,2},{12,4},{14,6},{16,24},{18,... | collective-permute-start | bytes 98312 | tf_op jit(solution)/shard_map/ppermute | solution.py:62
  78.4 4.9 %collective-permute-start.31 = (bf16[128,128]{1,0:T(8,128)(2,1)S(1)}, bf16[128,128]{1,0:T(8,128)(2,1)S(1)}, u32[]{:S(2)}, u32[]{:S(2)}) collective-permute-start(bf16[128,128]{1,0:T(8,128)(2,1)S(1)} %get-tuple-element.85), channel_id=1, source_target_pairs={{0,16},{2,18},{4,20},{6,22},{8,24},{10,26},{12,28},{14,30},{16,0},... | collective-permute-start | bytes 98312 | tf_op jit(solution)/shard_map/ppermute | solution.py:62
  80.4 5.7 %collective-permute-start.32 = (bf16[128,128]{1,0:T(8,128)(2,1)S(1)}, bf16[128,128]{1,0:T(8,128)(2,1)S(1)}, u32[]{:S(2)}, u32[]{:S(2)}) collective-permute-start(bf16[128,128]{1,0:T(8,128)(2,1)S(1)} %get-tuple-element.86), channel_id=1, source_target_pairs={{0,24},{2,26},{4,28},{6,30},{8,16},{10,18},{12,20},{14,22},{16,8},... | collective-permute-start | bytes 98312 | tf_op jit(solution)/shard_map/ppermute | solution.py:62
  86.5 5.2 %collective-permute-start.35 = (bf16[256,128]{1,0:T(8,128)(2,1)S(1)}, bf16[256,128]{1,0:T(8,128)(2,1)S(1)}, u32[]{:S(2)}, u32[]{:S(2)}) collective-permute-start(bf16[256,128]{1,0:T(8,128)(2,1)S(1)} %shard_map.130.refs_0_), channel_id=1, source_target_pairs={{0,5},{1,4},{2,7},{3,6},{4,1},{5,0},{6,3},{7,2},{8,13},{9,12},{10,... | collective-permute-start | bytes 196616 | tf_op jit(solution)/shard_map/ppermute | solution.py:70
  88.1 4.4 %collective-permute-start.34 = (bf16[256,128]{1,0:T(8,128)(2,1)S(1)}, bf16[256,128]{1,0:T(8,128)(2,1)S(1)}, u32[]{:S(2)}, u32[]{:S(2)}) collective-permute-start(bf16[256,128]{1,0:T(8,128)(2,1)S(1)} %shard_map.130.refs_0_), channel_id=1, source_target_pairs={{0,4},{2,6},{4,0},{6,2},{8,12},{10,14},{12,8},{14,10},{16,20},{18,... | collective-permute-start | bytes 196616 | tf_op jit(solution)/shard_map/ppermute | solution.py:62
  89.4 4.3 %collective-permute-start.33 = (bf16[256,128]{1,0:T(8,128)(2,1)S(1)}, bf16[256,128]{1,0:T(8,128)(2,1)S(1)}, u32[]{:S(2)}, u32[]{:S(2)}) collective-permute-start(bf16[256,128]{1,0:T(8,128)(2,1)S(1)} %shard_map.130.refs_0_), channel_id=1, source_target_pairs={{0,1},{1,0},{2,3},{3,2},{4,5},{5,4},{6,7},{7,6},{8,9},{9,8},{10,11... | collective-permute-start | bytes 196616 | tf_op jit(solution)/shard_map/ppermute | solution.py:64
  95.5 5.2 %collective-permute-start.37 = (bf16[256,128]{1,0:T(8,128)(2,1)S(1)}, bf16[256,128]{1,0:T(8,128)(2,1)S(1)}, u32[]{:S(2)}, u32[]{:S(2)}) collective-permute-start(bf16[256,128]{1,0:T(8,128)(2,1)S(1)} %get-tuple-element.91), channel_id=1, source_target_pairs={{0,8},{2,10},{4,12},{6,14},{8,0},{10,2},{12,4},{14,6},{16,24},{18,... | collective-permute-start | bytes 196616 | tf_op jit(solution)/shard_map/ppermute | solution.py:62
  95.6 8.0 %collective-permute-start.38 = (bf16[256,128]{1,0:T(8,128)(2,1)S(1)}, bf16[256,128]{1,0:T(8,128)(2,1)S(1)}, u32[]{:S(2)}, u32[]{:S(2)}) collective-permute-start(bf16[256,128]{1,0:T(8,128)(2,1)S(1)} %get-tuple-element.92), channel_id=1, source_target_pairs={{0,16},{2,18},{4,20},{6,22},{8,24},{10,26},{12,28},{14,30},{16,0},... | collective-permute-start | bytes 196616 | tf_op jit(solution)/shard_map/ppermute | solution.py:62
  98.2 6.2 %collective-permute-start.39 = (bf16[256,128]{1,0:T(8,128)(2,1)S(1)}, bf16[256,128]{1,0:T(8,128)(2,1)S(1)}, u32[]{:S(2)}, u32[]{:S(2)}) collective-permute-start(bf16[256,128]{1,0:T(8,128)(2,1)S(1)} %get-tuple-element.93), channel_id=1, source_target_pairs={{0,24},{2,26},{4,28},{6,30},{8,16},{10,18},{12,20},{14,22},{16,8},... | collective-permute-start | bytes 196616 | tf_op jit(solution)/shard_map/ppermute | solution.py:62
  (11 other events, 59.2 us)

commit v5 on v4

--- a/solution.py
+++ b/solution.py
@@ -147,16 +147,23 @@
         ],
     )
 
-    def first_partial(near, far, *refs):
+    def own_product(block_rows, a, side):
+        total = None
+        for y in range(n_y):
+            part = a[y][:, side * line_rows : (side + 1) * line_rows]
+            rows = block_rows[y * line_rows : (y + 1) * line_rows]
+            product = jnp.dot(part, rows, preferred_element_type=F32)
+            total = product if total is None else total + product
+        return total
+
+    def first_near(near, *refs):
+        refs[n_y][...] = own_product(near, refs[:n_y], 0)
+
+    def first_far(held, far, *refs):
         a, outs = refs[:n_y], refs[n_y:]
-        total = jnp.zeros((n_col * TILE, hidden), F32)
-        for y in range(n_y):
-            rows = slice(y * line_rows, (y + 1) * line_rows)
-            total += jnp.dot(a[y][:, :line_rows], near[rows], preferred_element_type=F32)
-            total += jnp.dot(a[y][:, line_rows : 2 * line_rows], far[rows], preferred_element_type=F32)
-        outs[0][...] = total[:TILE]
-        for x in range(1, n_col):
-            outs[x][...] = total[x * TILE : (x + 1) * TILE].astype(BF16)
+        total = held[...] + own_product(far, a, 1)
+        for x in range(n_col):
+            outs[x][...] = total[x * TILE : (x + 1) * TILE].astype(outs[x].dtype)
 
     n_square = len(square)
     square_rows = n_square * TILE
@@ -172,13 +179,15 @@
         rows = slice(y * n_col * TILE, (y + 1) * n_col * TILE)
         return held[rows] + jnp.dot(a[y][:, line_rows : 2 * line_rows], far[...], preferred_element_type=F32)
 
-    def forward_far(held, far, *refs):
+    def forward_far(held, far, fixed_ref, *refs):
         a, outs = refs[:n_y], refs[n_y:]
         for y in range(n_y):
             total = far_product(held, far, a, y)
             for x in range(n_col):
                 out = outs[y * n_col + x]
-                out[...] = total[x * TILE : (x + 1) * TILE].astype(out.dtype)
+                out[:TILE] = total[x * TILE : (x + 1) * TILE].astype(out.dtype)
+                if x > 0:
+                    out[TILE:] = fixed_ref[...]
 
     def forward_far_all(held, far, *refs):
         a, (kept, sent) = refs[:n_y], refs[n_y:]
@@ -191,7 +200,7 @@
     def advance(beta, peers):
         def body(*refs):
             sums, (w, anchor_ref, inject, out) = refs[:peers], refs[peers:]
-            u = tree_sum([s[...].astype(F32) for s in sums])
+            u = tree_sum([s[:TILE].astype(F32) for s in sums])
             bent = jnp.tanh(split_dot(u, w[...], ((1,), (0,))) + inject[...].astype(F32))
             out[...] = (beta * anchor_ref[...].astype(F32) + (1.0 - beta) * bent).astype(BF16)
 
@@ -199,8 +208,12 @@
 
     def meet(kept, *refs):
         got, refs = refs[: n_square - 1], refs[n_square - 1 :]
-        fixed_refs, (w, bent_out, slope_out, u_out, h_out) = refs[:n_col], refs[n_col:]
-        fixed = [fixed_refs[x].at[2 * y * TILE : 2 * (y + 1) * TILE] for y, x in square]
+        by_y, by_x, (w, bent_out, slope_out, u_out, h_out) = refs[0], refs[1 : -5], refs[-5:]
+        by_x = iter(by_x)
+        fixed = [
+            by_y.at[2 * y * TILE : 2 * (y + 1) * TILE] if x == 0 else next(by_x).at[TILE : 3 * TILE]
+            for y, x in square
+        ]
         u = jnp.concatenate(
             [
                 tree_sum(
@@ -237,12 +250,7 @@
     state = anchor
     for step in range(ITERS):
         beta = 1.0 / (step + 2.0)
-        if step == 2:
-            state, fixed_y = lax.optimization_barrier((state, fixed_y))
         line = [state] + along_line([state] * (LINE - 1))
-        if step == 2:
-            fixed = [fixed_y] + [exchange(fixed_y, 0, x) for x in range(1, n_col)]
-            line, fixed = lax.optimization_barrier((line, fixed))
         if step == 0:
             joined = jnp.concatenate(line, axis=0)
             joined, *parts, turned = lax.optimization_barrier((joined, *parts, turned))
@@ -252,8 +260,9 @@
                 bit *= 2
             sent = parts[1:]
             far = exchange(joined, 1)
+            (held,) = vmem_call(first_near, [((n_col * TILE, hidden), F32)], joined, *parts)
             outs = [(block, F32)] + [(block, BF16)] * (n_col - 1)
-            mine, *sends = vmem_call(first_partial, outs, joined, far, *parts)
+            mine, *sends = vmem_call(first_far, outs, held, far, *parts)
             parts = [parts[0]] + [exchange(p, 2 * (i + 1)) for i, p in enumerate(sent)]
             got = [exchange(v, 0, x + 1) for x, v in enumerate(sends)]
         else:
@@ -264,12 +273,13 @@
                 kept, sent = vmem_call(forward_far_all, outs, held, far, *parts)
                 got = to_square([sent] * (n_square - 1))
                 bent, slope, mixed, h_all = vmem_call(
-                    meet, [(block, F32)] * 3 + [((square_rows, hidden), BF16)], kept, *got, *fixed, weight
+                    meet, [(block, F32)] * 3 + [((square_rows, hidden), BF16)], kept, *got, fixed_y, *fixed_x, weight
                 )
                 break
-            outs = [(block, F32)] + [(block, BF16)] * (n_square - 1)
-            mine, *sends = vmem_call(forward_far, outs, held, far, *parts)
+            outs = [(block, F32)] + [((TILE if x == 0 else 3 * TILE, hidden), BF16) for y, x in square[1:]]
+            mine, *sends = vmem_call(forward_far, outs, held, far, fixed, *parts)
             got = to_square(sends)
+            fixed_x = [v for (y, x), v in zip(square[1:], got) if x > 0]
         if step == 1:
             *more, fixed_y = vmem_call(
                 turn,
@@ -282,10 +292,13 @@
             advance(beta, 1 + len(got)), [(block, BF16)], mine, *got, weight, anchor, injection
         )
 
-    def finish(bent_ref, anchor_ref, out):
+    def finish(bent_ref, anchor_ref, u, out, high, low):
         out[...] = (beta * anchor_ref[...].astype(F32) + (1.0 - beta) * bent_ref[...]).astype(BF16)
-
-    (state,) = vmem_call(finish, [(block, BF16)], bent, anchor)
+        high[...], low[...] = halves(u[...].T)
+
+    state, *mixed = vmem_call(
+        finish, [(block, BF16)] + [((hidden, TILE), BF16)] * 2, bent, anchor, mixed
+    )
 
     def line_product(h, a_t, rows):
         total = None
@@ -352,7 +365,9 @@
                 h = (g * slope_ref[...]).astype(BF16)
                 out[:TILE] = h
                 if ride:
-                    out[TILE:] = split_dot(rest[3][...], h, ((0,), (0,))).astype(BF16)
+                    term = jnp.dot(rest[3][...], h, preferred_element_type=F32)
+                    term += jnp.dot(rest[4][...], h, preferred_element_type=F32)
+                    out[TILE:] = term.astype(BF16)
 
         return body
 
@@ -383,7 +398,7 @@
         if last:
             *sends, total = sends
         got = along_line(sends)
-        inputs = (held, *got, fixed[0], weight, slope)
+        inputs = (held, *got, fixed, weight, slope)
         if last:
             adjoint, weight_grad = vmem_call(
                 pull(True, False), [(block, F32), ((hidden, hidden), F32)], *inputs, total
@@ -391,7 +406,7 @@
         else:
             rows = TILE + (hidden if ride else 0)
             (scaled,) = vmem_call(
-                pull(False, ride), [((rows, hidden), BF16)], *inputs, *([mixed] if ride else [])
+                pull(False, ride), [((rows, hidden), BF16)], *inputs, *(mixed if ride else [])
             )
     return state, adjoint, weight_grad
 

time: 105 us -> 105 us (level)
    ppermute x30, waiting for transfers between devices: 33.4 us -> 37.6 us  [exchange(): return lax.ppermute(value, 'row', [(i, i ^ row_xor) for i in range(n_row)])]
    ppermute x4, waiting for transfers between devices: 9.71 us -> 6.19 us  [exchange(): return lax.ppermute(value, ('row', 'col'), pairs)]
    ppermute x30, starting transfers between devices: 36.1 us -> 34.4 us  [exchange(): return lax.ppermute(value, 'row', [(i, i ^ row_xor) for i in range(n_row)])]
    ppermute x6 -> x5, starting transfers between devices: 5.6 us -> 6.33 us  [exchange(): return lax.ppermute(value, 'col', [(i, i ^ col_xor) for i in range(n_col)])]
    ppermute x6 -> x5, waiting for transfers between devices: 4.51 us -> 4.12 us  [exchange(): return lax.ppermute(value, 'col', [(i, i ^ col_xor) for i in range(n_col)])]
    pallas_call x23 -> x24, Pallas kernels: 9.25 us -> 9.22 us  [vmem_call(): pl.pallas_call(body, out_shape=[jax.ShapeDtypeStruct(shape, dtype) for sh...]
  transfers between devices with their start and end apart: 40 -> 39, of which waited for: 31 -> 29; matrix products, arithmetic and copies ran while one was open for 0% -> 0% of each run, Pallas kernels for 6% -> 6%
where the time goes in v5:
time: 105 us
  waiting for transfers between devices  47.9 us (46%)
  starting transfers between devices  46.3 us (44%)
  Pallas kernels  9.22 us (9%)
  between operations  1.56 us (1%)
    ppermute x30, waiting for transfers between devices, exchange(): return lax.ppermute(value, 'row', [(i, i ^ row_xor) for i in range(n_row)])  37.6 us
    ppermute x30, starting transfers between devices, exchange(): return lax.ppermute(value, 'row', [(i, i ^ row_xor) for i in range(n_row)])  34.4 us
    pallas_call x24, Pallas kernels, vmem_call(): pl.pallas_call(body, out_shape=[jax.ShapeDtypeStruct(shape, dtype) for sh...  9.22 us
    ppermute x5, starting transfers between devices, exchange(): return lax.ppermute(value, 'col', [(i, i ^ col_xor) for i in range(n_col)])  6.33 us
    ppermute x4, waiting for transfers between devices, exchange(): return lax.ppermute(value, ('row', 'col'), pairs)  6.19 us
    ppermute x4, starting transfers between devices, exchange(): return lax.ppermute(value, ('row', 'col'), pairs)  5.59 us
    ppermute x5, waiting for transfers between devices, exchange(): return lax.ppermute(value, 'col', [(i, i ^ col_xor) for i in range(n_col)])  4.12 us
  transfers between devices with their start and end apart: 39, of which 29 were waited for; matrix products, arithmetic and copies ran while one was open for 0% of the time, Pallas kernels for 6%

profile of v5, /device:TPU:0, one launch (start us, length us, event | category | flops | bytes accessed | tf_op | source)
XLA Modules:
  0.0 105.1 jit_solution(4527093476220643767)
XLA Ops:
  0.6 5.1 %collective-permute-start.2 = (bf16[128,128]{1,0:T(8,128)(2,1)}, bf16[128,128]{1,0:T(8,128)(2,1)S(1)}, u32[]{:S(2)}, u32[]{:S(2)}) collective-permute-start(bf16[128,128]{1,0:T(8,128)(2,1)} %anchor_ref.1), channel_id=1, source_target_pairs={{0,24},{2,26},{4,28},{6,30},{8,16},{10,18},{12,20},{14,22},{16,8},... | collective-permute-start | bytes 98312 | tf_op jit(solution)/shard_map/ppermute | solution.py:62
  7.1 3.0 %shard_map.112 = (bf16[256,1024]{1,0:T(8,128)(2,1)S(1)}, bf16[256,1152]{1,0:T(8,128)(2,1)S(1)}, bf16[1024,256]{1,0:T(8,128)(2,1)S(1)}, bf16[256,128]{1,0:T(8,128)(2,1)S(1)}) custom-call(s32[2]{0:T(128)S(1)} %pad_add_fusion.where_ref, s32[1,1]{1,0:T(1,128)S(6)} %copy.13.count, s32[1,1,64]{2,1,0:T(1,128)} %refs_0_.1, s32[1,1,64]{2,1,0:T(1,128)} %refs_1_.1, ...), custom_call_target="tpu_custom_call" | custom-call | tf_op jit(solution)/shard_map/pallas_call | solution.py:20
  10.8 1.6 %collective-permute-start.3 = (bf16[512,128]{1,0:T(8,128)(2,1)S(1)}, bf16[512,128]{1,0:T(8,128)(2,1)S(1)}, u32[]{:S(2)}, u32[]{:S(2)}) collective-permute-start(bf16[512,128]{1,0:T(8,128)(2,1)S(1)} %pad_maximum_fusion), channel_id=1, source_target_pairs={{0,4},{2,6},{4,0},{6,2},{8,12},{10,14},{12,8},{14,10},{16,20},{18,... | collective-permute-start | bytes 393224 | tf_op jit(solution)/shard_map/ppermute | solution.py:62
  12.9 4.4 %collective-permute-done.3 = bf16[512,128]{1,0:T(8,128)(2,1)S(1)} collective-permute-done((bf16[512,128]{1,0:T(8,128)(2,1)S(1)}, bf16[512,128]{1,0:T(8,128)(2,1)S(1)}, u32[]{:S(2)}, u32[]{:S(2)}) %collective-permute-start.3) | collective-permute-done | bytes 131104 | tf_op jit(solution)/shard_map/ppermute | solution.py:62
  19.2 1.5 %collective-permute-start.5 = (bf16[128,128]{1,0:T(8,128)(2,1)S(1)}, bf16[128,128]{1,0:T(8,128)(2,1)S(1)}, u32[]{:S(2)}, u32[]{:S(2)}) collective-permute-start(bf16[128,128]{1,0:T(8,128)(2,1)S(1)} %get-tuple-element.52), channel_id=1, source_target_pairs={{0,1},{1,0},{2,3},{3,2},{4,5},{5,4},{6,7},{7,6},{8,9},{9,8},{10,11... | collective-permute-start | bytes 98312 | tf_op jit(solution)/shard_map/ppermute | solution.py:64
  20.7 2.5 %collective-permute-done.5.refs_1_ = bf16[128,128]{1,0:T(8,128)(2,1)S(1)} collective-permute-done((bf16[128,128]{1,0:T(8,128)(2,1)S(1)}, bf16[128,128]{1,0:T(8,128)(2,1)S(1)}, u32[]{:S(2)}, u32[]{:S(2)}) %collective-permute-start.5) | collective-permute-done | bytes 32800 | tf_op jit(solution)/shard_map/ppermute | solution.py:64
  23.4 3.5 %collective-permute-start.8 = (bf16[128,128]{1,0:T(8,128)(2,1)S(1)}, bf16[128,128]{1,0:T(8,128)(2,1)S(1)}, u32[]{:S(2)}, u32[]{:S(2)}) collective-permute-start(bf16[128,128]{1,0:T(8,128)(2,1)S(1)} %shard_map.115.z0), channel_id=1, source_target_pairs={{0,24},{2,26},{4,28},{6,30},{8,16},{10,18},{12,20},{14,22},{16,8},... | collective-permute-start | bytes 98312 | tf_op jit(solution)/shard_map/ppermute | solution.py:62
  27.8 1.4 %collective-permute-done.8.z3 = bf16[128,128]{1,0:T(8,128)(2,1)S(1)} collective-permute-done((bf16[128,128]{1,0:T(8,128)(2,1)S(1)}, bf16[128,128]{1,0:T(8,128)(2,1)S(1)}, u32[]{:S(2)}, u32[]{:S(2)}) %collective-permute-start.8) | collective-permute-done | bytes 32800 | tf_op jit(solution)/shard_map/ppermute | solution.py:62
  29.3 2.5 %collective-permute-done.7.z2 = bf16[128,128]{1,0:T(8,128)(2,1)S(1)} collective-permute-done((bf16[128,128]{1,0:T(8,128)(2,1)S(1)}, bf16[128,128]{1,0:T(8,128)(2,1)S(1)}, u32[]{:S(2)}, u32[]{:S(2)}) %collective-permute-start.7) | collective-permute-done | bytes 32800 | tf_op jit(solution)/shard_map/ppermute | solution.py:62
  33.4 2.1 %collective-permute-start.11 = (bf16[384,128]{1,0:T(8,128)(2,1)S(1)}, bf16[384,128]{1,0:T(8,128)(2,1)S(1)}, u32[]{:S(2)}, u32[]{:S(2)}) collective-permute-start(bf16[384,128]{1,0:T(8,128)(2,1)S(1)} %get-tuple-element.55), channel_id=1, source_target_pairs={{0,1},{1,0},{2,3},{3,2},{4,5},{5,4},{6,7},{7,6},{8,9},{9,8},{10,11... | collective-permute-start | bytes 294920 | tf_op jit(solution)/shard_map/ppermute | solution.py:64
  35.6 1.4 %collective-permute-start.12 = (bf16[128,128]{1,0:T(8,128)(2,1)S(1)}, bf16[128,128]{1,0:T(8,128)(2,1)S(1)}, u32[]{:S(2)}, u32[]{:S(2)}) collective-permute-start(bf16[128,128]{1,0:T(8,128)(2,1)S(1)} %get-tuple-element.56), channel_id=1, source_target_pairs={{0,4},{2,6},{4,0},{6,2},{8,12},{10,14},{12,8},{14,10},{16,20},{18,... | collective-permute-start | bytes 98312 | tf_op jit(solution)/shard_map/ppermute | solution.py:62
  37.1 4.3 %collective-permute-done.12.refs_2_ = bf16[128,128]{1,0:T(8,128)(2,1)S(1)} collective-permute-done((bf16[128,128]{1,0:T(8,128)(2,1)S(1)}, bf16[128,128]{1,0:T(8,128)(2,1)S(1)}, u32[]{:S(2)}, u32[]{:S(2)}) %collective-permute-start.12) | collective-permute-done | bytes 32800 | tf_op jit(solution)/shard_map/ppermute | solution.py:62
  41.5 1.5 %collective-permute-start.16 = (bf16[128,128]{1,0:T(8,128)(2,1)S(1)}, bf16[128,128]{1,0:T(8,128)(2,1)S(1)}, u32[]{:S(2)}, u32[]{:S(2)}) collective-permute-start(bf16[128,128]{1,0:T(8,128)(2,1)S(1)} %shard_map.118.z0), channel_id=1, source_target_pairs={{0,24},{2,26},{4,28},{6,30},{8,16},{10,18},{12,20},{14,22},{16,8},... | collective-permute-start | bytes 98312 | tf_op jit(solution)/shard_map/ppermute | solution.py:62
  43.7 2.3 %collective-permute-start.14 = (bf16[128,128]{1,0:T(8,128)(2,1)S(1)}, bf16[128,128]{1,0:T(8,128)(2,1)S(1)}, u32[]{:S(2)}, u32[]{:S(2)}) collective-permute-start(bf16[128,128]{1,0:T(8,128)(2,1)S(1)} %shard_map.118.z0), channel_id=1, source_target_pairs={{0,8},{2,10},{4,12},{6,14},{8,0},{10,2},{12,4},{14,6},{16,24},{18,... | collective-permute-start | bytes 98312 | tf_op jit(solution)/shard_map/ppermute | solution.py:62
  46.0 1.3 %collective-permute-done.16.z3 = bf16[128,128]{1,0:T(8,128)(2,1)S(1)} collective-permute-done((bf16[128,128]{1,0:T(8,128)(2,1)S(1)}, bf16[128,128]{1,0:T(8,128)(2,1)S(1)}, u32[]{:S(2)}, u32[]{:S(2)}) %collective-permute-start.16) | collective-permute-done | bytes 32800 | tf_op jit(solution)/shard_map/ppermute | solution.py:62
  49.9 2.4 %collective-permute-start.20 = (bf16[512,128]{1,0:T(8,128)(2,1)S(1)}, bf16[512,128]{1,0:T(8,128)(2,1)S(1)}, u32[]{:S(2)}, u32[]{:S(2)}) collective-permute-start(bf16[512,128]{1,0:T(8,128)(2,1)S(1)} %get-tuple-element.59), channel_id=1, source_target_pairs={{0,5},{1,4},{2,7},{3,6},{4,1},{5,0},{6,3},{7,2},{8,13},{9,12},{10,... | collective-permute-start | bytes 393224 | tf_op jit(solution)/shard_map/ppermute | solution.py:70
  53.7 3.1 %collective-permute-done.20.refs_2_ = bf16[512,128]{1,0:T(8,128)(2,1)S(1)} collective-permute-done((bf16[512,128]{1,0:T(8,128)(2,1)S(1)}, bf16[512,128]{1,0:T(8,128)(2,1)S(1)}, u32[]{:S(2)}, u32[]{:S(2)}) %collective-permute-start.20) | collective-permute-done | bytes 131104 | tf_op jit(solution)/shard_map/ppermute | solution.py:70
  56.8 2.4 %collective-permute-done.19.refs_1_ = bf16[512,128]{1,0:T(8,128)(2,1)S(1)} collective-permute-done((bf16[512,128]{1,0:T(8,128)(2,1)S(1)}, bf16[512,128]{1,0:T(8,128)(2,1)S(1)}, u32[]{:S(2)}, u32[]{:S(2)}) %collective-permute-start.19) | collective-permute-done | bytes 131104 | tf_op jit(solution)/shard_map/ppermute | solution.py:62
  61.2 1.7 %collective-permute-start.22 = (bf16[128,128]{1,0:T(8,128)(2,1)S(1)}, bf16[128,128]{1,0:T(8,128)(2,1)S(1)}, u32[]{:S(2)}, u32[]{:S(2)}) collective-permute-start(bf16[128,128]{1,0:T(8,128)(2,1)S(1)} %get-tuple-element.68), channel_id=1, source_target_pairs={{0,8},{2,10},{4,12},{6,14},{8,0},{10,2},{12,4},{14,6},{16,24},{18,... | collective-permute-start | bytes 98312 | tf_op jit(solution)/shard_map/ppermute | solution.py:62
  64.2 1.5 %collective-permute-start.24 = (bf16[128,128]{1,0:T(8,128)(2,1)S(1)}, bf16[128,128]{1,0:T(8,128)(2,1)S(1)}, u32[]{:S(2)}, u32[]{:S(2)}) collective-permute-start(bf16[128,128]{1,0:T(8,128)(2,1)S(1)} %get-tuple-element.70), channel_id=1, source_target_pairs={{0,24},{2,26},{4,28},{6,30},{8,16},{10,18},{12,20},{14,22},{16,8},... | collective-permute-start | bytes 98312 | tf_op jit(solution)/shard_map/ppermute | solution.py:62
  65.7 2.3 %collective-permute-done.23.refs_1_ = bf16[128,128]{1,0:T(8,128)(2,1)S(1)} collective-permute-done((bf16[128,128]{1,0:T(8,128)(2,1)S(1)}, bf16[128,128]{1,0:T(8,128)(2,1)S(1)}, u32[]{:S(2)}, u32[]{:S(2)}) %collective-permute-start.23) | collective-permute-done | bytes 32800 | tf_op jit(solution)/shard_map/ppermute | solution.py:62
  68.0 1.9 %collective-permute-done.24.refs_2_ = bf16[128,128]{1,0:T(8,128)(2,1)S(1)} collective-permute-done((bf16[128,128]{1,0:T(8,128)(2,1)S(1)}, bf16[128,128]{1,0:T(8,128)(2,1)S(1)}, u32[]{:S(2)}, u32[]{:S(2)}) %collective-permute-start.24) | collective-permute-done | bytes 32800 | tf_op jit(solution)/shard_map/ppermute | solution.py:62
  70.1 1.8 %collective-permute-start.27 = (bf16[128,128]{1,0:T(8,128)(2,1)S(1)}, bf16[128,128]{1,0:T(8,128)(2,1)S(1)}, u32[]{:S(2)}, u32[]{:S(2)}) collective-permute-start(bf16[128,128]{1,0:T(8,128)(2,1)S(1)} %shard_map.127.refs_0_), channel_id=1, source_target_pairs={{0,5},{1,4},{2,7},{3,6},{4,1},{5,0},{6,3},{7,2},{8,13},{9,12},{10,... | collective-permute-start | bytes 98312 | tf_op jit(solution)/shard_map/ppermute | solution.py:70
  78.9 2.0 %collective-permute-start.30 = (bf16[128,128]{1,0:T(8,128)(2,1)S(1)}, bf16[128,128]{1,0:T(8,128)(2,1)S(1)}, u32[]{:S(2)}, u32[]{:S(2)}) collective-permute-start(bf16[128,128]{1,0:T(8,128)(2,1)S(1)} %get-tuple-element.74), channel_id=1, source_target_pairs={{0,16},{2,18},{4,20},{6,22},{8,24},{10,26},{12,28},{14,30},{16,0},... | collective-permute-start | bytes 98312 | tf_op jit(solution)/shard_map/ppermute | solution.py:62
  80.9 2.4 %collective-permute-start.31 = (bf16[128,128]{1,0:T(8,128)(2,1)S(1)}, bf16[128,128]{1,0:T(8,128)(2,1)S(1)}, u32[]{:S(2)}, u32[]{:S(2)}) collective-permute-start(bf16[128,128]{1,0:T(8,128)(2,1)S(1)} %get-tuple-element.75), channel_id=1, source_target_pairs={{0,24},{2,26},{4,28},{6,30},{8,16},{10,18},{12,20},{14,22},{16,8},... | collective-permute-start | bytes 98312 | tf_op jit(solution)/shard_map/ppermute | solution.py:62
  83.9 2.7 %collective-permute-done.31.refs_2_ = bf16[128,128]{1,0:T(8,128)(2,1)S(1)} collective-permute-done((bf16[128,128]{1,0:T(8,128)(2,1)S(1)}, bf16[128,128]{1,0:T(8,128)(2,1)S(1)}, u32[]{:S(2)}, u32[]{:S(2)}) %collective-permute-start.31) | collective-permute-done | bytes 32800 | tf_op jit(solution)/shard_map/ppermute | solution.py:62
  89.0 1.5 %collective-permute-start.32 = (bf16[256,128]{1,0:T(8,128)(2,1)S(1)}, bf16[256,128]{1,0:T(8,128)(2,1)S(1)}, u32[]{:S(2)}, u32[]{:S(2)}) collective-permute-start(bf16[256,128]{1,0:T(8,128)(2,1)S(1)} %shard_map.131.refs_0_), channel_id=1, source_target_pairs={{0,1},{1,0},{2,3},{3,2},{4,5},{5,4},{6,7},{7,6},{8,9},{9,8},{10,11... | collective-permute-start | bytes 196616 | tf_op jit(solution)/shard_map/ppermute | solution.py:64
  90.5 1.7 %collective-permute-done.34.refs_3_ = bf16[256,128]{1,0:T(8,128)(2,1)S(1)} collective-permute-done((bf16[256,128]{1,0:T(8,128)(2,1)S(1)}, bf16[256,128]{1,0:T(8,128)(2,1)S(1)}, u32[]{:S(2)}, u32[]{:S(2)}) %collective-permute-start.34) | collective-permute-done | bytes 65568 | tf_op jit(solution)/shard_map/ppermute | solution.py:70
  95.2 2.9 %collective-permute-start.37 = (bf16[256,128]{1,0:T(8,128)(2,1)S(1)}, bf16[256,128]{1,0:T(8,128)(2,1)S(1)}, u32[]{:S(2)}, u32[]{:S(2)}) collective-permute-start(bf16[256,128]{1,0:T(8,128)(2,1)S(1)} %get-tuple-element.82), channel_id=1, source_target_pairs={{0,16},{2,18},{4,20},{6,22},{8,24},{10,26},{12,28},{14,30},{16,0},... | collective-permute-start | bytes 196616 | tf_op jit(solution)/shard_map/ppermute | solution.py:62
  98.1 1.5 %collective-permute-start.38 = (bf16[256,128]{1,0:T(8,128)(2,1)S(1)}, bf16[256,128]{1,0:T(8,128)(2,1)S(1)}, u32[]{:S(2)}, u32[]{:S(2)}) collective-permute-start(bf16[256,128]{1,0:T(8,128)(2,1)S(1)} %get-tuple-element.83), channel_id=1, source_target_pairs={{0,24},{2,26},{4,28},{6,30},{8,16},{10,18},{12,20},{14,22},{16,8},... | collective-permute-start | bytes 196616 | tf_op jit(solution)/shard_map/ppermute | solution.py:62
  100.5 2.4 %collective-permute-done.37.refs_1_ = bf16[256,128]{1,0:T(8,128)(2,1)S(1)} collective-permute-done((bf16[256,128]{1,0:T(8,128)(2,1)S(1)}, bf16[256,128]{1,0:T(8,128)(2,1)S(1)}, u32[]{:S(2)}, u32[]{:S(2)}) %collective-permute-start.37) | collective-permute-done | bytes 65568 | tf_op jit(solution)/shard_map/ppermute | solution.py:62
  102.9 1.4 %collective-permute-done.38.refs_2_ = bf16[256,128]{1,0:T(8,128)(2,1)S(1)} collective-permute-done((bf16[256,128]{1,0:T(8,128)(2,1)S(1)}, bf16[256,128]{1,0:T(8,128)(2,1)S(1)}, u32[]{:S(2)}, u32[]{:S(2)}) %collective-permute-start.38) | collective-permute-done | bytes 65568 | tf_op jit(solution)/shard_map/ppermute | solution.py:62
  (82 shorter events, 29.5 us)
Async XLA Ops:
  0.6 9.5 %collective-permute-start.2 = (bf16[128,128]{1,0:T(8,128)(2,1)}, bf16[128,128]{1,0:T(8,128)(2,1)S(1)}, u32[]{:S(2)}, u32[]{:S(2)}) collective-permute-start(bf16[128,128]{1,0:T(8,128)(2,1)} %anchor_ref.1), channel_id=1, source_target_pairs={{0,24},{2,26},{4,28},{6,30},{8,16},{10,18},{12,20},{14,22},{16,8},... | collective-permute-start | bytes 98312 | tf_op jit(solution)/shard_map/ppermute | solution.py:62
  5.8 5.0 %collective-permute-start.1 = (bf16[128,128]{1,0:T(8,128)(2,1)}, bf16[128,128]{1,0:T(8,128)(2,1)S(1)}, u32[]{:S(2)}, u32[]{:S(2)}) collective-permute-start(bf16[128,128]{1,0:T(8,128)(2,1)} %anchor_ref.1), channel_id=1, source_target_pairs={{0,16},{2,18},{4,20},{6,22},{8,24},{10,26},{12,28},{14,30},{16,0},... | collective-permute-start | bytes 98312 | tf_op jit(solution)/shard_map/ppermute | solution.py:62
  5.8 5.0 %collective-permute-start = (bf16[128,128]{1,0:T(8,128)(2,1)}, bf16[128,128]{1,0:T(8,128)(2,1)S(1)}, u32[]{:S(2)}, u32[]{:S(2)}) collective-permute-start(bf16[128,128]{1,0:T(8,128)(2,1)} %anchor_ref.1), channel_id=1, source_target_pairs={{0,8},{2,10},{4,12},{6,14},{8,0},{10,2},{12,4},{14,6},{16,24},{18,... | collective-permute-start | bytes 98312 | tf_op jit(solution)/shard_map/ppermute | solution.py:62
  10.8 6.5 %collective-permute-start.3 = (bf16[512,128]{1,0:T(8,128)(2,1)S(1)}, bf16[512,128]{1,0:T(8,128)(2,1)S(1)}, u32[]{:S(2)}, u32[]{:S(2)}) collective-permute-start(bf16[512,128]{1,0:T(8,128)(2,1)S(1)} %pad_maximum_fusion), channel_id=1, source_target_pairs={{0,4},{2,6},{4,0},{6,2},{8,12},{10,14},{12,8},{14,10},{16,20},{18,... | collective-permute-start | bytes 393224 | tf_op jit(solution)/shard_map/ppermute | solution.py:62
  12.4 19.4 %collective-permute-start.9 = (bf16[256,1152]{1,0:T(8,128)(2,1)S(1)}, bf16[256,1152]{1,0:T(8,128)(2,1)S(1)}, u32[]{:S(2)}, u32[]{:S(2)}) collective-permute-start(bf16[256,1152]{1,0:T(8,128)(2,1)S(1)} %get-tuple-element.50.refs_1_), channel_id=1, source_target_pairs={{0,4},{2,6},{4,0},{6,2},{8,12},{10,14},{12,8},{14,10},{16,20},{18,... | collective-permute-start | bytes 1769480 | tf_op jit(solution)/shard_map/ppermute | solution.py:62
  19.2 4.0 %collective-permute-start.5 = (bf16[128,128]{1,0:T(8,128)(2,1)S(1)}, bf16[128,128]{1,0:T(8,128)(2,1)S(1)}, u32[]{:S(2)}, u32[]{:S(2)}) collective-permute-start(bf16[128,128]{1,0:T(8,128)(2,1)S(1)} %get-tuple-element.52), channel_id=1, source_target_pairs={{0,1},{1,0},{2,3},{3,2},{4,5},{5,4},{6,7},{7,6},{8,9},{9,8},{10,11... | collective-permute-start | bytes 98312 | tf_op jit(solution)/shard_map/ppermute | solution.py:64
  23.4 5.9 %collective-permute-start.8 = (bf16[128,128]{1,0:T(8,128)(2,1)S(1)}, bf16[128,128]{1,0:T(8,128)(2,1)S(1)}, u32[]{:S(2)}, u32[]{:S(2)}) collective-permute-start(bf16[128,128]{1,0:T(8,128)(2,1)S(1)} %shard_map.115.z0), channel_id=1, source_target_pairs={{0,24},{2,26},{4,28},{6,30},{8,16},{10,18},{12,20},{14,22},{16,8},... | collective-permute-start | bytes 98312 | tf_op jit(solution)/shard_map/ppermute | solution.py:62
  26.9 4.8 %collective-permute-start.7 = (bf16[128,128]{1,0:T(8,128)(2,1)S(1)}, bf16[128,128]{1,0:T(8,128)(2,1)S(1)}, u32[]{:S(2)}, u32[]{:S(2)}) collective-permute-start(bf16[128,128]{1,0:T(8,128)(2,1)S(1)} %shard_map.115.z0), channel_id=1, source_target_pairs={{0,16},{2,18},{4,20},{6,22},{8,24},{10,26},{12,28},{14,30},{16,0},... | collective-permute-start | bytes 98312 | tf_op jit(solution)/shard_map/ppermute | solution.py:62
  26.9 4.8 %collective-permute-start.6 = (bf16[128,128]{1,0:T(8,128)(2,1)S(1)}, bf16[128,128]{1,0:T(8,128)(2,1)S(1)}, u32[]{:S(2)}, u32[]{:S(2)}) collective-permute-start(bf16[128,128]{1,0:T(8,128)(2,1)S(1)} %shard_map.115.z0), channel_id=1, source_target_pairs={{0,8},{2,10},{4,12},{6,14},{8,0},{10,2},{12,4},{14,6},{16,24},{18,... | collective-permute-start | bytes 98312 | tf_op jit(solution)/shard_map/ppermute | solution.py:62
  33.4 7.9 %collective-permute-start.11 = (bf16[384,128]{1,0:T(8,128)(2,1)S(1)}, bf16[384,128]{1,0:T(8,128)(2,1)S(1)}, u32[]{:S(2)}, u32[]{:S(2)}) collective-permute-start(bf16[384,128]{1,0:T(8,128)(2,1)S(1)} %get-tuple-element.55), channel_id=1, source_target_pairs={{0,1},{1,0},{2,3},{3,2},{4,5},{5,4},{6,7},{7,6},{8,9},{9,8},{10,11... | collective-permute-start | bytes 294920 | tf_op jit(solution)/shard_map/ppermute | solution.py:64
  35.5 5.8 %collective-permute-start.13 = (bf16[384,128]{1,0:T(8,128)(2,1)S(1)}, bf16[384,128]{1,0:T(8,128)(2,1)S(1)}, u32[]{:S(2)}, u32[]{:S(2)}) collective-permute-start(bf16[384,128]{1,0:T(8,128)(2,1)S(1)} %get-tuple-element.57), channel_id=1, source_target_pairs={{0,5},{1,4},{2,7},{3,6},{4,1},{5,0},{6,3},{7,2},{8,13},{9,12},{10,... | collective-permute-start | bytes 294920 | tf_op jit(solution)/shard_map/ppermute | solution.py:70
  35.6 5.7 %collective-permute-start.12 = (bf16[128,128]{1,0:T(8,128)(2,1)S(1)}, bf16[128,128]{1,0:T(8,128)(2,1)S(1)}, u32[]{:S(2)}, u32[]{:S(2)}) collective-permute-start(bf16[128,128]{1,0:T(8,128)(2,1)S(1)} %get-tuple-element.56), channel_id=1, source_target_pairs={{0,4},{2,6},{4,0},{6,2},{8,12},{10,14},{12,8},{14,10},{16,20},{18,... | collective-permute-start | bytes 98312 | tf_op jit(solution)/shard_map/ppermute | solution.py:62
  41.5 5.8 %collective-permute-start.16 = (bf16[128,128]{1,0:T(8,128)(2,1)S(1)}, bf16[128,128]{1,0:T(8,128)(2,1)S(1)}, u32[]{:S(2)}, u32[]{:S(2)}) collective-permute-start(bf16[128,128]{1,0:T(8,128)(2,1)S(1)} %shard_map.118.z0), channel_id=1, source_target_pairs={{0,24},{2,26},{4,28},{6,30},{8,16},{10,18},{12,20},{14,22},{16,8},... | collective-permute-start | bytes 98312 | tf_op jit(solution)/shard_map/ppermute | solution.py:62
  43.1 4.8 %collective-permute-start.15 = (bf16[128,128]{1,0:T(8,128)(2,1)S(1)}, bf16[128,128]{1,0:T(8,128)(2,1)S(1)}, u32[]{:S(2)}, u32[]{:S(2)}) collective-permute-start(bf16[128,128]{1,0:T(8,128)(2,1)S(1)} %shard_map.118.z0), channel_id=1, source_target_pairs={{0,16},{2,18},{4,20},{6,22},{8,24},{10,26},{12,28},{14,30},{16,0},... | collective-permute-start | bytes 98312 | tf_op jit(solution)/shard_map/ppermute | solution.py:62
  43.7 4.5 %collective-permute-start.14 = (bf16[128,128]{1,0:T(8,128)(2,1)S(1)}, bf16[128,128]{1,0:T(8,128)(2,1)S(1)}, u32[]{:S(2)}, u32[]{:S(2)}) collective-permute-start(bf16[128,128]{1,0:T(8,128)(2,1)S(1)} %shard_map.118.z0), channel_id=1, source_target_pairs={{0,8},{2,10},{4,12},{6,14},{8,0},{10,2},{12,4},{14,6},{16,24},{18,... | collective-permute-start | bytes 98312 | tf_op jit(solution)/shard_map/ppermute | solution.py:62
  49.9 6.9 %collective-permute-start.20 = (bf16[512,128]{1,0:T(8,128)(2,1)S(1)}, bf16[512,128]{1,0:T(8,128)(2,1)S(1)}, u32[]{:S(2)}, u32[]{:S(2)}) collective-permute-start(bf16[512,128]{1,0:T(8,128)(2,1)S(1)} %get-tuple-element.59), channel_id=1, source_target_pairs={{0,5},{1,4},{2,7},{3,6},{4,1},{5,0},{6,3},{7,2},{8,13},{9,12},{10,... | collective-permute-start | bytes 393224 | tf_op jit(solution)/shard_map/ppermute | solution.py:70
  52.4 6.9 %collective-permute-start.19 = (bf16[512,128]{1,0:T(8,128)(2,1)S(1)}, bf16[512,128]{1,0:T(8,128)(2,1)S(1)}, u32[]{:S(2)}, u32[]{:S(2)}) collective-permute-start(bf16[512,128]{1,0:T(8,128)(2,1)S(1)} %get-tuple-element.59), channel_id=1, source_target_pairs={{0,4},{2,6},{4,0},{6,2},{8,12},{10,14},{12,8},{14,10},{16,20},{18,... | collective-permute-start | bytes 393224 | tf_op jit(solution)/shard_map/ppermute | solution.py:62
  52.7 6.5 %collective-permute-start.18 = (bf16[512,128]{1,0:T(8,128)(2,1)S(1)}, bf16[512,128]{1,0:T(8,128)(2,1)S(1)}, u32[]{:S(2)}, u32[]{:S(2)}) collective-permute-start(bf16[512,128]{1,0:T(8,128)(2,1)S(1)} %get-tuple-element.59), channel_id=1, source_target_pairs={{0,1},{1,0},{2,3},{3,2},{4,5},{5,4},{6,7},{7,6},{8,9},{9,8},{10,11... | collective-permute-start | bytes 393224 | tf_op jit(solution)/shard_map/ppermute | solution.py:64
  61.2 4.5 %collective-permute-start.22 = (bf16[128,128]{1,0:T(8,128)(2,1)S(1)}, bf16[128,128]{1,0:T(8,128)(2,1)S(1)}, u32[]{:S(2)}, u32[]{:S(2)}) collective-permute-start(bf16[128,128]{1,0:T(8,128)(2,1)S(1)} %get-tuple-element.68), channel_id=1, source_target_pairs={{0,8},{2,10},{4,12},{6,14},{8,0},{10,2},{12,4},{14,6},{16,24},{18,... | collective-permute-start | bytes 98312 | tf_op jit(solution)/shard_map/ppermute | solution.py:62
  63.0 5.0 %collective-permute-start.23 = (bf16[128,128]{1,0:T(8,128)(2,1)S(1)}, bf16[128,128]{1,0:T(8,128)(2,1)S(1)}, u32[]{:S(2)}, u32[]{:S(2)}) collective-permute-start(bf16[128,128]{1,0:T(8,128)(2,1)S(1)} %get-tuple-element.69), channel_id=1, source_target_pairs={{0,16},{2,18},{4,20},{6,22},{8,24},{10,26},{12,28},{14,30},{16,0},... | collective-permute-start | bytes 98312 | tf_op jit(solution)/shard_map/ppermute | solution.py:62
  64.2 5.7 %collective-permute-start.24 = (bf16[128,128]{1,0:T(8,128)(2,1)S(1)}, bf16[128,128]{1,0:T(8,128)(2,1)S(1)}, u32[]{:S(2)}, u32[]{:S(2)}) collective-permute-start(bf16[128,128]{1,0:T(8,128)(2,1)S(1)} %get-tuple-element.70), channel_id=1, source_target_pairs={{0,24},{2,26},{4,28},{6,30},{8,16},{10,18},{12,20},{14,22},{16,8},... | collective-permute-start | bytes 98312 | tf_op jit(solution)/shard_map/ppermute | solution.py:62
  70.1 4.9 %collective-permute-start.27 = (bf16[128,128]{1,0:T(8,128)(2,1)S(1)}, bf16[128,128]{1,0:T(8,128)(2,1)S(1)}, u32[]{:S(2)}, u32[]{:S(2)}) collective-permute-start(bf16[128,128]{1,0:T(8,128)(2,1)S(1)} %shard_map.127.refs_0_), channel_id=1, source_target_pairs={{0,5},{1,4},{2,7},{3,6},{4,1},{5,0},{6,3},{7,2},{8,13},{9,12},{10,... | collective-permute-start | bytes 98312 | tf_op jit(solution)/shard_map/ppermute | solution.py:70
  71.9 3.9 %collective-permute-start.26 = (bf16[128,128]{1,0:T(8,128)(2,1)S(1)}, bf16[128,128]{1,0:T(8,128)(2,1)S(1)}, u32[]{:S(2)}, u32[]{:S(2)}) collective-permute-start(bf16[128,128]{1,0:T(8,128)(2,1)S(1)} %shard_map.127.refs_0_), channel_id=1, source_target_pairs={{0,4},{2,6},{4,0},{6,2},{8,12},{10,14},{12,8},{14,10},{16,20},{18,... | collective-permute-start | bytes 98312 | tf_op jit(solution)/shard_map/ppermute | solution.py:62
  78.8 5.1 %collective-permute-start.29 = (bf16[128,128]{1,0:T(8,128)(2,1)S(1)}, bf16[128,128]{1,0:T(8,128)(2,1)S(1)}, u32[]{:S(2)}, u32[]{:S(2)}) collective-permute-start(bf16[128,128]{1,0:T(8,128)(2,1)S(1)} %get-tuple-element.73), channel_id=1, source_target_pairs={{0,8},{2,10},{4,12},{6,14},{8,0},{10,2},{12,4},{14,6},{16,24},{18,... | collective-permute-start | bytes 98312 | tf_op jit(solution)/shard_map/ppermute | solution.py:62
  78.9 5.0 %collective-permute-start.30 = (bf16[128,128]{1,0:T(8,128)(2,1)S(1)}, bf16[128,128]{1,0:T(8,128)(2,1)S(1)}, u32[]{:S(2)}, u32[]{:S(2)}) collective-permute-start(bf16[128,128]{1,0:T(8,128)(2,1)S(1)} %get-tuple-element.74), channel_id=1, source_target_pairs={{0,16},{2,18},{4,20},{6,22},{8,24},{10,26},{12,28},{14,30},{16,0},... | collective-permute-start | bytes 98312 | tf_op jit(solution)/shard_map/ppermute | solution.py:62
  80.9 5.7 %collective-permute-start.31 = (bf16[128,128]{1,0:T(8,128)(2,1)S(1)}, bf16[128,128]{1,0:T(8,128)(2,1)S(1)}, u32[]{:S(2)}, u32[]{:S(2)}) collective-permute-start(bf16[128,128]{1,0:T(8,128)(2,1)S(1)} %get-tuple-element.75), channel_id=1, source_target_pairs={{0,24},{2,26},{4,28},{6,30},{8,16},{10,18},{12,20},{14,22},{16,8},... | collective-permute-start | bytes 98312 | tf_op jit(solution)/shard_map/ppermute | solution.py:62
  87.0 5.3 %collective-permute-start.34 = (bf16[256,128]{1,0:T(8,128)(2,1)S(1)}, bf16[256,128]{1,0:T(8,128)(2,1)S(1)}, u32[]{:S(2)}, u32[]{:S(2)}) collective-permute-start(bf16[256,128]{1,0:T(8,128)(2,1)S(1)} %shard_map.131.refs_0_), channel_id=1, source_target_pairs={{0,5},{1,4},{2,7},{3,6},{4,1},{5,0},{6,3},{7,2},{8,13},{9,12},{10,... | collective-permute-start | bytes 196616 | tf_op jit(solution)/shard_map/ppermute | solution.py:70
  88.2 4.7 %collective-permute-start.33 = (bf16[256,128]{1,0:T(8,128)(2,1)S(1)}, bf16[256,128]{1,0:T(8,128)(2,1)S(1)}, u32[]{:S(2)}, u32[]{:S(2)}) collective-permute-start(bf16[256,128]{1,0:T(8,128)(2,1)S(1)} %shard_map.131.refs_0_), channel_id=1, source_target_pairs={{0,4},{2,6},{4,0},{6,2},{8,12},{10,14},{12,8},{14,10},{16,20},{18,... | collective-permute-start | bytes 196616 | tf_op jit(solution)/shard_map/ppermute | solution.py:62
  89.0 4.3 %collective-permute-start.32 = (bf16[256,128]{1,0:T(8,128)(2,1)S(1)}, bf16[256,128]{1,0:T(8,128)(2,1)S(1)}, u32[]{:S(2)}, u32[]{:S(2)}) collective-permute-start(bf16[256,128]{1,0:T(8,128)(2,1)S(1)} %shard_map.131.refs_0_), channel_id=1, source_target_pairs={{0,1},{1,0},{2,3},{3,2},{4,5},{5,4},{6,7},{7,6},{8,9},{9,8},{10,11... | collective-permute-start | bytes 196616 | tf_op jit(solution)/shard_map/ppermute | solution.py:64
  95.1 5.4 %collective-permute-start.36 = (bf16[256,128]{1,0:T(8,128)(2,1)S(1)}, bf16[256,128]{1,0:T(8,128)(2,1)S(1)}, u32[]{:S(2)}, u32[]{:S(2)}) collective-permute-start(bf16[256,128]{1,0:T(8,128)(2,1)S(1)} %get-tuple-element.81), channel_id=1, source_target_pairs={{0,8},{2,10},{4,12},{6,14},{8,0},{10,2},{12,4},{14,6},{16,24},{18,... | collective-permute-start | bytes 196616 | tf_op jit(solution)/shard_map/ppermute | solution.py:62
  95.2 7.7 %collective-permute-start.37 = (bf16[256,128]{1,0:T(8,128)(2,1)S(1)}, bf16[256,128]{1,0:T(8,128)(2,1)S(1)}, u32[]{:S(2)}, u32[]{:S(2)}) collective-permute-start(bf16[256,128]{1,0:T(8,128)(2,1)S(1)} %get-tuple-element.82), channel_id=1, source_target_pairs={{0,16},{2,18},{4,20},{6,22},{8,24},{10,26},{12,28},{14,30},{16,0},... | collective-permute-start | bytes 196616 | tf_op jit(solution)/shard_map/ppermute | solution.py:62
  98.1 6.2 %collective-permute-start.38 = (bf16[256,128]{1,0:T(8,128)(2,1)S(1)}, bf16[256,128]{1,0:T(8,128)(2,1)S(1)}, u32[]{:S(2)}, u32[]{:S(2)}) collective-permute-start(bf16[256,128]{1,0:T(8,128)(2,1)S(1)} %get-tuple-element.83), channel_id=1, source_target_pairs={{0,24},{2,26},{4,28},{6,30},{8,16},{10,18},{12,20},{14,22},{16,8},... | collective-permute-start | bytes 196616 | tf_op jit(solution)/shard_map/ppermute | solution.py:62
  (10 other events, 49.0 us)

commit v6 on v5

--- a/solution.py
+++ b/solution.py
@@ -75,7 +75,7 @@
     def to_square(values):
         return [exchange(v, 2 * y, x) for (y, x), v in zip(square[1:], values)]
 
-    chunk = min(16, slots)
+    chunk = min(8, slots)
     n_chunks = slots // chunk
     assert slots % chunk == 0
 

time: 105 us -> 105 us (level)
  transfers between devices with their start and end apart: 39 -> 39, of which waited for: 29 -> 28; matrix products, arithmetic and copies ran while one was open for 0% -> 0% of each run, Pallas kernels for 6% -> 5%
where the time goes in v6:
time: 105 us
  waiting for transfers between devices  48.2 us (46%)
  starting transfers between devices  46.4 us (44%)
  Pallas kernels  8.75 us (8%)
  between operations  1.56 us (1%)
    ppermute x30, waiting for transfers between devices, exchange(): return lax.ppermute(value, 'row', [(i, i ^ row_xor) for i in range(n_row)])  37.8 us
    ppermute x30, starting transfers between devices, exchange(): return lax.ppermute(value, 'row', [(i, i ^ row_xor) for i in range(n_row)])  34.7 us
    pallas_call x24, Pallas kernels, vmem_call(): pl.pallas_call(body, out_shape=[jax.ShapeDtypeStruct(shape, dtype) for sh...  8.75 us
    ppermute x4, waiting for transfers between devices, exchange(): return lax.ppermute(value, ('row', 'col'), pairs)  6.63 us
    ppermute x4, starting transfers between devices, exchange(): return lax.ppermute(value, ('row', 'col'), pairs)  6 us
    ppermute x5, starting transfers between devices, exchange(): return lax.ppermute(value, 'col', [(i, i ^ col_xor) for i in range(n_col)])  5.72 us
    ppermute x5, waiting for transfers between devices, exchange(): return lax.ppermute(value, 'col', [(i, i ^ col_xor) for i in range(n_col)])  3.87 us
  transfers between devices with their start and end apart: 39, of which 28 were waited for; matrix products, arithmetic and copies ran while one was open for 0% of the time, Pallas kernels for 5%

profile of v6, /device:TPU:0, one launch (start us, length us, event | category | flops | bytes accessed | tf_op | source)
XLA Modules:
  0.0 105.2 jit_solution(2386219090306202891)
XLA Ops:
  0.6 5.1 %collective-permute-start.2 = (bf16[128,128]{1,0:T(8,128)(2,1)}, bf16[128,128]{1,0:T(8,128)(2,1)S(1)}, u32[]{:S(2)}, u32[]{:S(2)}) collective-permute-start(bf16[128,128]{1,0:T(8,128)(2,1)} %anchor_ref.1), channel_id=1, source_target_pairs={{0,24},{2,26},{4,28},{6,30},{8,16},{10,18},{12,20},{14,22},{16,8},... | collective-permute-start | bytes 98312 | tf_op jit(solution)/shard_map/ppermute | solution.py:62
  7.1 2.5 %shard_map.112 = (bf16[256,1024]{1,0:T(8,128)(2,1)S(1)}, bf16[256,1152]{1,0:T(8,128)(2,1)S(1)}, bf16[1024,256]{1,0:T(8,128)(2,1)S(1)}, bf16[256,128]{1,0:T(8,128)(2,1)S(1)}) custom-call(s32[2]{0:T(128)S(1)} %pad_add_fusion.where_ref, s32[1,1]{1,0:T(1,128)S(6)} %copy.13.count, s32[1,1,64]{2,1,0:T(1,128)} %refs_0_.1, s32[1,1,64]{2,1,0:T(1,128)} %refs_1_.1, ...), custom_call_target="tpu_custom_call" | custom-call | tf_op jit(solution)/shard_map/pallas_call | solution.py:20
  10.8 1.6 %collective-permute-start.3 = (bf16[512,128]{1,0:T(8,128)(2,1)S(1)}, bf16[512,128]{1,0:T(8,128)(2,1)S(1)}, u32[]{:S(2)}, u32[]{:S(2)}) collective-permute-start(bf16[512,128]{1,0:T(8,128)(2,1)S(1)} %pad_maximum_fusion), channel_id=1, source_target_pairs={{0,4},{2,6},{4,0},{6,2},{8,12},{10,14},{12,8},{14,10},{16,20},{18,... | collective-permute-start | bytes 393224 | tf_op jit(solution)/shard_map/ppermute | solution.py:62
  12.9 4.2 %collective-permute-done.3 = bf16[512,128]{1,0:T(8,128)(2,1)S(1)} collective-permute-done((bf16[512,128]{1,0:T(8,128)(2,1)S(1)}, bf16[512,128]{1,0:T(8,128)(2,1)S(1)}, u32[]{:S(2)}, u32[]{:S(2)}) %collective-permute-start.3) | collective-permute-done | bytes 131104 | tf_op jit(solution)/shard_map/ppermute | solution.py:62
  19.1 1.7 %collective-permute-start.5 = (bf16[128,128]{1,0:T(8,128)(2,1)S(1)}, bf16[128,128]{1,0:T(8,128)(2,1)S(1)}, u32[]{:S(2)}, u32[]{:S(2)}) collective-permute-start(bf16[128,128]{1,0:T(8,128)(2,1)S(1)} %get-tuple-element.52), channel_id=1, source_target_pairs={{0,1},{1,0},{2,3},{3,2},{4,5},{5,4},{6,7},{7,6},{8,9},{9,8},{10,11... | collective-permute-start | bytes 98312 | tf_op jit(solution)/shard_map/ppermute | solution.py:64
  20.8 2.3 %collective-permute-done.5.refs_1_ = bf16[128,128]{1,0:T(8,128)(2,1)S(1)} collective-permute-done((bf16[128,128]{1,0:T(8,128)(2,1)S(1)}, bf16[128,128]{1,0:T(8,128)(2,1)S(1)}, u32[]{:S(2)}, u32[]{:S(2)}) %collective-permute-start.5) | collective-permute-done | bytes 32800 | tf_op jit(solution)/shard_map/ppermute | solution.py:64
  23.2 3.2 %collective-permute-start.8 = (bf16[128,128]{1,0:T(8,128)(2,1)S(1)}, bf16[128,128]{1,0:T(8,128)(2,1)S(1)}, u32[]{:S(2)}, u32[]{:S(2)}) collective-permute-start(bf16[128,128]{1,0:T(8,128)(2,1)S(1)} %shard_map.115.z0), channel_id=1, source_target_pairs={{0,24},{2,26},{4,28},{6,30},{8,16},{10,18},{12,20},{14,22},{16,8},... | collective-permute-start | bytes 98312 | tf_op jit(solution)/shard_map/ppermute | solution.py:62
  27.7 1.3 %collective-permute-done.8.z3 = bf16[128,128]{1,0:T(8,128)(2,1)S(1)} collective-permute-done((bf16[128,128]{1,0:T(8,128)(2,1)S(1)}, bf16[128,128]{1,0:T(8,128)(2,1)S(1)}, u32[]{:S(2)}, u32[]{:S(2)}) %collective-permute-start.8) | collective-permute-done | bytes 32800 | tf_op jit(solution)/shard_map/ppermute | solution.py:62
  29.0 2.2 %collective-permute-done.7.z2 = bf16[128,128]{1,0:T(8,128)(2,1)S(1)} collective-permute-done((bf16[128,128]{1,0:T(8,128)(2,1)S(1)}, bf16[128,128]{1,0:T(8,128)(2,1)S(1)}, u32[]{:S(2)}, u32[]{:S(2)}) %collective-permute-start.7) | collective-permute-done | bytes 32800 | tf_op jit(solution)/shard_map/ppermute | solution.py:62
  32.9 1.7 %collective-permute-start.11 = (bf16[384,128]{1,0:T(8,128)(2,1)S(1)}, bf16[384,128]{1,0:T(8,128)(2,1)S(1)}, u32[]{:S(2)}, u32[]{:S(2)}) collective-permute-start(bf16[384,128]{1,0:T(8,128)(2,1)S(1)} %get-tuple-element.55), channel_id=1, source_target_pairs={{0,1},{1,0},{2,3},{3,2},{4,5},{5,4},{6,7},{7,6},{8,9},{9,8},{10,11... | collective-permute-start | bytes 294920 | tf_op jit(solution)/shard_map/ppermute | solution.py:64
  34.6 1.5 %collective-permute-start.13 = (bf16[384,128]{1,0:T(8,128)(2,1)S(1)}, bf16[384,128]{1,0:T(8,128)(2,1)S(1)}, u32[]{:S(2)}, u32[]{:S(2)}) collective-permute-start(bf16[384,128]{1,0:T(8,128)(2,1)S(1)} %get-tuple-element.57), channel_id=1, source_target_pairs={{0,5},{1,4},{2,7},{3,6},{4,1},{5,0},{6,3},{7,2},{8,13},{9,12},{10,... | collective-permute-start | bytes 294920 | tf_op jit(solution)/shard_map/ppermute | solution.py:70
  36.5 4.9 %collective-permute-done.12.refs_2_ = bf16[128,128]{1,0:T(8,128)(2,1)S(1)} collective-permute-done((bf16[128,128]{1,0:T(8,128)(2,1)S(1)}, bf16[128,128]{1,0:T(8,128)(2,1)S(1)}, u32[]{:S(2)}, u32[]{:S(2)}) %collective-permute-start.12) | collective-permute-done | bytes 32800 | tf_op jit(solution)/shard_map/ppermute | solution.py:62
  41.6 1.7 %collective-permute-start.16 = (bf16[128,128]{1,0:T(8,128)(2,1)S(1)}, bf16[128,128]{1,0:T(8,128)(2,1)S(1)}, u32[]{:S(2)}, u32[]{:S(2)}) collective-permute-start(bf16[128,128]{1,0:T(8,128)(2,1)S(1)} %shard_map.118.z0), channel_id=1, source_target_pairs={{0,24},{2,26},{4,28},{6,30},{8,16},{10,18},{12,20},{14,22},{16,8},... | collective-permute-start | bytes 98312 | tf_op jit(solution)/shard_map/ppermute | solution.py:62
  43.8 2.3 %collective-permute-start.14 = (bf16[128,128]{1,0:T(8,128)(2,1)S(1)}, bf16[128,128]{1,0:T(8,128)(2,1)S(1)}, u32[]{:S(2)}, u32[]{:S(2)}) collective-permute-start(bf16[128,128]{1,0:T(8,128)(2,1)S(1)} %shard_map.118.z0), channel_id=1, source_target_pairs={{0,8},{2,10},{4,12},{6,14},{8,0},{10,2},{12,4},{14,6},{16,24},{18,... | collective-permute-start | bytes 98312 | tf_op jit(solution)/shard_map/ppermute | solution.py:62
  46.0 1.4 %collective-permute-done.16.z3 = bf16[128,128]{1,0:T(8,128)(2,1)S(1)} collective-permute-done((bf16[128,128]{1,0:T(8,128)(2,1)S(1)}, bf16[128,128]{1,0:T(8,128)(2,1)S(1)}, u32[]{:S(2)}, u32[]{:S(2)}) %collective-permute-start.16) | collective-permute-done | bytes 32800 | tf_op jit(solution)/shard_map/ppermute | solution.py:62
  50.0 1.5 %collective-permute-start.20 = (bf16[512,128]{1,0:T(8,128)(2,1)S(1)}, bf16[512,128]{1,0:T(8,128)(2,1)S(1)}, u32[]{:S(2)}, u32[]{:S(2)}) collective-permute-start(bf16[512,128]{1,0:T(8,128)(2,1)S(1)} %get-tuple-element.59), channel_id=1, source_target_pairs={{0,5},{1,4},{2,7},{3,6},{4,1},{5,0},{6,3},{7,2},{8,13},{9,12},{10,... | collective-permute-start | bytes 393224 | tf_op jit(solution)/shard_map/ppermute | solution.py:70
  51.4 1.8 %collective-permute-start.19 = (bf16[512,128]{1,0:T(8,128)(2,1)S(1)}, bf16[512,128]{1,0:T(8,128)(2,1)S(1)}, u32[]{:S(2)}, u32[]{:S(2)}) collective-permute-start(bf16[512,128]{1,0:T(8,128)(2,1)S(1)} %get-tuple-element.59), channel_id=1, source_target_pairs={{0,4},{2,6},{4,0},{6,2},{8,12},{10,14},{12,8},{14,10},{16,20},{18,... | collective-permute-start | bytes 393224 | tf_op jit(solution)/shard_map/ppermute | solution.py:62
  53.7 3.6 %collective-permute-done.20.refs_2_ = bf16[512,128]{1,0:T(8,128)(2,1)S(1)} collective-permute-done((bf16[512,128]{1,0:T(8,128)(2,1)S(1)}, bf16[512,128]{1,0:T(8,128)(2,1)S(1)}, u32[]{:S(2)}, u32[]{:S(2)}) %collective-permute-start.20) | collective-permute-done | bytes 131104 | tf_op jit(solution)/shard_map/ppermute | solution.py:70
  57.3 2.0 %collective-permute-done.19.refs_1_ = bf16[512,128]{1,0:T(8,128)(2,1)S(1)} collective-permute-done((bf16[512,128]{1,0:T(8,128)(2,1)S(1)}, bf16[512,128]{1,0:T(8,128)(2,1)S(1)}, u32[]{:S(2)}, u32[]{:S(2)}) %collective-permute-start.19) | collective-permute-done | bytes 131104 | tf_op jit(solution)/shard_map/ppermute | solution.py:62
  61.3 1.7 %collective-permute-start.22 = (bf16[128,128]{1,0:T(8,128)(2,1)S(1)}, bf16[128,128]{1,0:T(8,128)(2,1)S(1)}, u32[]{:S(2)}, u32[]{:S(2)}) collective-permute-start(bf16[128,128]{1,0:T(8,128)(2,1)S(1)} %get-tuple-element.68), channel_id=1, source_target_pairs={{0,8},{2,10},{4,12},{6,14},{8,0},{10,2},{12,4},{14,6},{16,24},{18,... | collective-permute-start | bytes 98312 | tf_op jit(solution)/shard_map/ppermute | solution.py:62
  64.3 1.5 %collective-permute-start.24 = (bf16[128,128]{1,0:T(8,128)(2,1)S(1)}, bf16[128,128]{1,0:T(8,128)(2,1)S(1)}, u32[]{:S(2)}, u32[]{:S(2)}) collective-permute-start(bf16[128,128]{1,0:T(8,128)(2,1)S(1)} %get-tuple-element.70), channel_id=1, source_target_pairs={{0,24},{2,26},{4,28},{6,30},{8,16},{10,18},{12,20},{14,22},{16,8},... | collective-permute-start | bytes 98312 | tf_op jit(solution)/shard_map/ppermute | solution.py:62
  65.8 2.3 %collective-permute-done.23.refs_1_ = bf16[128,128]{1,0:T(8,128)(2,1)S(1)} collective-permute-done((bf16[128,128]{1,0:T(8,128)(2,1)S(1)}, bf16[128,128]{1,0:T(8,128)(2,1)S(1)}, u32[]{:S(2)}, u32[]{:S(2)}) %collective-permute-start.23) | collective-permute-done | bytes 32800 | tf_op jit(solution)/shard_map/ppermute | solution.py:62
  68.0 2.0 %collective-permute-done.24.refs_2_ = bf16[128,128]{1,0:T(8,128)(2,1)S(1)} collective-permute-done((bf16[128,128]{1,0:T(8,128)(2,1)S(1)}, bf16[128,128]{1,0:T(8,128)(2,1)S(1)}, u32[]{:S(2)}, u32[]{:S(2)}) %collective-permute-start.24) | collective-permute-done | bytes 32800 | tf_op jit(solution)/shard_map/ppermute | solution.py:62
  70.2 1.8 %collective-permute-start.27 = (bf16[128,128]{1,0:T(8,128)(2,1)S(1)}, bf16[128,128]{1,0:T(8,128)(2,1)S(1)}, u32[]{:S(2)}, u32[]{:S(2)}) collective-permute-start(bf16[128,128]{1,0:T(8,128)(2,1)S(1)} %shard_map.127.refs_0_), channel_id=1, source_target_pairs={{0,5},{1,4},{2,7},{3,6},{4,1},{5,0},{6,3},{7,2},{8,13},{9,12},{10,... | collective-permute-start | bytes 98312 | tf_op jit(solution)/shard_map/ppermute | solution.py:70
  78.6 2.0 %collective-permute-start.30 = (bf16[128,128]{1,0:T(8,128)(2,1)S(1)}, bf16[128,128]{1,0:T(8,128)(2,1)S(1)}, u32[]{:S(2)}, u32[]{:S(2)}) collective-permute-start(bf16[128,128]{1,0:T(8,128)(2,1)S(1)} %get-tuple-element.74), channel_id=1, source_target_pairs={{0,16},{2,18},{4,20},{6,22},{8,24},{10,26},{12,28},{14,30},{16,0},... | collective-permute-start | bytes 98312 | tf_op jit(solution)/shard_map/ppermute | solution.py:62
  80.6 2.4 %collective-permute-start.31 = (bf16[128,128]{1,0:T(8,128)(2,1)S(1)}, bf16[128,128]{1,0:T(8,128)(2,1)S(1)}, u32[]{:S(2)}, u32[]{:S(2)}) collective-permute-start(bf16[128,128]{1,0:T(8,128)(2,1)S(1)} %get-tuple-element.75), channel_id=1, source_target_pairs={{0,24},{2,26},{4,28},{6,30},{8,16},{10,18},{12,20},{14,22},{16,8},... | collective-permute-start | bytes 98312 | tf_op jit(solution)/shard_map/ppermute | solution.py:62
  83.6 2.7 %collective-permute-done.31.refs_2_ = bf16[128,128]{1,0:T(8,128)(2,1)S(1)} collective-permute-done((bf16[128,128]{1,0:T(8,128)(2,1)S(1)}, bf16[128,128]{1,0:T(8,128)(2,1)S(1)}, u32[]{:S(2)}, u32[]{:S(2)}) %collective-permute-start.31) | collective-permute-done | bytes 32800 | tf_op jit(solution)/shard_map/ppermute | solution.py:62
  90.2 1.7 %collective-permute-done.34.refs_3_ = bf16[256,128]{1,0:T(8,128)(2,1)S(1)} collective-permute-done((bf16[256,128]{1,0:T(8,128)(2,1)S(1)}, bf16[256,128]{1,0:T(8,128)(2,1)S(1)}, u32[]{:S(2)}, u32[]{:S(2)}) %collective-permute-start.34) | collective-permute-done | bytes 65568 | tf_op jit(solution)/shard_map/ppermute | solution.py:70
  95.3 2.9 %collective-permute-start.37 = (bf16[256,128]{1,0:T(8,128)(2,1)S(1)}, bf16[256,128]{1,0:T(8,128)(2,1)S(1)}, u32[]{:S(2)}, u32[]{:S(2)}) collective-permute-start(bf16[256,128]{1,0:T(8,128)(2,1)S(1)} %get-tuple-element.82), channel_id=1, source_target_pairs={{0,16},{2,18},{4,20},{6,22},{8,24},{10,26},{12,28},{14,30},{16,0},... | collective-permute-start | bytes 196616 | tf_op jit(solution)/shard_map/ppermute | solution.py:62
  98.2 1.5 %collective-permute-start.38 = (bf16[256,128]{1,0:T(8,128)(2,1)S(1)}, bf16[256,128]{1,0:T(8,128)(2,1)S(1)}, u32[]{:S(2)}, u32[]{:S(2)}) collective-permute-start(bf16[256,128]{1,0:T(8,128)(2,1)S(1)} %get-tuple-element.83), channel_id=1, source_target_pairs={{0,24},{2,26},{4,28},{6,30},{8,16},{10,18},{12,20},{14,22},{16,8},... | collective-permute-start | bytes 196616 | tf_op jit(solution)/shard_map/ppermute | solution.py:62
  100.6 2.4 %collective-permute-done.37.refs_1_ = bf16[256,128]{1,0:T(8,128)(2,1)S(1)} collective-permute-done((bf16[256,128]{1,0:T(8,128)(2,1)S(1)}, bf16[256,128]{1,0:T(8,128)(2,1)S(1)}, u32[]{:S(2)}, u32[]{:S(2)}) %collective-permute-start.37) | collective-permute-done | bytes 65568 | tf_op jit(solution)/shard_map/ppermute | solution.py:62
  103.0 1.4 %collective-permute-done.38.refs_2_ = bf16[256,128]{1,0:T(8,128)(2,1)S(1)} collective-permute-done((bf16[256,128]{1,0:T(8,128)(2,1)S(1)}, bf16[256,128]{1,0:T(8,128)(2,1)S(1)}, u32[]{:S(2)}, u32[]{:S(2)}) %collective-permute-start.38) | collective-permute-done | bytes 65568 | tf_op jit(solution)/shard_map/ppermute | solution.py:62
  (82 shorter events, 31.0 us)
Async XLA Ops:
  0.6 9.0 %collective-permute-start.2 = (bf16[128,128]{1,0:T(8,128)(2,1)}, bf16[128,128]{1,0:T(8,128)(2,1)S(1)}, u32[]{:S(2)}, u32[]{:S(2)}) collective-permute-start(bf16[128,128]{1,0:T(8,128)(2,1)} %anchor_ref.1), channel_id=1, source_target_pairs={{0,24},{2,26},{4,28},{6,30},{8,16},{10,18},{12,20},{14,22},{16,8},... | collective-permute-start | bytes 98312 | tf_op jit(solution)/shard_map/ppermute | solution.py:62
  5.8 5.0 %collective-permute-start.1 = (bf16[128,128]{1,0:T(8,128)(2,1)}, bf16[128,128]{1,0:T(8,128)(2,1)S(1)}, u32[]{:S(2)}, u32[]{:S(2)}) collective-permute-start(bf16[128,128]{1,0:T(8,128)(2,1)} %anchor_ref.1), channel_id=1, source_target_pairs={{0,16},{2,18},{4,20},{6,22},{8,24},{10,26},{12,28},{14,30},{16,0},... | collective-permute-start | bytes 98312 | tf_op jit(solution)/shard_map/ppermute | solution.py:62
  5.8 5.0 %collective-permute-start = (bf16[128,128]{1,0:T(8,128)(2,1)}, bf16[128,128]{1,0:T(8,128)(2,1)S(1)}, u32[]{:S(2)}, u32[]{:S(2)}) collective-permute-start(bf16[128,128]{1,0:T(8,128)(2,1)} %anchor_ref.1), channel_id=1, source_target_pairs={{0,8},{2,10},{4,12},{6,14},{8,0},{10,2},{12,4},{14,6},{16,24},{18,... | collective-permute-start | bytes 98312 | tf_op jit(solution)/shard_map/ppermute | solution.py:62
  10.8 6.3 %collective-permute-start.3 = (bf16[512,128]{1,0:T(8,128)(2,1)S(1)}, bf16[512,128]{1,0:T(8,128)(2,1)S(1)}, u32[]{:S(2)}, u32[]{:S(2)}) collective-permute-start(bf16[512,128]{1,0:T(8,128)(2,1)S(1)} %pad_maximum_fusion), channel_id=1, source_target_pairs={{0,4},{2,6},{4,0},{6,2},{8,12},{10,14},{12,8},{14,10},{16,20},{18,... | collective-permute-start | bytes 393224 | tf_op jit(solution)/shard_map/ppermute | solution.py:62
  12.4 18.9 %collective-permute-start.9 = (bf16[256,1152]{1,0:T(8,128)(2,1)S(1)}, bf16[256,1152]{1,0:T(8,128)(2,1)S(1)}, u32[]{:S(2)}, u32[]{:S(2)}) collective-permute-start(bf16[256,1152]{1,0:T(8,128)(2,1)S(1)} %get-tuple-element.50.refs_1_), channel_id=1, source_target_pairs={{0,4},{2,6},{4,0},{6,2},{8,12},{10,14},{12,8},{14,10},{16,20},{18,... | collective-permute-start | bytes 1769480 | tf_op jit(solution)/shard_map/ppermute | solution.py:62
  19.1 4.0 %collective-permute-start.5 = (bf16[128,128]{1,0:T(8,128)(2,1)S(1)}, bf16[128,128]{1,0:T(8,128)(2,1)S(1)}, u32[]{:S(2)}, u32[]{:S(2)}) collective-permute-start(bf16[128,128]{1,0:T(8,128)(2,1)S(1)} %get-tuple-element.52), channel_id=1, source_target_pairs={{0,1},{1,0},{2,3},{3,2},{4,5},{5,4},{6,7},{7,6},{8,9},{9,8},{10,11... | collective-permute-start | bytes 98312 | tf_op jit(solution)/shard_map/ppermute | solution.py:64
  23.2 5.8 %collective-permute-start.8 = (bf16[128,128]{1,0:T(8,128)(2,1)S(1)}, bf16[128,128]{1,0:T(8,128)(2,1)S(1)}, u32[]{:S(2)}, u32[]{:S(2)}) collective-permute-start(bf16[128,128]{1,0:T(8,128)(2,1)S(1)} %shard_map.115.z0), channel_id=1, source_target_pairs={{0,24},{2,26},{4,28},{6,30},{8,16},{10,18},{12,20},{14,22},{16,8},... | collective-permute-start | bytes 98312 | tf_op jit(solution)/shard_map/ppermute | solution.py:62
  26.4 4.8 %collective-permute-start.7 = (bf16[128,128]{1,0:T(8,128)(2,1)S(1)}, bf16[128,128]{1,0:T(8,128)(2,1)S(1)}, u32[]{:S(2)}, u32[]{:S(2)}) collective-permute-start(bf16[128,128]{1,0:T(8,128)(2,1)S(1)} %shard_map.115.z0), channel_id=1, source_target_pairs={{0,16},{2,18},{4,20},{6,22},{8,24},{10,26},{12,28},{14,30},{16,0},... | collective-permute-start | bytes 98312 | tf_op jit(solution)/shard_map/ppermute | solution.py:62
  26.4 4.8 %collective-permute-start.6 = (bf16[128,128]{1,0:T(8,128)(2,1)S(1)}, bf16[128,128]{1,0:T(8,128)(2,1)S(1)}, u32[]{:S(2)}, u32[]{:S(2)}) collective-permute-start(bf16[128,128]{1,0:T(8,128)(2,1)S(1)} %shard_map.115.z0), channel_id=1, source_target_pairs={{0,8},{2,10},{4,12},{6,14},{8,0},{10,2},{12,4},{14,6},{16,24},{18,... | collective-permute-start | bytes 98312 | tf_op jit(solution)/shard_map/ppermute | solution.py:62
  32.9 8.5 %collective-permute-start.11 = (bf16[384,128]{1,0:T(8,128)(2,1)S(1)}, bf16[384,128]{1,0:T(8,128)(2,1)S(1)}, u32[]{:S(2)}, u32[]{:S(2)}) collective-permute-start(bf16[384,128]{1,0:T(8,128)(2,1)S(1)} %get-tuple-element.55), channel_id=1, source_target_pairs={{0,1},{1,0},{2,3},{3,2},{4,5},{5,4},{6,7},{7,6},{8,9},{9,8},{10,11... | collective-permute-start | bytes 294920 | tf_op jit(solution)/shard_map/ppermute | solution.py:64
  34.6 6.8 %collective-permute-start.13 = (bf16[384,128]{1,0:T(8,128)(2,1)S(1)}, bf16[384,128]{1,0:T(8,128)(2,1)S(1)}, u32[]{:S(2)}, u32[]{:S(2)}) collective-permute-start(bf16[384,128]{1,0:T(8,128)(2,1)S(1)} %get-tuple-element.57), channel_id=1, source_target_pairs={{0,5},{1,4},{2,7},{3,6},{4,1},{5,0},{6,3},{7,2},{8,13},{9,12},{10,... | collective-permute-start | bytes 294920 | tf_op jit(solution)/shard_map/ppermute | solution.py:70
  36.1 5.3 %collective-permute-start.12 = (bf16[128,128]{1,0:T(8,128)(2,1)S(1)}, bf16[128,128]{1,0:T(8,128)(2,1)S(1)}, u32[]{:S(2)}, u32[]{:S(2)}) collective-permute-start(bf16[128,128]{1,0:T(8,128)(2,1)S(1)} %get-tuple-element.56), channel_id=1, source_target_pairs={{0,4},{2,6},{4,0},{6,2},{8,12},{10,14},{12,8},{14,10},{16,20},{18,... | collective-permute-start | bytes 98312 | tf_op jit(solution)/shard_map/ppermute | solution.py:62
  41.6 5.8 %collective-permute-start.16 = (bf16[128,128]{1,0:T(8,128)(2,1)S(1)}, bf16[128,128]{1,0:T(8,128)(2,1)S(1)}, u32[]{:S(2)}, u32[]{:S(2)}) collective-permute-start(bf16[128,128]{1,0:T(8,128)(2,1)S(1)} %shard_map.118.z0), channel_id=1, source_target_pairs={{0,24},{2,26},{4,28},{6,30},{8,16},{10,18},{12,20},{14,22},{16,8},... | collective-permute-start | bytes 98312 | tf_op jit(solution)/shard_map/ppermute | solution.py:62
  43.3 4.9 %collective-permute-start.15 = (bf16[128,128]{1,0:T(8,128)(2,1)S(1)}, bf16[128,128]{1,0:T(8,128)(2,1)S(1)}, u32[]{:S(2)}, u32[]{:S(2)}) collective-permute-start(bf16[128,128]{1,0:T(8,128)(2,1)S(1)} %shard_map.118.z0), channel_id=1, source_target_pairs={{0,16},{2,18},{4,20},{6,22},{8,24},{10,26},{12,28},{14,30},{16,0},... | collective-permute-start | bytes 98312 | tf_op jit(solution)/shard_map/ppermute | solution.py:62
  43.8 4.5 %collective-permute-start.14 = (bf16[128,128]{1,0:T(8,128)(2,1)S(1)}, bf16[128,128]{1,0:T(8,128)(2,1)S(1)}, u32[]{:S(2)}, u32[]{:S(2)}) collective-permute-start(bf16[128,128]{1,0:T(8,128)(2,1)S(1)} %shard_map.118.z0), channel_id=1, source_target_pairs={{0,8},{2,10},{4,12},{6,14},{8,0},{10,2},{12,4},{14,6},{16,24},{18,... | collective-permute-start | bytes 98312 | tf_op jit(solution)/shard_map/ppermute | solution.py:62
  50.0 7.3 %collective-permute-start.20 = (bf16[512,128]{1,0:T(8,128)(2,1)S(1)}, bf16[512,128]{1,0:T(8,128)(2,1)S(1)}, u32[]{:S(2)}, u32[]{:S(2)}) collective-permute-start(bf16[512,128]{1,0:T(8,128)(2,1)S(1)} %get-tuple-element.59), channel_id=1, source_target_pairs={{0,5},{1,4},{2,7},{3,6},{4,1},{5,0},{6,3},{7,2},{8,13},{9,12},{10,... | collective-permute-start | bytes 393224 | tf_op jit(solution)/shard_map/ppermute | solution.py:70
  51.4 7.9 %collective-permute-start.19 = (bf16[512,128]{1,0:T(8,128)(2,1)S(1)}, bf16[512,128]{1,0:T(8,128)(2,1)S(1)}, u32[]{:S(2)}, u32[]{:S(2)}) collective-permute-start(bf16[512,128]{1,0:T(8,128)(2,1)S(1)} %get-tuple-element.59), channel_id=1, source_target_pairs={{0,4},{2,6},{4,0},{6,2},{8,12},{10,14},{12,8},{14,10},{16,20},{18,... | collective-permute-start | bytes 393224 | tf_op jit(solution)/shard_map/ppermute | solution.py:62
  53.2 6.1 %collective-permute-start.18 = (bf16[512,128]{1,0:T(8,128)(2,1)S(1)}, bf16[512,128]{1,0:T(8,128)(2,1)S(1)}, u32[]{:S(2)}, u32[]{:S(2)}) collective-permute-start(bf16[512,128]{1,0:T(8,128)(2,1)S(1)} %get-tuple-element.59), channel_id=1, source_target_pairs={{0,1},{1,0},{2,3},{3,2},{4,5},{5,4},{6,7},{7,6},{8,9},{9,8},{10,11... | collective-permute-start | bytes 393224 | tf_op jit(solution)/shard_map/ppermute | solution.py:64
  61.3 4.5 %collective-permute-start.22 = (bf16[128,128]{1,0:T(8,128)(2,1)S(1)}, bf16[128,128]{1,0:T(8,128)(2,1)S(1)}, u32[]{:S(2)}, u32[]{:S(2)}) collective-permute-start(bf16[128,128]{1,0:T(8,128)(2,1)S(1)} %get-tuple-element.68), channel_id=1, source_target_pairs={{0,8},{2,10},{4,12},{6,14},{8,0},{10,2},{12,4},{14,6},{16,24},{18,... | collective-permute-start | bytes 98312 | tf_op jit(solution)/shard_map/ppermute | solution.py:62
  63.0 5.0 %collective-permute-start.23 = (bf16[128,128]{1,0:T(8,128)(2,1)S(1)}, bf16[128,128]{1,0:T(8,128)(2,1)S(1)}, u32[]{:S(2)}, u32[]{:S(2)}) collective-permute-start(bf16[128,128]{1,0:T(8,128)(2,1)S(1)} %get-tuple-element.69), channel_id=1, source_target_pairs={{0,16},{2,18},{4,20},{6,22},{8,24},{10,26},{12,28},{14,30},{16,0},... | collective-permute-start | bytes 98312 | tf_op jit(solution)/shard_map/ppermute | solution.py:62
  64.3 5.7 %collective-permute-start.24 = (bf16[128,128]{1,0:T(8,128)(2,1)S(1)}, bf16[128,128]{1,0:T(8,128)(2,1)S(1)}, u32[]{:S(2)}, u32[]{:S(2)}) collective-permute-start(bf16[128,128]{1,0:T(8,128)(2,1)S(1)} %get-tuple-element.70), channel_id=1, source_target_pairs={{0,24},{2,26},{4,28},{6,30},{8,16},{10,18},{12,20},{14,22},{16,8},... | collective-permute-start | bytes 98312 | tf_op jit(solution)/shard_map/ppermute | solution.py:62
  70.2 4.9 %collective-permute-start.27 = (bf16[128,128]{1,0:T(8,128)(2,1)S(1)}, bf16[128,128]{1,0:T(8,128)(2,1)S(1)}, u32[]{:S(2)}, u32[]{:S(2)}) collective-permute-start(bf16[128,128]{1,0:T(8,128)(2,1)S(1)} %shard_map.127.refs_0_), channel_id=1, source_target_pairs={{0,5},{1,4},{2,7},{3,6},{4,1},{5,0},{6,3},{7,2},{8,13},{9,12},{10,... | collective-permute-start | bytes 98312 | tf_op jit(solution)/shard_map/ppermute | solution.py:70
  72.0 3.9 %collective-permute-start.26 = (bf16[128,128]{1,0:T(8,128)(2,1)S(1)}, bf16[128,128]{1,0:T(8,128)(2,1)S(1)}, u32[]{:S(2)}, u32[]{:S(2)}) collective-permute-start(bf16[128,128]{1,0:T(8,128)(2,1)S(1)} %shard_map.127.refs_0_), channel_id=1, source_target_pairs={{0,4},{2,6},{4,0},{6,2},{8,12},{10,14},{12,8},{14,10},{16,20},{18,... | collective-permute-start | bytes 98312 | tf_op jit(solution)/shard_map/ppermute | solution.py:62
  78.5 5.1 %collective-permute-start.29 = (bf16[128,128]{1,0:T(8,128)(2,1)S(1)}, bf16[128,128]{1,0:T(8,128)(2,1)S(1)}, u32[]{:S(2)}, u32[]{:S(2)}) collective-permute-start(bf16[128,128]{1,0:T(8,128)(2,1)S(1)} %get-tuple-element.73), channel_id=1, source_target_pairs={{0,8},{2,10},{4,12},{6,14},{8,0},{10,2},{12,4},{14,6},{16,24},{18,... | collective-permute-start | bytes 98312 | tf_op jit(solution)/shard_map/ppermute | solution.py:62
  78.6 5.0 %collective-permute-start.30 = (bf16[128,128]{1,0:T(8,128)(2,1)S(1)}, bf16[128,128]{1,0:T(8,128)(2,1)S(1)}, u32[]{:S(2)}, u32[]{:S(2)}) collective-permute-start(bf16[128,128]{1,0:T(8,128)(2,1)S(1)} %get-tuple-element.74), channel_id=1, source_target_pairs={{0,16},{2,18},{4,20},{6,22},{8,24},{10,26},{12,28},{14,30},{16,0},... | collective-permute-start | bytes 98312 | tf_op jit(solution)/shard_map/ppermute | solution.py:62
  80.6 5.7 %collective-permute-start.31 = (bf16[128,128]{1,0:T(8,128)(2,1)S(1)}, bf16[128,128]{1,0:T(8,128)(2,1)S(1)}, u32[]{:S(2)}, u32[]{:S(2)}) collective-permute-start(bf16[128,128]{1,0:T(8,128)(2,1)S(1)} %get-tuple-element.75), channel_id=1, source_target_pairs={{0,24},{2,26},{4,28},{6,30},{8,16},{10,18},{12,20},{14,22},{16,8},... | collective-permute-start | bytes 98312 | tf_op jit(solution)/shard_map/ppermute | solution.py:62
  86.6 5.3 %collective-permute-start.34 = (bf16[256,128]{1,0:T(8,128)(2,1)S(1)}, bf16[256,128]{1,0:T(8,128)(2,1)S(1)}, u32[]{:S(2)}, u32[]{:S(2)}) collective-permute-start(bf16[256,128]{1,0:T(8,128)(2,1)S(1)} %shard_map.131.refs_0_), channel_id=1, source_target_pairs={{0,5},{1,4},{2,7},{3,6},{4,1},{5,0},{6,3},{7,2},{8,13},{9,12},{10,... | collective-permute-start | bytes 196616 | tf_op jit(solution)/shard_map/ppermute | solution.py:70
  87.9 4.7 %collective-permute-start.33 = (bf16[256,128]{1,0:T(8,128)(2,1)S(1)}, bf16[256,128]{1,0:T(8,128)(2,1)S(1)}, u32[]{:S(2)}, u32[]{:S(2)}) collective-permute-start(bf16[256,128]{1,0:T(8,128)(2,1)S(1)} %shard_map.131.refs_0_), channel_id=1, source_target_pairs={{0,4},{2,6},{4,0},{6,2},{8,12},{10,14},{12,8},{14,10},{16,20},{18,... | collective-permute-start | bytes 196616 | tf_op jit(solution)/shard_map/ppermute | solution.py:62
  89.1 4.3 %collective-permute-start.32 = (bf16[256,128]{1,0:T(8,128)(2,1)S(1)}, bf16[256,128]{1,0:T(8,128)(2,1)S(1)}, u32[]{:S(2)}, u32[]{:S(2)}) collective-permute-start(bf16[256,128]{1,0:T(8,128)(2,1)S(1)} %shard_map.131.refs_0_), channel_id=1, source_target_pairs={{0,1},{1,0},{2,3},{3,2},{4,5},{5,4},{6,7},{7,6},{8,9},{9,8},{10,11... | collective-permute-start | bytes 196616 | tf_op jit(solution)/shard_map/ppermute | solution.py:64
  95.2 5.4 %collective-permute-start.36 = (bf16[256,128]{1,0:T(8,128)(2,1)S(1)}, bf16[256,128]{1,0:T(8,128)(2,1)S(1)}, u32[]{:S(2)}, u32[]{:S(2)}) collective-permute-start(bf16[256,128]{1,0:T(8,128)(2,1)S(1)} %get-tuple-element.81), channel_id=1, source_target_pairs={{0,8},{2,10},{4,12},{6,14},{8,0},{10,2},{12,4},{14,6},{16,24},{18,... | collective-permute-start | bytes 196616 | tf_op jit(solution)/shard_map/ppermute | solution.py:62
  95.3 7.7 %collective-permute-start.37 = (bf16[256,128]{1,0:T(8,128)(2,1)S(1)}, bf16[256,128]{1,0:T(8,128)(2,1)S(1)}, u32[]{:S(2)}, u32[]{:S(2)}) collective-permute-start(bf16[256,128]{1,0:T(8,128)(2,1)S(1)} %get-tuple-element.82), channel_id=1, source_target_pairs={{0,16},{2,18},{4,20},{6,22},{8,24},{10,26},{12,28},{14,30},{16,0},... | collective-permute-start | bytes 196616 | tf_op jit(solution)/shard_map/ppermute | solution.py:62
  98.2 6.2 %collective-permute-start.38 = (bf16[256,128]{1,0:T(8,128)(2,1)S(1)}, bf16[256,128]{1,0:T(8,128)(2,1)S(1)}, u32[]{:S(2)}, u32[]{:S(2)}) collective-permute-start(bf16[256,128]{1,0:T(8,128)(2,1)S(1)} %get-tuple-element.83), channel_id=1, source_target_pairs={{0,24},{2,26},{4,28},{6,30},{8,16},{10,18},{12,20},{14,22},{16,8},... | collective-permute-start | bytes 196616 | tf_op jit(solution)/shard_map/ppermute | solution.py:62
  (10 other events, 49.7 us)
